TPU v7x, 32 devices: a whole 2x2x4 slice. The times are simulated.
32 devices in a mesh: shard: 2 (over x), ctx: 4 (over y, core), tp: 4 (over z).
Axes of the slice: x: 2, y: 2, z: 4, core: 2. Of those that a mesh axis runs over, the one named last changes fastest.
Arguments:
- tokens: bfloat16 [4, 4096, 1024], P('shard', ('ctx', 'tp')), may hold values from -6 to 6
- positions: int32 [4, 4096], P('shard', 'ctx'), may hold values from 0 to 12287, as said below
- first_gain: float32 [1024], replicated, may hold values from 0.5 to 1.5
- query_weight: bfloat16 [1024, 1024], P(('shard', 'ctx'), 'tp'), may hold values from -0.1875 to 0.1875
- key_weight: bfloat16 [1024, 512], P(('shard', 'ctx'), 'tp'), may hold values from -0.1875 to 0.1875
- value_weight: bfloat16 [1024, 512], P(('shard', 'ctx'), 'tp'), may hold values from -0.1875 to 0.1875
- query_gain: float32 [64], replicated, may hold values from 0.1 to 1.9
- key_gain: float32 [64], replicated, may hold values from 0.1 to 1.9
- output_weight: bfloat16 [1024, 1024], P('tp', ('shard', 'ctx')), may hold values from -1 to 1
- second_gain: float32 [1024], replicated, may hold values from 0.5 to 1.5
- gate_weight: bfloat16 [1024, 4608], P(('shard', 'ctx'), 'tp'), may hold values from -0.1875 to 0.1875
- up_weight: bfloat16 [1024, 4608], P(('shard', 'ctx'), 'tp'), may hold values from -0.1875 to 0.1875
- down_weight: bfloat16 [4608, 1024], P('tp', ('shard', 'ctx')), may hold values from -0.09375 to 0.09375
- upstream: bfloat16 [4, 4096, 1024], P('shard', ('ctx', 'tp')), may hold values from -6 to 6
Outputs:
- block_output: bfloat16 [4, 4096, 1024], P('shard', ('ctx', 'tp'))
- token_gradient: float32 [4, 4096, 1024], P('shard', ('ctx', 'tp'))
- query_gradient: float32 [1024, 1024], P(('shard', 'ctx'), 'tp')
- key_gradient: float32 [1024, 512], P(('shard', 'ctx'), 'tp')
- value_gradient: float32 [1024, 512], P(('shard', 'ctx'), 'tp')
- output_gradient: float32 [1024, 1024], P('tp', ('shard', 'ctx'))
- gate_gradient: float32 [1024, 4608], P(('shard', 'ctx'), 'tp')
- up_gradient: float32 [1024, 4608], P(('shard', 'ctx'), 'tp')
- down_gradient: float32 [4608, 1024], P('tp', ('shard', 'ctx'))
- first_gain_gradient: float32 [1024], replicated
- second_gain_gradient: float32 [1024], replicated
- query_gain_gradient: float32 [64], replicated
- key_gain_gradient: float32 [64], replicated
Inputs may be any that keep to these rules, and one draw needn't show every extreme that they name: `positions`: along each sequence a position exceeds the one before it by 1 to 3; the first is at most 2.
All inputs are finite; a program needn't handle non-finite values.
Results may differ from a plain program's by a relative error of at most 0.02.
Values may be sent and summed in bfloat16 or wider, within the bound.
No kernel may reach another device: no remote copies, remote signals or barrier semaphores. Data moves between devices by JAX's collectives and lax.ppermute only.
A program may use at most 192 MiB of HBM per device.

v0:
```python
import math

import jax
import jax.numpy as jnp
from jax import lax
from jax.sharding import PartitionSpec as P

EPS = 1e-05
THETA = 1000000.0
NEGATIVE = -1e30


def norm_rows(values, gain):
    return values * lax.rsqrt(jnp.mean(values * values, axis=-1, keepdims=True) + EPS) * gain


def rotary_tables(places, width):
    freqs = jnp.exp(-math.log(THETA) * jnp.arange(0, width, 2).astype(jnp.float32) / width)
    angles = places.astype(jnp.float32)[:, None] * freqs[None, :]
    cosine = jnp.concatenate([jnp.cos(angles), jnp.cos(angles)], axis=-1)[:, None, :]
    sine = jnp.concatenate([jnp.sin(angles), jnp.sin(angles)], axis=-1)[:, None, :]
    return (cosine, sine)


def shape_heads(raw, gain, cosine, sine):
    normed = norm_rows(raw, gain)
    half = normed.shape[-1] // 2
    turned = jnp.concatenate([-normed[..., half:], normed[..., :half]], axis=-1)
    return normed * cosine + turned * sine


def dot_first(left, right):
    return lax.dot_general(
        left, right, (((0,), (0,)), ((), ())), preferred_element_type=jnp.float32
    )


def dot_last(left, right):
    return lax.dot_general(
        left, right, (((1,), (1,)), ((), ())), preferred_element_type=jnp.float32
    )


def project_rows(left, right):
    return jnp.dot(left, right, preferred_element_type=jnp.float32)


def project_pair(gate_back, gate_full, up_back, up_full):
    first_part = dot_last(gate_back, gate_full)
    return first_part + dot_last(up_back, up_full)


def project_three(query_back, query_full, key_back, key_full, value_back, value_full):
    total = dot_last(query_back, query_full)
    total = total + dot_last(key_back, key_full)
    return total + dot_last(value_back, value_full)


def fetch_weights(
    query_weight, key_weight, value_weight, output_weight, gate_weight, up_weight, down_weight
):
    return (
        lax.all_gather(query_weight, ("shard", "ctx"), axis=0, tiled=True),
        lax.all_gather(key_weight, ("shard", "ctx"), axis=0, tiled=True),
        lax.all_gather(value_weight, ("shard", "ctx"), axis=0, tiled=True),
        lax.all_gather(output_weight, ("shard", "ctx"), axis=1, tiled=True),
        lax.all_gather(gate_weight, ("shard", "ctx"), axis=0, tiled=True),
        lax.all_gather(up_weight, ("shard", "ctx"), axis=0, tiled=True),
        lax.all_gather(down_weight, ("shard", "ctx"), axis=1, tiled=True),
    )


def attend(query_b, key_b, value_b, first_query):
    span_rows, kv_heads, group, width = query_b.shape
    scale = 1.0 / math.sqrt(width)
    query_index = first_query + jnp.arange(span_rows)
    last_query = first_query + span_rows - 1
    init = (
        jnp.full((kv_heads, group, span_rows), NEGATIVE, jnp.float32),
        jnp.zeros((kv_heads, group, span_rows), jnp.float32),
        jnp.zeros((kv_heads, group, span_rows, width), jnp.float32),
    )
    key_piece = lax.all_gather(key_b, "ctx", axis=0, tiled=True)
    value_piece = lax.all_gather(value_b, "ctx", axis=0, tiled=True)

    def update(state):
        peak, total, accum = state
        scores = (
            jnp.einsum("qkgd,nkd->kgqn", query_b, key_piece, preferred_element_type=jnp.float32)
            * scale
        )
        key_index = jnp.arange(key_piece.shape[0])
        allowed = key_index[None, :] <= query_index[:, None]
        masked = jnp.where(allowed, scores, NEGATIVE)
        new_peak = jnp.maximum(peak, jnp.max(masked, axis=-1))
        weights = jnp.where(allowed, jnp.exp(masked - new_peak[..., None]), 0.0)
        total = jnp.sum(weights, axis=-1)
        accum = jnp.einsum(
            "kgqn,nkd->kgqd",
            weights.astype(jnp.bfloat16),
            value_piece,
            preferred_element_type=jnp.float32,
        )
        return (new_peak, total, accum)

    peak, total, accum = lax.cond(jnp.int32(0) <= last_query, update, lambda state: state, init)
    return (accum / total[..., None], peak + jnp.log(total))


def attend_back(query_b, keys_all, values_all, back_b, attention, logsum, first_query):
    span_rows, kv_heads, group, width = query_b.shape
    scale = 1.0 / math.sqrt(width)
    query_index = first_query + jnp.arange(span_rows)
    delta = jnp.einsum("qkgd,kgqd->kgq", back_b.astype(jnp.float32), attention)

    def block(index, carry):
        query_back, key_buffer, value_buffer = carry
        key_block = lax.dynamic_slice_in_dim(keys_all, index * span_rows, span_rows, 0)
        value_block = lax.dynamic_slice_in_dim(values_all, index * span_rows, span_rows, 0)
        scores = (
            jnp.einsum("qkgd,nkd->kgqn", query_b, key_block, preferred_element_type=jnp.float32)
            * scale
        )
        key_index = index * span_rows + jnp.arange(span_rows)
        allowed = key_index[None, :] <= query_index[:, None]
        probs = jnp.where(allowed, jnp.exp(scores - logsum[..., None]), 0.0)
        value_part = jnp.einsum(
            "kgqn,qkgd->nkd", probs.astype(jnp.bfloat16), back_b, preferred_element_type=jnp.float32
        )
        slopes = jnp.einsum(
            "qkgd,nkd->kgqn", back_b, value_block, preferred_element_type=jnp.float32
        )
        score_back = (probs * (slopes - delta[..., None])).astype(jnp.bfloat16)
        query_back = (
            query_back
            + jnp.einsum(
                "kgqn,nkd->qkgd", score_back, key_block, preferred_element_type=jnp.float32
            )
            * scale
        )
        key_part = (
            jnp.einsum("kgqn,qkgd->nkd", score_back, query_b, preferred_element_type=jnp.float32)
            * scale
        )
        key_buffer = lax.dynamic_update_slice_in_dim(key_buffer, key_part, index * span_rows, 0)
        value_buffer = lax.dynamic_update_slice_in_dim(
            value_buffer, value_part, index * span_rows, 0
        )
        return (query_back, key_buffer, value_buffer)

    init = (
        jnp.zeros(query_b.shape, jnp.float32),
        jnp.zeros(keys_all.shape, jnp.float32),
        jnp.zeros(values_all.shape, jnp.float32),
    )
    return lax.fori_loop(0, first_query // span_rows + 1, block, init)


def per_device(
    tokens,
    positions,
    first_gain,
    query_weight,
    key_weight,
    value_weight,
    query_gain,
    key_gain,
    output_weight,
    second_gain,
    gate_weight,
    up_weight,
    down_weight,
    upstream,
):
    sequences, rows, width = tokens.shape
    span_rows = positions.shape[1]
    head_dim = query_gain.shape[0]
    first_query = lax.axis_index("ctx") * span_rows
    query_acc = jnp.zeros((width, query_weight.shape[1]), jnp.float32)
    key_acc = jnp.zeros((width, key_weight.shape[1]), jnp.float32)
    value_acc = jnp.zeros((width, value_weight.shape[1]), jnp.float32)
    output_acc = jnp.zeros((output_weight.shape[0], width), jnp.float32)
    gate_acc = jnp.zeros((width, gate_weight.shape[1]), jnp.float32)
    up_acc = jnp.zeros((width, up_weight.shape[1]), jnp.float32)
    down_acc = jnp.zeros((down_weight.shape[0], width), jnp.float32)
    first_gain_acc = jnp.zeros_like(first_gain)
    second_gain_acc = jnp.zeros_like(second_gain)
    query_gain_acc = jnp.zeros_like(query_gain)
    key_gain_acc = jnp.zeros_like(key_gain)
    results = []
    gradients = []
    for seq in range(sequences):
        current = fetch_weights(
            query_weight,
            key_weight,
            value_weight,
            output_weight,
            gate_weight,
            up_weight,
            down_weight,
        )
        query_full, key_full, value_full, output_full, gate_full, up_full, down_full = current
        token_rows = tokens[seq].astype(jnp.float32)
        first = norm_rows(token_rows, first_gain).astype(jnp.bfloat16)
        first_all = lax.all_gather(first, "tp", axis=0, tiled=True)
        cosine, sine = rotary_tables(positions[seq], head_dim)
        query_raw = jnp.dot(first_all, query_full, preferred_element_type=jnp.float32).reshape(
            span_rows, -1, head_dim
        )
        key_raw = jnp.dot(first_all, key_full, preferred_element_type=jnp.float32).reshape(
            span_rows, -1, head_dim
        )
        value_b = (
            jnp.dot(first_all, value_full, preferred_element_type=jnp.float32)
            .astype(jnp.bfloat16)
            .reshape(span_rows, -1, head_dim)
        )
        kv_heads = key_raw.shape[1]
        group = query_raw.shape[1] // kv_heads

        def query_shape(raw, gain):
            return shape_heads(raw, gain, cosine, sine)

        query_b = (
            query_shape(query_raw, query_gain)
            .astype(jnp.bfloat16)
            .reshape(span_rows, kv_heads, group, head_dim)
        )
        key_b = query_shape(key_raw, key_gain).astype(jnp.bfloat16)
        attention, logsum = attend(query_b, key_b, value_b, first_query)
        mixed_b = jnp.transpose(attention, (2, 0, 1, 3)).reshape(span_rows, -1).astype(jnp.bfloat16)
        attn_rows = lax.psum_scatter(
            project_rows(mixed_b, output_full).astype(jnp.bfloat16),
            "tp",
            scatter_dimension=0,
            tiled=True,
        ).astype(jnp.float32)
        middle = token_rows + attn_rows
        second = norm_rows(middle, second_gain).astype(jnp.bfloat16)
        second_all = lax.all_gather(second, "tp", axis=0, tiled=True)
        gate = jnp.dot(second_all, gate_full, preferred_element_type=jnp.float32)
        up = jnp.dot(second_all, up_full, preferred_element_type=jnp.float32)
        gate_sig = jax.nn.sigmoid(gate)
        swish = gate * gate_sig
        hidden_b = (swish * up).astype(jnp.bfloat16)
        ffn_rows = lax.psum_scatter(
            project_rows(hidden_b, down_full).astype(jnp.bfloat16),
            "tp",
            scatter_dimension=0,
            tiled=True,
        ).astype(jnp.float32)
        results.append((middle + ffn_rows).astype(jnp.bfloat16))
        current = fetch_weights(
            query_weight,
            key_weight,
            value_weight,
            output_weight,
            gate_weight,
            up_weight,
            down_weight,
        )
        query_full, key_full, value_full, output_full, gate_full, up_full, down_full = current
        upstream_b = upstream[seq]
        upstream_all = lax.all_gather(upstream_b, "tp", axis=0, tiled=True)
        down_acc = down_acc + dot_first(hidden_b, upstream_all)
        hidden_back = dot_last(upstream_all, down_full)
        gate_back = (hidden_back * up * (gate_sig * (1.0 + gate * (1.0 - gate_sig)))).astype(
            jnp.bfloat16
        )
        up_back = (hidden_back * swish).astype(jnp.bfloat16)
        gate_acc = gate_acc + dot_first(second_all, gate_back)
        up_acc = up_acc + dot_first(second_all, up_back)
        second_back = lax.psum_scatter(
            project_pair(gate_back, gate_full, up_back, up_full).astype(jnp.bfloat16),
            "tp",
            scatter_dimension=0,
            tiled=True,
        ).astype(jnp.float32)
        unused_second, second_fn = jax.vjp(norm_rows, middle, second_gain)
        middle_part, second_part = second_fn(second_back)
        second_gain_acc = second_gain_acc + second_part
        middle_back = upstream_b.astype(jnp.float32) + middle_part
        mixed_back_all = lax.all_gather(middle_back.astype(jnp.bfloat16), "tp", axis=0, tiled=True)
        output_acc = output_acc + dot_first(mixed_b, mixed_back_all)
        attention_back = (
            dot_last(mixed_back_all, output_full)
            .astype(jnp.bfloat16)
            .reshape(span_rows, kv_heads, group, head_dim)
        )
        keys_all, values_all = (
            lax.all_gather(key_b, "ctx", axis=0, tiled=True),
            lax.all_gather(value_b, "ctx", axis=0, tiled=True),
        )
        query_back, key_buffer, value_buffer = attend_back(
            query_b, keys_all, values_all, attention_back, attention, logsum, first_query
        )
        key_back, value_back = (
            lax.psum_scatter(
                key_buffer.astype(jnp.bfloat16), "ctx", scatter_dimension=0, tiled=True
            ).astype(jnp.float32),
            lax.psum_scatter(
                value_buffer.astype(jnp.bfloat16), "ctx", scatter_dimension=0, tiled=True
            ).astype(jnp.float32),
        )
        value_back_b = value_back.reshape(span_rows, -1).astype(jnp.bfloat16)
        unused_key, key_fn = jax.vjp(query_shape, key_raw, key_gain)
        key_raw_back, key_gain_part = key_fn(key_back)
        unused_query, query_fn = jax.vjp(query_shape, query_raw, query_gain)
        query_raw_back, query_gain_part = query_fn(query_back.reshape(span_rows, -1, head_dim))
        key_raw_b = key_raw_back.reshape(span_rows, -1).astype(jnp.bfloat16)
        query_raw_b = query_raw_back.reshape(span_rows, -1).astype(jnp.bfloat16)
        key_gain_acc = key_gain_acc + key_gain_part
        query_gain_acc = query_gain_acc + query_gain_part
        query_acc = query_acc + dot_first(first_all, query_raw_b)
        key_acc = key_acc + dot_first(first_all, key_raw_b)
        value_acc = value_acc + dot_first(first_all, value_back_b)
        first_back = lax.psum_scatter(
            project_three(
                query_raw_b, query_full, key_raw_b, key_full, value_back_b, value_full
            ).astype(jnp.bfloat16),
            "tp",
            scatter_dimension=0,
            tiled=True,
        ).astype(jnp.float32)
        unused_first, first_fn = jax.vjp(norm_rows, token_rows, first_gain)
        token_part, first_part = first_fn(first_back)
        first_gain_acc = first_gain_acc + first_part
        gradients.append(middle_back + token_part)
    query_out, key_out, value_out, output_out, gate_out, up_out, down_out = (
        lax.psum_scatter(query_acc, ("shard", "ctx"), scatter_dimension=0, tiled=True),
        lax.psum_scatter(key_acc, ("shard", "ctx"), scatter_dimension=0, tiled=True),
        lax.psum_scatter(value_acc, ("shard", "ctx"), scatter_dimension=0, tiled=True),
        lax.psum_scatter(output_acc, ("shard", "ctx"), scatter_dimension=1, tiled=True),
        lax.psum_scatter(gate_acc, ("shard", "ctx"), scatter_dimension=0, tiled=True),
        lax.psum_scatter(up_acc, ("shard", "ctx"), scatter_dimension=0, tiled=True),
        lax.psum_scatter(down_acc, ("shard", "ctx"), scatter_dimension=1, tiled=True),
    )
    first_total, second_total, query_total, key_total = lax.psum(
        (first_gain_acc, second_gain_acc, query_gain_acc, key_gain_acc), ("shard", "ctx", "tp")
    )
    return (
        jnp.stack(results),
        jnp.stack(gradients),
        query_out,
        key_out,
        value_out,
        output_out,
        gate_out,
        up_out,
        down_out,
        first_total,
        second_total,
        query_total,
        key_total,
    )


def solution(mesh):
    in_specs = (
        P("shard", ("ctx", "tp"), None),
        P("shard", "ctx"),
        P(),
        P(("shard", "ctx"), "tp"),
        P(("shard", "ctx"), "tp"),
        P(("shard", "ctx"), "tp"),
        P(),
        P(),
        P("tp", ("shard", "ctx")),
        P(),
        P(("shard", "ctx"), "tp"),
        P(("shard", "ctx"), "tp"),
        P("tp", ("shard", "ctx")),
        P("shard", ("ctx", "tp"), None),
    )
    out_specs = (
        P("shard", ("ctx", "tp"), None),
        P("shard", ("ctx", "tp"), None),
        P(("shard", "ctx"), "tp"),
        P(("shard", "ctx"), "tp"),
        P(("shard", "ctx"), "tp"),
        P("tp", ("shard", "ctx")),
        P(("shard", "ctx"), "tp"),
        P(("shard", "ctx"), "tp"),
        P("tp", ("shard", "ctx")),
        P(),
        P(),
        P(),
        P(),
    )
    return jax.shard_map(
        per_device, mesh=mesh, in_specs=in_specs, out_specs=out_specs, check_vma=False
    )
```

profile of v0, /device:TPU:6, one launch (start us, length us, event | category | flops | bytes accessed | tf_op | source)
XLA Modules:
  0.0 1651.3 jit_solution(1743868269783206539)
XLA Ops:
  24.2 36.3 %all-gather.18.cloned.1.call-done = bf16[1024,1024]{1,0:T(8,128)(2,1)} async-done(((bf16[256,1024]{1,0:T(8,128)(2,1)}), bf16[1024,1024]{1,0:T(8,128)(2,1)}) %all-gather.18.cloned.1.call-update) | async-done | bytes 2097168 | tf_op jit(solution)/shard_map/all_gather | solution.py:205
  63.6 43.7 %all-gather.32.cloned.1.call-done = bf16[1024,1024]{1,0:T(8,128)(2,1)} async-done(((bf16[256,1024]{1,0:T(8,128)(2,1)}), bf16[1024,1024]{1,0:T(8,128)(2,1)}) %all-gather.32.cloned.1.call-update) | async-done | bytes 2097168 | tf_op jit(solution)/shard_map/all_gather | solution.py:205
  161.9 84.9 %conditional.2 = (f32[2,2,1024]{2,1,0:T(2,128)}, f32[2,2,1024]{2,1,0:T(2,128)}, f32[2,2,1024,64]{2,3,1,0:T(8,128)S(1)}, f32[2,2,1024]{2,1,0:T(2,128)S(1)}) conditional(s32[]{:T(128)} %convert_element_type.260, () %tuple.36, (s32[1024]{0:T(1024)S(1)}, bf16[4096,2,64]{0,2,1:T(8,128)(2,1)}, bf16[1024,2,2,64]{0,3,2,1:T(8,128)(2,1)}, ...), branch_computations={%region_3.0_spmd, %region_4.7_spmd} | conditional | flops 4517261312 | bytes 226103360 | solution.py:106
  250.7 83.5 %conditional.3 = (f32[2,2,1024]{2,1,0:T(2,128)}, f32[2,2,1024]{2,1,0:T(2,128)}, f32[2,2,1024,64]{2,3,1,0:T(8,128)S(1)}, f32[2,2,1024]{2,1,0:T(2,128)S(1)}) conditional(s32[]{:T(128)} %convert_element_type.260, () %tuple.38, (s32[1024]{0:T(1024)S(1)}, bf16[4096,2,64]{0,2,1:T(8,128)(2,1)}, bf16[1024,2,2,64]{0,3,2,1:T(8,128)(2,1)S(1)}, ...), branch_computations={%region_13.14_spmd, %region_14.17_spmd} | conditional | flops 4517261312 | bytes 230297696 | solution.py:106
  337.9 42.9 %reduce-scatter.24.cloned.1.call-done = bf16[256,1024]{1,0:T(8,128)(2,1)} async-done(((bf16[1024,1024]{1,0:T(8,128)(2,1)}), bf16[256,1024]{1,0:T(8,128)(2,1)}) %reduce-scatter.24.cloned.1.call-update) | async-done | bytes 524304 | tf_op jit(solution)/shard_map/reduce_scatter | solution.py:232
  389.5 40.7 %all-gather.24.cloned.1.call-done = bf16[1024,1024]{1,0:T(8,128)(2,1)} async-done(((bf16[256,1024]{1,0:T(8,128)(2,1)}), bf16[1024,1024]{1,0:T(8,128)(2,1)}) %all-gather.24.cloned.1.call-update) | async-done | bytes 2097168 | tf_op jit(solution)/shard_map/all_gather | solution.py:240
  466.1 41.3 %all-gather.44.cloned.1.call-done = bf16[1,1024,1024]{2,1,0:T(8,128)(2,1)} async-done(((bf16[1,256,1024]{2,1,0:T(8,128)(2,1)}), bf16[1,1024,1024]{2,1,0:T(8,128)(2,1)}) %all-gather.44.cloned.1.call-update) | async-done | bytes 2097168 | tf_op jit(solution)/shard_map/all_gather | solution.py:264
  554.9 49.6 %all-gather.38.cloned.1.call-done = bf16[1024,1024]{1,0:T(8,128)(2,1)} async-done(((bf16[256,1024]{1,0:T(8,128)(2,1)}), bf16[1024,1024]{1,0:T(8,128)(2,1)}) %all-gather.38.cloned.1.call-update) | async-done | bytes 2097168 | tf_op jit(solution)/shard_map/all_gather | solution.py:240
  616.5 36.9 %all-gather.46.cloned.1.call-done = bf16[1,1024,1024]{2,1,0:T(8,128)(2,1)} async-done(((bf16[1,256,1024]{2,1,0:T(8,128)(2,1)}), bf16[1,1024,1024]{2,1,0:T(8,128)(2,1)}) %all-gather.46.cloned.1.call-update) | async-done | bytes 2097168 | tf_op jit(solution)/shard_map/all_gather | solution.py:264
  679.1 35.6 %reduce-scatter.36.cloned.1.call-done = bf16[256,1024]{1,0:T(8,128)(2,1)} async-done(((bf16[1024,1024]{1,0:T(8,128)(2,1)}), bf16[256,1024]{1,0:T(8,128)(2,1)}) %reduce-scatter.36.cloned.1.call-update) | async-done | bytes 524304 | tf_op jit(solution)/shard_map/reduce_scatter | solution.py:273
  717.6 42.7 %reduce-scatter.26.cloned.1.call-done = bf16[256,1024]{1,0:T(8,128)(2,1)} async-done(((bf16[1024,1024]{1,0:T(8,128)(2,1)}), bf16[256,1024]{1,0:T(8,128)(2,1)}) %reduce-scatter.26.cloned.1.call-update) | async-done | bytes 524304 | tf_op jit(solution)/shard_map/reduce_scatter | solution.py:246
  765.6 43.3 %all-gather.40.cloned.1.call-done = bf16[1024,1024]{1,0:T(8,128)(2,1)} async-done(((bf16[256,1024]{1,0:T(8,128)(2,1)}), bf16[1024,1024]{1,0:T(8,128)(2,1)}) %all-gather.40.cloned.1.call-update) | async-done | bytes 2097168 | tf_op jit(solution)/shard_map/all_gather | solution.py:283
  813.9 105.2 %while.30 = (s32[]{:T(128)}, f32[1024,2,2,64]{0,3,2,1:T(8,128)S(1)}, bf16[4096,2,64]{0,2,1:T(8,128)(2,1)}, bf16[4096,2,64]{0,2,1:T(8,128)(2,1)}, s32[]{:T(128)},...) while((s32[]{:T(128)}, ...), condition=%wide.region_23.24_spmd.clone, body=%wide.region_22.23_spmd.clone.sunk | while | flops 2728003584 | bytes 93126936 | solution.py:156
  925.0 103.5 %while.31 = (s32[]{:T(128)}, f32[1024,2,2,64]{0,3,2,1:T(8,128)S(1)}, bf16[4096,2,64]{0,2,1:T(8,128)(2,1)}, bf16[4096,2,64]{0,2,1:T(8,128)(2,1)}, s32[]{:T(128)},...) while((s32[]{:T(128)}, ...), condition=%wide.region_33.34_spmd.clone, body=%wide.region_32.33_spmd.clone.sunk | while | flops 2728003584 | bytes 99418456 | solution.py:156
  1042.9 78.1 %reduce-scatter.38.cloned.1.call-done = bf16[1024,2,64]{0,2,1:T(8,128)(2,1)} async-done(((bf16[4096,2,64]{0,2,1:T(8,128)(2,1)}), bf16[1024,2,64]{0,2,1:T(8,128)(2,1)}) %reduce-scatter.38.cloned.1.call-update) | async-done | bytes 262160 | tf_op jit(solution)/shard_map/reduce_scatter | solution.py:298
  1236.1 33.2 %reduce-scatter.42.cloned.1.call-done = bf16[256,1024]{1,0:T(8,128)(2,1)} async-done(((bf16[1024,1024]{1,0:T(8,128)(2,1)}), bf16[256,1024]{1,0:T(8,128)(2,1)}) %reduce-scatter.42.cloned.1.call-update) | async-done | bytes 524304 | tf_op jit(solution)/shard_map/reduce_scatter | solution.py:317
  1271.5 43.3 %reduce-scatter.22.cloned.1.call-done = bf16[256,1024]{1,0:T(8,128)(2,1)} async-done(((bf16[1024,1024]{1,0:T(8,128)(2,1)}), bf16[256,1024]{1,0:T(8,128)(2,1)}) %reduce-scatter.22.cloned.1.call-update) | async-done | bytes 524304 | tf_op jit(solution)/shard_map/reduce_scatter | solution.py:246
  1318.1 40.2 %all-reduce.8 = (f32[1024]{0:T(1024)}, f32[1024]{0:T(1024)}, f32[64]{0:T(128)}, f32[64]{0:T(128)}) all-reduce(f32[1024]{0:T(1024)S(1)} %add.369, f32[1024]{0:T(1024)S(1)} %add.370, f32[64]{0:T(128)S(1)} %add.371, f32[64]{0:T(128)S(1)} %add.372), channel_id=1, replica_groups=mesh['shard'=2,'ctx'=4,'tp'=4] {'shard','ctx','tp'}, use_global_device_ids=true, to_apply=%region_49.50 | all-reduce | flops 2176 | bytes 17408 | tf_op jit(solution)/shard_map/psum | solution.py:338
  1371.7 58.2 %reduce-scatter.54.cloned.1.call-done = f32[128,1152]{1,0:T(8,128)} async-done(((f32[1024,1152]{1,0:T(8,128)}), f32[128,1152]{1,0:T(8,128)}) %reduce-scatter.54.cloned.1.call-update) | async-done | bytes 589840 | tf_op jit(solution)/shard_map/reduce_scatter | solution.py:335
  1429.9 58.0 %reduce-scatter.56.cloned.1.call-done = f32[1152,128]{1,0:T(8,128)} async-done(((f32[1152,1024]{1,0:T(8,128)}), f32[1152,128]{1,0:T(8,128)}) %reduce-scatter.56.cloned.1.call-update) | async-done | bytes 589840 | tf_op jit(solution)/shard_map/reduce_scatter | solution.py:336
  1487.9 40.1 %reduce-scatter.44.cloned.1.call-done = f32[128,256]{1,0:T(8,128)} async-done(((f32[1024,256]{1,0:T(8,128)}), f32[128,256]{1,0:T(8,128)}) %reduce-scatter.44.cloned.1.call-update) | async-done | bytes 131088 | tf_op jit(solution)/shard_map/reduce_scatter | solution.py:330
  1528.0 40.1 %reduce-scatter.50.cloned.1.call-done = f32[256,128]{1,0:T(8,128)} async-done(((f32[256,1024]{1,0:T(8,128)}), f32[256,128]{1,0:T(8,128)}) %reduce-scatter.50.cloned.1.call-update) | async-done | bytes 131088 | tf_op jit(solution)/shard_map/reduce_scatter | solution.py:333
  1568.1 38.0 %reduce-scatter.46.cloned.1.call-done = f32[128,128]{1,0:T(8,128)} async-done(((f32[1024,128]{1,0:T(8,128)}), f32[128,128]{1,0:T(8,128)}) %reduce-scatter.46.cloned.1.call-update) | async-done | bytes 65552 | tf_op jit(solution)/shard_map/reduce_scatter | solution.py:331
  1606.1 37.7 %reduce-scatter.48.cloned.1.call-done = f32[128,128]{1,0:T(8,128)} async-done(((f32[1024,128]{1,0:T(8,128)}), f32[128,128]{1,0:T(8,128)}) %reduce-scatter.48.cloned.1.call-update) | async-done | bytes 65552 | tf_op jit(solution)/shard_map/reduce_scatter | solution.py:332
  (553 shorter events, 753.0 us)
Async XLA Ops:
  14.0 147.9 %all-gather.20.cloned.1.call-start = ((), (), s32[]{:S(2)}) async-start(), calls=%async_computation.20 | async-start | bytes 1310720 | tf_op jit(solution)/shard_map/all_gather | solution.py:83
  122.7 127.9 %all-gather.34.cloned.1.call-start = ((), (), s32[]{:S(2)}) async-start(), calls=%async_computation.29 | async-start | bytes 1310720 | tf_op jit(solution)/shard_map/all_gather | solution.py:83
  154.3 183.6 %reduce-scatter.20.cloned.1.call-start = ((), (), s32[]{:S(2)}) async-start(), calls=%async_computation.22 | async-start | bytes 2621440 | tf_op jit(solution)/shard_map/reduce_scatter | solution.py:232
  250.4 130.5 %reduce-scatter.24.cloned.1.call-start = ((), (), s32[]{:S(2)}) async-start(), calls=%async_computation.31 | async-start | bytes 2621440 | tf_op jit(solution)/shard_map/reduce_scatter | solution.py:232
  385.8 121.6 %all-gather.44.cloned.1.call-start = ((), (), s32[]{:S(2)}) async-start(), calls=%async_computation.51 | async-start | bytes 2621440 | tf_op jit(solution)/shard_map/all_gather | solution.py:264
  386.9 149.5 %all-gather.30.cloned.1.call-start = ((), (), s32[]{:S(2)}) async-start(), calls=%async_computation.26 | async-start | bytes 2654208 | tf_op jit(solution)/shard_map/all_gather | solution.py:69
  387.7 216.8 %all-gather.38.cloned.1.call-start = ((), (), s32[]{:S(2)}) async-start(), calls=%async_computation.32 | async-start | bytes 2621440 | tf_op jit(solution)/shard_map/all_gather | solution.py:240
  388.4 265.0 %all-gather.46.cloned.1.call-start = ((), (), s32[]{:S(2)}) async-start(), calls=%async_computation.52 | async-start | bytes 2621440 | tf_op jit(solution)/shard_map/all_gather | solution.py:264
  389.0 290.2 %reduce-scatter.28.cloned.1.call-start = ((), (), s32[]{:S(2)}) async-start(), calls=%async_computation.34 | async-start | bytes 2621440 | tf_op jit(solution)/shard_map/reduce_scatter | solution.py:273
  554.7 160.0 %reduce-scatter.36.cloned.1.call-start = ((), (), s32[]{:S(2)}) async-start(), calls=%async_computation.39 | async-start | bytes 2621440 | tf_op jit(solution)/shard_map/reduce_scatter | solution.py:273
  678.7 130.2 %all-gather.40.cloned.1.call-start = ((), (), s32[]{:S(2)}) async-start(), calls=%async_computation.35 | async-start | bytes 2621440 | tf_op jit(solution)/shard_map/all_gather | solution.py:283
  763.9 155.3 %all-gather.42.cloned.1.call-start = ((), (), s32[]{:S(2)}) async-start(), calls=%async_computation.40 | async-start | bytes 2621440 | tf_op jit(solution)/shard_map/all_gather | solution.py:283
  765.5 276.3 %reduce-scatter.30.cloned.1.call-start = ((), (), s32[]{:S(2)}) async-start(), calls=%async_computation.36 | async-start | bytes 1310720 | tf_op jit(solution)/shard_map/reduce_scatter | solution.py:298
  919.1 201.9 %reduce-scatter.38.cloned.1.call-start = ((), (), s32[]{:S(2)}) async-start(), calls=%async_computation.41 | async-start | bytes 1310720 | tf_op jit(solution)/shard_map/reduce_scatter | solution.py:298
  1032.0 144.3 %reduce-scatter.40.cloned.1.call-start = ((), (), s32[]{:S(2)}) async-start(), calls=%async_computation.42 | async-start | bytes 1310720 | tf_op jit(solution)/shard_map/reduce_scatter | solution.py:301
  1041.7 194.4 %reduce-scatter.34.cloned.1.call-start = ((), (), s32[]{:S(2)}) async-start(), calls=%async_computation.38 | async-start | bytes 2621440 | tf_op jit(solution)/shard_map/reduce_scatter | solution.py:317
  1181.9 132.9 %reduce-scatter.22.cloned.1.call-start = ((), (), s32[]{:S(2)}) async-start(), calls=%async_computation.27 | async-start | bytes 2621440 | tf_op jit(solution)/shard_map/reduce_scatter | solution.py:246
  1188.7 183.0 %reduce-scatter.52.cloned.1.call-start = ((), (), s32[]{:S(2)}) async-start(), calls=%async_computation.48 | async-start | bytes 5308416 | tf_op jit(solution)/shard_map/reduce_scatter | solution.py:334
  1198.9 231.0 %reduce-scatter.54.cloned.1.call-start = ((), (), s32[]{:S(2)}) async-start(), calls=%async_computation.49 | async-start | bytes 5308416 | tf_op jit(solution)/shard_map/reduce_scatter | solution.py:335
  1208.5 279.3 %reduce-scatter.56.cloned.1.call-start = ((), (), s32[]{:S(2)}) async-start(), calls=%async_computation.50 | async-start | bytes 5308416 | tf_op jit(solution)/shard_map/reduce_scatter | solution.py:336
  1219.0 309.0 %reduce-scatter.44.cloned.1.call-start = ((), (), s32[]{:S(2)}) async-start(), calls=%async_computation.44 | async-start | bytes 1179648 | tf_op jit(solution)/shard_map/reduce_scatter | solution.py:330
  1225.2 342.9 %reduce-scatter.50.cloned.1.call-start = ((), (), s32[]{:S(2)}) async-start(), calls=%async_computation.47 | async-start | bytes 1179648 | tf_op jit(solution)/shard_map/reduce_scatter | solution.py:333
  1229.4 376.6 %reduce-scatter.46.cloned.1.call-start = ((), (), s32[]{:S(2)}) async-start(), calls=%async_computation.45 | async-start | bytes 589824 | tf_op jit(solution)/shard_map/reduce_scatter | solution.py:331
  1232.7 411.1 %reduce-scatter.48.cloned.1.call-start = ((), (), s32[]{:S(2)}) async-start(), calls=%async_computation.46 | async-start | bytes 589824 | tf_op jit(solution)/shard_map/reduce_scatter | solution.py:332
  (159 other events, 5413.0 us)
Sparse Core Ops, SparseCore 0:
  13.4 47.0 all-gather.17
  62.7 44.5 all-gather.31
  129.3 17.8 all-gather.21
  148.5 17.9 all-gather.33
  167.9 16.7 all-gather.35
  250.5 43.3 reduce-scatter.19
  337.4 43.4 reduce-scatter.23
  554.8 64.2 reduce-scatter.27
  672.0 42.6 reduce-scatter.35
  717.1 43.1 reduce-scatter.25
  919.2 57.6 reduce-scatter.29
  1028.7 92.2 reduce-scatter.37
  1124.1 24.8 reduce-scatter.31
  1151.4 24.8 reduce-scatter.39
  1179.1 44.7 reduce-scatter.33
  1226.1 43.1 reduce-scatter.41
  1271.6 43.1 reduce-scatter.21
  1318.8 52.8 reduce-scatter.51
  1376.0 53.8 reduce-scatter.53
  1433.9 53.8 reduce-scatter.55
  1491.9 36.0 reduce-scatter.43
  1532.1 35.9 reduce-scatter.49
  1571.9 34.0 reduce-scatter.45
  1609.7 34.0 reduce-scatter.47
  (1 shorter events, 14.6 us)
Sparse Core Ops, SparseCore 1:
  339.6 27.4 all-gather.25
  385.3 44.9 all-gather.23
  432.0 26.7 all-gather.27
  460.9 46.5 all-gather.43
  509.3 27.0 all-gather.29
  538.6 65.8 all-gather.37
  606.0 47.3 all-gather.45
  764.0 44.8 all-gather.39
  810.9 44.3 all-gather.41
where the time goes:
time: 1660 us; the launch traced here: 1650 us
  waiting for transfers between devices  939 us (57%)
  matrix products  464 us (28%)
  other arithmetic  123 us (7%)
  blocking collectives  80.1 us (5%)
  local copies, waits for them, and re-layouts  23.6 us (1%)
  between operations  17.9 us (1%)
    all_gather x2, waiting for transfers between devices, per_device(): second_all = lax.all_gather(second, 'tp', axis=0, tiled=True)  90.2 us
    reduce_scatter x2, waiting for transfers between devices, per_device(): lax.psum_scatter(project_rows(hidden_b, down_full).astype(jnp.bfloat16),...  86.1 us
    all_gather x2, waiting for transfers between devices, per_device(): first_all = lax.all_gather(first, 'tp', axis=0, tiled=True)  80 us
    all_gather x2, waiting for transfers between devices, per_device(): upstream_all = lax.all_gather(upstream_b, 'tp', axis=0, tiled=True)  78.2 us
    reduce_scatter x2, waiting for transfers between devices, per_device(): lax.psum_scatter(key_buffer.astype(jnp.bfloat16), 'ctx', scatter_dimensio...  78.1 us
    dot_general x14, matrix products, dot_last(): lax.dot_general(left, right, (((1,), (1,)), ((), ())), preferred_element_...  64.4 us
    reduce_scatter x1, waiting for transfers between devices, per_device(): lax.psum_scatter(up_acc, ('shard', 'ctx'), scatter_dimension=0, tiled=True)  58.2 us
    reduce_scatter x1, waiting for transfers between devices, per_device(): lax.psum_scatter(down_acc, ('shard', 'ctx'), scatter_dimension=1, tiled=T...  58 us
  transfers between devices with their start and end apart: 34, of which 24 were waited for; matrix products, arithmetic and copies ran while one was open for 35% of the time, Pallas kernels for 0%

commit v1 on v0

v1 whole, which is shorter than its diff:
```python
import functools
import math

import jax
import jax.numpy as jnp
from jax import lax
from jax.experimental import pallas as pl
from jax.experimental.pallas import tpu as pltpu
from jax.sharding import PartitionSpec as P

EPS = 1e-05
THETA = 1000000.0
LOG2E = 1.4426950408889634
F32 = jnp.float32
BF16 = jnp.bfloat16
NEAR = [(0, 1), (1, 0), (2, 3), (3, 2)]
FAR = [(0, 2), (2, 0), (1, 3), (3, 1)]
LIMIT = 56 * 1024 * 1024


def dot_nn(left, right):
    return lax.dot_general(left, right, (((1,), (0,)), ((), ())), preferred_element_type=F32)


def dot_nt(left, right):
    return lax.dot_general(left, right, (((1,), (1,)), ((), ())), preferred_element_type=F32)


def dot_tn(left, right):
    return lax.dot_general(left, right, (((0,), (0,)), ((), ())), preferred_element_type=F32)


def swap_bits(j):
    return ((j & 1) << 1) | (j >> 1)


def gather_ctx(own):
    far = lax.ppermute(own, "ctx", FAR)
    near = lax.ppermute(own, "ctx", NEAR)
    both = lax.ppermute(far, "ctx", NEAR)
    return jnp.stack([own, far, near, both])


def reduce_ctx(parts):
    got = lax.ppermute(parts[2:], "ctx", NEAR)
    mine = parts[0].astype(F32) + got[0].astype(F32)
    away = (parts[1].astype(F32) + got[1].astype(F32)).astype(BF16)
    return mine + lax.ppermute(away, "ctx", FAR).astype(F32)


def gather_tp(own, count):
    up = [(i, i + 1) for i in range(count - 1)]
    down = [(i + 1, i) for i in range(count - 1)]
    from_low, from_high = [], []
    low = high = own
    for _ in range(count - 1):
        low = lax.ppermute(low, "tp", up)
        high = lax.ppermute(high, "tp", down)
        from_low.append(low)
        from_high.append(high)
    index = lax.axis_index("tp")
    slots = [own]
    for i in range(1, count):
        slots.append(jnp.where(index >= i, from_low[i - 1], from_high[count - i - 1]))
    return jnp.stack(slots)


def reduce_tp(parts, count):
    up = [(i, i + 1) for i in range(count - 1)]
    down = [(i + 1, i) for i in range(count - 1)]
    going_up = going_down = None
    for k in range(count - 1, 0, -1):
        high, low = parts[count - k], parts[k]
        if going_up is not None:
            high = (high.astype(F32) + going_up.astype(F32)).astype(BF16)
            low = (low.astype(F32) + going_down.astype(F32)).astype(BF16)
        going_up = lax.ppermute(high, "tp", up)
        going_down = lax.ppermute(low, "tp", down)
    return parts[0].astype(F32) + going_up.astype(F32) + going_down.astype(F32)


def sum_all(vector, sizes):
    for name, size in sizes:
        step = 1
        while step < size:
            other = lax.ppermute(vector, name, [(i, i ^ step) for i in range(size)])
            vector = vector + other
            step *= 2
    return vector


def params():
    return pltpu.CompilerParams(vmem_limit_bytes=LIMIT)


def head_sums(values):
    rows = lax.broadcasted_iota(jnp.int32, (128, 128), 0) >> 6
    columns = lax.broadcasted_iota(jnp.int32, (128, 128), 1) >> 6
    ones = jnp.where(rows == columns, 1.0, 0.0).astype(BF16)
    high = values.astype(BF16)
    rest = values - high.astype(F32)
    low = rest.astype(BF16)
    return dot_nn(high, ones) + dot_nn(low, ones)


def pad_heads(pair, low):
    zero = jnp.zeros_like(pair)
    return jnp.where(low, pair, zero), jnp.where(low, pltpu.roll(pair, 64, 1), zero)


def pad_heads_high(pair, low):
    zero = jnp.zeros_like(pair)
    return jnp.where(low, zero, pltpu.roll(pair, 64, 1)), jnp.where(low, zero, pair)


def pad_four(first, second, low):
    a, b = pad_heads(first, low)
    c, d = pad_heads_high(second, low)
    return a, b, c, d


def join_four(values, rows, low):
    a, b, c, d = (values[h * rows : (h + 1) * rows] for h in range(4))
    return jnp.where(low, a, pltpu.roll(b, 64, 1)), jnp.where(low, pltpu.roll(c, 64, 1), d)


def qkv_kernel(x_ref, w_ref, cos_ref, sin_ref, gain_ref, q_ref, kv_ref, raw_ref):
    rows = x_ref.shape[1]
    y = dot_nn(x_ref[0], w_ref[:, :512])
    raw_ref[0] = y[:, :384]
    lane = lax.broadcasted_iota(jnp.int32, (rows, 128), 1)
    early, low = (lane & 32) == 0, lane < 64
    cosine, sine = cos_ref[0], sin_ref[0]
    turned = []
    for b in range(3):
        u = y[:, b * 128 : (b + 1) * 128]
        r = lax.rsqrt(head_sums(u * u) * (1.0 / 64.0) + EPS)
        n = u * r * gain_ref[:, b * 128 : (b + 1) * 128]
        other = jnp.where(early, -pltpu.roll(n, 96, 1), pltpu.roll(n, 32, 1))
        turned.append(n * cosine + other * sine)
    heads = pad_four(turned[0] * 0.125, turned[1] * 0.125, low)
    for h in range(4):
        q_ref[0, h] = heads[h].astype(BF16)
    kv_ref[0, :, 0:128] = turned[2].astype(BF16)
    kv_ref[0, :, 128:256] = y[:, 384:512].astype(BF16)


def qkv_call(x, w, cosine, sine, gains):
    slots, rows, width = x.shape
    return pl.pallas_call(
        qkv_kernel,
        grid=(slots,),
        in_specs=[
            pl.BlockSpec((1, rows, width), lambda j: (j, 0, 0)),
            pl.BlockSpec(w.shape, lambda j: (0, 0)),
            pl.BlockSpec((1, rows, 128), lambda j: (j, 0, 0)),
            pl.BlockSpec((1, rows, 128), lambda j: (j, 0, 0)),
            pl.BlockSpec((1, 384), lambda j: (0, 0)),
        ],
        out_specs=[
            pl.BlockSpec((1, 4, rows, 128), lambda j: (j, 0, 0, 0)),
            pl.BlockSpec((1, rows, 256), lambda j: (j, 0, 0)),
            pl.BlockSpec((1, rows, 384), lambda j: (j, 0, 0)),
        ],
        out_shape=[
            jax.ShapeDtypeStruct((slots, 4, rows, 128), BF16),
            jax.ShapeDtypeStruct((slots, rows, 256), BF16),
            jax.ShapeDtypeStruct((slots, rows, 384), F32),
        ],
        compiler_params=params(),
        name="qkv",
    )(x, w, cosine, sine, gains)


def slot_of(n, c, t):
    return (t - (n & 3)) & 3, swap_bits(c ^ (n >> 2))


def attend_kernel(place_ref, q_ref, kv_ref, w_ref, o_ref, lse_ref, mixed_ref, part_ref, acc_ref, sum_ref):
    c, t, j = place_ref[0], place_ref[1], pl.program_id(0)
    rows = q_ref.shape[2]
    wide = 4 * rows
    queries = q_ref[0].reshape(wide, 128)
    acc_ref[...] = jnp.zeros_like(acc_ref)
    sum_ref[...] = jnp.zeros_like(sum_ref)

    def scores(n):
        i, jj = slot_of(n, c, t)
        keys = kv_ref[i, jj, :, 0:128]
        values = kv_ref[i, jj, :, 128:256]
        return jnp.exp2(dot_nt(keys, queries) * LOG2E), values

    def add(weights, values):
        sum_ref[...] += jnp.sum(weights, axis=0, keepdims=True)
        acc_ref[...] += dot_tn(values, weights.astype(BF16))

    last = 4 * (c ^ swap_bits(j)) + t

    def body(n, carry):
        add(*scores(n))
        return carry

    lax.fori_loop(0, last, body, 0)
    weights, values = scores(last)
    key = lax.broadcasted_iota(jnp.int32, (rows, wide), 0)
    query = lax.broadcasted_iota(jnp.int32, (rows, wide), 1) & (rows - 1)
    add(jnp.where(key <= query, weights, 0.0), values)
    total = sum_ref[...]
    out = acc_ref[...] / total
    o_ref[0] = out
    lse_ref[0] = jnp.log(total) * LOG2E
    low = lax.broadcasted_iota(jnp.int32, (rows, 128), 1) < 64
    first, second = join_four(jnp.transpose(out), rows, low)
    mixed = jnp.concatenate([first, second], axis=1).astype(BF16)
    mixed_ref[0] = mixed
    part_ref[0] = dot_nt(mixed, w_ref[:, 512:768]).astype(BF16)


def attend_call(place, q, kv, w):
    slots, _, rows, _ = q.shape
    width = w.shape[0]
    return pl.pallas_call(
        attend_kernel,
        grid=(slots,),
        in_specs=[
            pl.BlockSpec(memory_space=pltpu.SMEM),
            pl.BlockSpec((1, 4, rows, 128), lambda j: (j, 0, 0, 0)),
            pl.BlockSpec(kv.shape, lambda j: (0, 0, 0, 0)),
            pl.BlockSpec(w.shape, lambda j: (0, 0)),
        ],
        out_specs=[
            pl.BlockSpec((1, 128, 4 * rows), lambda j: (j, 0, 0)),
            pl.BlockSpec((1, 1, 4 * rows), lambda j: (j, 0, 0)),
            pl.BlockSpec((1, rows, 256), lambda j: (j, 0, 0)),
            pl.BlockSpec((1, rows, width), lambda j: (j, 0, 0)),
        ],
        out_shape=[
            jax.ShapeDtypeStruct((slots, 128, 4 * rows), F32),
            jax.ShapeDtypeStruct((slots, 1, 4 * rows), F32),
            jax.ShapeDtypeStruct((slots, rows, 256), BF16),
            jax.ShapeDtypeStruct((slots, rows, width), BF16),
        ],
        scratch_shapes=[pltpu.VMEM((128, 4 * rows), F32), pltpu.VMEM((1, 4 * rows), F32)],
        compiler_params=params(),
        name="attend",
    )(place, q, kv, w)


def attend_back_kernel(
    place_ref, q_ref, kv_ref, w_ref, o_ref, lse_ref, back_ref, dq_ref, dkv_ref, dk_ref, dv_ref, acc_ref
):
    c, t, j = place_ref[0], place_ref[1], pl.program_id(0)
    rows = q_ref.shape[2]
    wide = 4 * rows

    @pl.when(j == 0)
    def _():
        dk_ref[...] = jnp.zeros_like(dk_ref)
        dv_ref[...] = jnp.zeros_like(dv_ref)

    queries = q_ref[0].reshape(wide, 128)
    low = lax.broadcasted_iota(jnp.int32, (rows, 128), 1) < 64
    flat = dot_nn(back_ref[0], w_ref[:, 512:768])
    wide_back = jnp.concatenate(pad_four(flat[:, 0:128], flat[:, 128:256], low), axis=0).astype(BF16)
    delta = jnp.sum(jnp.transpose(wide_back.astype(F32)) * o_ref[0], axis=0, keepdims=True)
    lse = lse_ref[0]
    acc_ref[...] = jnp.zeros_like(acc_ref)

    def block(n, allowed):
        i, jj = slot_of(n, c, t)
        keys = kv_ref[i, jj, :, 0:128]
        values = kv_ref[i, jj, :, 128:256]
        probs = jnp.exp2(dot_nt(keys, queries) * LOG2E - lse)
        if allowed is not None:
            probs = jnp.where(allowed, probs, 0.0)
        slopes = dot_nt(values, wide_back)
        score_back = (probs * (slopes - delta)).astype(BF16)
        dv_ref[i, jj] += dot_nn(probs.astype(BF16), wide_back)
        dk_ref[i, jj] += dot_nn(score_back, queries)
        acc_ref[...] += dot_tn(score_back, keys)

    last = 4 * (c ^ swap_bits(j)) + t

    def body(n, carry):
        block(n, None)
        return carry

    lax.fori_loop(0, last, body, 0)
    key = lax.broadcasted_iota(jnp.int32, (rows, wide), 0)
    query = lax.broadcasted_iota(jnp.int32, (rows, wide), 1) & (rows - 1)
    block(last, key <= query)
    first, second = join_four(acc_ref[...] * 0.125, rows, low)
    dq_ref[0, :, 0:128] = first
    dq_ref[0, :, 128:256] = second

    @pl.when(j == pl.num_programs(0) - 1)
    def _():
        dkv_ref[:, :, :, 0:128] = dk_ref[...].astype(BF16)
        dkv_ref[:, :, :, 128:256] = dv_ref[...].astype(BF16)


def attend_back_call(place, q, kv, w, o, lse, back):
    slots, _, rows, _ = q.shape
    width = w.shape[0]
    return pl.pallas_call(
        attend_back_kernel,
        grid=(slots,),
        in_specs=[
            pl.BlockSpec(memory_space=pltpu.SMEM),
            pl.BlockSpec((1, 4, rows, 128), lambda j: (j, 0, 0, 0)),
            pl.BlockSpec(kv.shape, lambda j: (0, 0, 0, 0)),
            pl.BlockSpec(w.shape, lambda j: (0, 0)),
            pl.BlockSpec((1, 128, 4 * rows), lambda j: (j, 0, 0)),
            pl.BlockSpec((1, 1, 4 * rows), lambda j: (j, 0, 0)),
            pl.BlockSpec((1, rows, width), lambda j: (j, 0, 0)),
        ],
        out_specs=[
            pl.BlockSpec((1, rows, 256), lambda j: (j, 0, 0)),
            pl.BlockSpec(kv.shape, lambda j: (0, 0, 0, 0)),
        ],
        out_shape=[
            jax.ShapeDtypeStruct((slots, rows, 256), F32),
            jax.ShapeDtypeStruct(kv.shape, BF16),
        ],
        scratch_shapes=[
            pltpu.VMEM((*kv.shape[:3], 128), F32),
            pltpu.VMEM((*kv.shape[:3], 128), F32),
            pltpu.VMEM((4 * rows, 128), F32),
        ],
        compiler_params=params(),
        name="attend_back",
    )(place, q, kv, w, o, lse, back)


def qkv_back_kernel(dq_ref, dkv_ref, raw_ref, cos_ref, sin_ref, gain_ref, w_ref, back_ref, part_ref, share_ref):
    rows = dq_ref.shape[1]
    lane = lax.broadcasted_iota(jnp.int32, (rows, 128), 1)
    early = (lane & 32) == 0
    cosine, sine = cos_ref[0], sin_ref[0]

    @pl.when(pl.program_id(0) == 0)
    def _():
        share_ref[...] = jnp.zeros_like(share_ref)

    outs = []
    for b in range(3):
        given = dq_ref[0, :, b * 128 : (b + 1) * 128] if b < 2 else dkv_ref[0, :, 0:128]
        z = sine * given
        cotangent = given * cosine + jnp.where(early, pltpu.roll(z, 96, 1), -pltpu.roll(z, 32, 1))
        u = raw_ref[0, :, b * 128 : (b + 1) * 128]
        gain = gain_ref[:, b * 128 : (b + 1) * 128]
        r = lax.rsqrt(head_sums(u * u) * (1.0 / 64.0) + EPS)
        mean = head_sums(u * gain * cotangent) * (1.0 / 64.0)
        share_ref[:, b * 128 : (b + 1) * 128] += jnp.sum(cotangent * u * r, axis=0, keepdims=True)
        outs.append((r * gain * cotangent - u * (r * r * r) * mean).astype(BF16))
    outs.append(dkv_ref[0, :, 128:256].astype(BF16))
    back = jnp.concatenate(outs, axis=1)
    back_ref[0] = back
    part_ref[0] = dot_nt(back, w_ref[:, :512]).astype(BF16)


def qkv_back_call(dq, dkv, raw, cosine, sine, gains, w):
    slots, rows, _ = dq.shape
    width = w.shape[0]
    return pl.pallas_call(
        qkv_back_kernel,
        grid=(slots,),
        in_specs=[
            pl.BlockSpec((1, rows, 256), lambda j: (j, 0, 0)),
            pl.BlockSpec((1, rows, 256), lambda j: (j, 0, 0)),
            pl.BlockSpec((1, rows, 384), lambda j: (j, 0, 0)),
            pl.BlockSpec((1, rows, 128), lambda j: (j, 0, 0)),
            pl.BlockSpec((1, rows, 128), lambda j: (j, 0, 0)),
            pl.BlockSpec((1, 384), lambda j: (0, 0)),
            pl.BlockSpec(w.shape, lambda j: (0, 0)),
        ],
        out_specs=[
            pl.BlockSpec((1, rows, 512), lambda j: (j, 0, 0)),
            pl.BlockSpec((1, rows, width), lambda j: (j, 0, 0)),
            pl.BlockSpec((1, 384), lambda j: (0, 0)),
        ],
        out_shape=[
            jax.ShapeDtypeStruct((slots, rows, 512), BF16),
            jax.ShapeDtypeStruct((slots, rows, width), BF16),
            jax.ShapeDtypeStruct((1, 384), F32),
        ],
        compiler_params=params(),
        name="qkv_back",
    )(dq, dkv, raw, cosine, sine, gains, w)


def ffn_kernel(x_ref, up_ref, w_ref, hidden_ref, gate_back_ref, up_back_ref, part_ref, back_ref):
    slots, rows, width = x_ref.shape
    count = slots * rows
    x = x_ref[...].reshape(count, width)
    given = up_ref[...].reshape(count, width)
    gate = dot_nt(x, w_ref[0])
    up = dot_nt(x, w_ref[1])
    sig = jax.nn.sigmoid(gate)
    swish = gate * sig
    hidden = (swish * up).astype(BF16)
    hidden_ref[...] = hidden.reshape(hidden_ref.shape)
    part_ref[...] = dot_nn(hidden, w_ref[2]).astype(BF16).reshape(part_ref.shape)
    hidden_back = dot_nt(given, w_ref[2])
    gate_back = (hidden_back * up * (sig * (1.0 + gate * (1.0 - sig)))).astype(BF16)
    up_back = (hidden_back * swish).astype(BF16)
    gate_back_ref[...] = gate_back.reshape(gate_back_ref.shape)
    up_back_ref[...] = up_back.reshape(up_back_ref.shape)
    back = dot_nn(gate_back, w_ref[0]) + dot_nn(up_back, w_ref[1])
    back_ref[...] = back.astype(BF16).reshape(back_ref.shape)


def ffn_call(x, given, w):
    slots, rows, width = x.shape
    hidden = w.shape[1]
    step = 2
    token = pl.BlockSpec((step, rows, width), lambda j: (j, 0, 0))
    unit = pl.BlockSpec((step, rows, hidden), lambda j: (j, 0, 0))
    return pl.pallas_call(
        ffn_kernel,
        grid=(slots // step,),
        in_specs=[token, token, pl.BlockSpec(w.shape, lambda j: (0, 0, 0), pipeline_mode=pl.Buffered(1))],
        out_specs=[unit, unit, unit, token, token],
        out_shape=[jax.ShapeDtypeStruct((slots, rows, hidden), BF16)] * 3
        + [jax.ShapeDtypeStruct((slots, rows, width), BF16)] * 2,
        compiler_params=params(),
        name="ffn",
    )(x, given, w)


def inverse_root(values):
    return lax.rsqrt(jnp.mean(values * values, axis=-1, keepdims=True) + EPS)


def norm_back(values, root, gain, given):
    mean = jnp.mean(values * gain * given, axis=-1, keepdims=True)
    return root * gain * given - values * (root * root * root) * mean


def per_device(
    sizes,
    tokens,
    positions,
    first_gain,
    query_weight,
    key_weight,
    value_weight,
    query_gain,
    key_gain,
    output_weight,
    second_gain,
    gate_weight,
    up_weight,
    down_weight,
    upstream,
):
    shards, ctx, tp = sizes["shard"], sizes["ctx"], sizes["tp"]
    groups = ("shard", "tp")
    sequences, rows, width = tokens.shape
    head_dim = query_gain.shape[0]
    depth = query_weight.shape[0]
    units = gate_weight.shape[1]
    c, t = lax.axis_index("ctx"), lax.axis_index("tp")
    place = jnp.stack([c, t]).astype(jnp.int32)
    trade = [(i * tp + k, k * ctx + i) for i in range(ctx) for k in range(tp)]

    small = jnp.concatenate([query_weight, key_weight, value_weight, output_weight.T], axis=1)
    small = lax.ppermute(small, ("ctx", "tp"), trade)
    w_attn = lax.all_gather(small, groups, axis=0, tiled=True)

    large = jnp.stack([gate_weight.T, up_weight.T, down_weight]).reshape(3, ctx, units // ctx, depth)
    large = lax.all_to_all(large, "ctx", 1, 1, tiled=True)
    large = large.transpose(0, 2, 1, 3).reshape(3, units // ctx, ctx * depth)
    w_ffn = lax.all_gather(large, groups, axis=0, tiled=False)
    w_ffn = w_ffn.reshape(shards, tp, 3, units // ctx, ctx * depth)
    w_ffn = w_ffn.transpose(2, 1, 3, 0, 4).reshape(3, units, width)

    mine = lax.dynamic_slice_in_dim(positions, t * rows, rows, 1).astype(F32)
    places = gather_ctx(mine)
    freqs = jnp.exp(-math.log(THETA) * jnp.arange(0, head_dim, 2).astype(F32) / head_dim)
    angles = places[..., None] * freqs
    cosine, sine = jnp.cos(angles), jnp.sin(angles)
    cosine = jnp.concatenate([cosine] * 4, axis=-1)
    sine = jnp.concatenate([sine] * 4, axis=-1)
    gains = jnp.concatenate([jnp.tile(query_gain, 4), jnp.tile(key_gain, 2)])[None]

    x = tokens.astype(F32)
    root = inverse_root(x)
    first = (x * root * first_gain).astype(BF16)
    given = upstream.astype(F32)

    first_all = [gather_ctx(first[s]) for s in range(sequences)]
    q, kv, raw = [], [], []
    for s in range(sequences):
        one = qkv_call(first_all[s], w_attn, cosine[:, s], sine[:, s], gains)
        q.append(one[0])
        kv.append(gather_tp(one[1], tp))
        raw.append(one[2])
    upstream_all = [gather_ctx(upstream[s]) for s in range(sequences)]
    attended = [attend_call(place, q[s], kv[s], w_attn) for s in range(sequences)]
    results, second_share, back_rows, mixed_back_all = [], 0.0, [], []
    seconds, ffn = [], []
    for s in range(sequences):
        middle = x[s] + reduce_ctx(attended[s][3])
        middle_root = inverse_root(middle)
        second = (middle * middle_root * second_gain).astype(BF16)
        second_all = gather_ctx(second)
        seconds.append(second_all)
        hidden, gate_back, up_back, part, back_part = ffn_call(second_all, upstream_all[s], w_ffn)
        ffn.append((hidden, gate_back, up_back))
        second_back = reduce_ctx(back_part)
        middle_back = given[s] + norm_back(middle, middle_root, second_gain, second_back)
        second_share = second_share + jnp.sum(second_back * middle * middle_root, axis=0)
        back_rows.append(middle_back)
        mixed_back_all.append(gather_ctx(middle_back.astype(BF16)))
        results.append((middle + reduce_ctx(part)).astype(BF16))

    flat = lambda v: v.reshape(-1, v.shape[-1])
    grads = []
    for left, right in ((1, seconds), (2, seconds), (0, upstream_all)):
        total = 0.0
        for s in range(sequences):
            total = total + dot_tn(flat(ffn[s][left]), flat(right[s]))
        grads.append(total.astype(BF16))
    g_ffn = jnp.stack(grads).reshape(3, tp, units // ctx, shards, ctx * depth)
    g_ffn = g_ffn.transpose(3, 1, 0, 2, 4).reshape(shards * tp * 3, units // ctx, ctx * depth)
    g_ffn = lax.psum_scatter(g_ffn, groups, scatter_dimension=0, tiled=True)
    g_ffn = g_ffn.reshape(3, units // ctx, ctx, depth).transpose(0, 2, 1, 3)
    g_ffn = lax.all_to_all(g_ffn, "ctx", 1, 1, tiled=True)
    g_ffn = g_ffn.reshape(3, units, depth).astype(F32)

    gradients, first_share, head_share = [], 0.0, 0.0
    g_out, g_qkv = 0.0, 0.0
    for s in range(sequences):
        o, lse, mixed, _ = attended[s]
        dq, dkv = attend_back_call(place, q[s], kv[s], w_attn, o, lse, mixed_back_all[s])
        g_out = g_out + dot_tn(flat(mixed_back_all[s]), flat(mixed))
        dkv = reduce_tp(dkv, tp)
        back, part, share = qkv_back_call(dq, dkv, raw[s], cosine[:, s], sine[:, s], gains, w_attn)
        head_share = head_share + share
        g_qkv = g_qkv + dot_tn(flat(first_all[s]), flat(back))
        first_back = reduce_ctx(part)
        gradients.append(back_rows[s] + norm_back(x[s], root[s], first_gain, first_back))
        first_share = first_share + jnp.sum(first_back * x[s] * root[s], axis=0)

    g_attn = jnp.concatenate([g_qkv, g_out], axis=1).astype(BF16)
    g_attn = lax.psum_scatter(g_attn, groups, scatter_dimension=0, tiled=True)
    g_attn = lax.ppermute(g_attn, ("ctx", "tp"), trade).astype(F32)
    heads = query_weight.shape[1]
    pairs = key_weight.shape[1]

    shares = jnp.concatenate([first_share, second_share, head_share[0]])
    shares = sum_all(shares, [(name, sizes[name]) for name in ("ctx", "shard", "tp")])
    head_total = shares[2 * width :]
    return (
        jnp.stack(results),
        jnp.stack(gradients),
        g_attn[:, :heads],
        g_attn[:, heads : heads + pairs],
        g_attn[:, heads + pairs : heads + 2 * pairs],
        g_attn[:, heads + 2 * pairs :].T,
        g_ffn[0].T,
        g_ffn[1].T,
        g_ffn[2],
        shares[:width],
        shares[width : 2 * width],
        jnp.sum(head_total[: 4 * head_dim].reshape(4, head_dim), axis=0),
        jnp.sum(head_total[4 * head_dim :].reshape(2, head_dim), axis=0),
    )


def solution(mesh):
    rows = P("shard", ("ctx", "tp"), None)
    wide = P(("shard", "ctx"), "tp")
    tall = P("tp", ("shard", "ctx"))
    none = P()
    in_specs = (
        rows, P("shard", "ctx"), none, wide, wide, wide, none, none, tall, none, wide, wide, tall, rows,
    )
    out_specs = (rows, rows, wide, wide, wide, tall, wide, wide, tall, none, none, none, none)
    sizes = {name: mesh.shape[name] for name in ("shard", "ctx", "tp")}
    return jax.shard_map(
        functools.partial(per_device, sizes), mesh=mesh, in_specs=in_specs, out_specs=out_specs, check_vma=False
    )
```

time: 1660 us -> 972 us (0.59)
  waiting for transfers between devices: 939 us -> 389 us
  matrix products: 464 us -> 43.7 us
  Pallas kernels: 0 us -> 174 us
  starting transfers between devices: 3.94 us -> 150 us
  local copies, waits for them, and re-layouts: 23.6 us -> 113 us
  blocking collectives: 80.1 us -> 14.1 us
  other arithmetic: 123 us -> 58.2 us
    reduce_scatter x19 -> x1, waiting for transfers between devices: 592 us -> 95.8 us  [per_device(): g_ffn = lax.psum_scatter(g_ffn, groups, scatter_dimension=0, tiled=True)]
    dot_general x76 -> x10, matrix products: 464 us -> 43.7 us  [dot_tn(): lax.dot_general(left, right, (((0,), (0,)), ((), ())), preferred_element_...]
    all_gather x15 -> x2, waiting for transfers between devices: 342 us -> 0.01 us  [the longest x1 0.01 us: per_device(): w_attn = lax.all_gather(small, groups, axis=0, tiled=True)]
    ppermute x0 -> x74, waiting for transfers between devices: none -> 285 us  [the longest x8 87.3 us: reduce_ctx(): return mine + lax.ppermute(away, 'ctx', FAR).astype(F32)]
    pallas_call x0 -> x10, Pallas kernels: none -> 174 us  [the longest x2 63.6 us: attend_back_call(): pl.pallas_call(attend_back_kernel, grid=(slots,), in_specs=[pl.BlockSpec(...]
    ppermute x0 -> x74, starting transfers between devices: none -> 146 us  [the longest x6 62 us: reduce_tp(): going_up = lax.ppermute(high, 'tp', up)]
    reduce_sum x8 -> x7, other arithmetic: 58.9 us -> 7.76 us  [the longest x2 2.89 us: inverse_root(): return lax.rsqrt(jnp.mean(values * values, axis=-1, keepdims=True) + EPS)]
    psum x1 -> x0, blocking collectives: 40.2 us -> none  [per_device(): lax.psum((first_gain_acc, second_gain_acc, query_gain_acc, key_gain_acc),...]
  transfers between devices with their start and end apart: 34 -> 79, of which waited for: 24 -> 42; matrix products, arithmetic and copies ran while one was open for 35% -> 15% of each run, Pallas kernels for 0% -> 13%
where the time goes in v1:
time: 972 us; the launch traced here: 958 us
  waiting for transfers between devices  389 us (40%)
  Pallas kernels  174 us (18%)
  starting transfers between devices  150 us (15%)
  local copies, waits for them, and re-layouts  113 us (12%)
  other arithmetic  58.2 us (6%)
  matrix products  43.7 us (4%)
  between operations  15.6 us (2%)
  blocking collectives  14.1 us (1%)
    reduce_scatter x1, waiting for transfers between devices, per_device(): g_ffn = lax.psum_scatter(g_ffn, groups, scatter_dimension=0, tiled=True)  95.8 us
    ppermute x8, waiting for transfers between devices, reduce_ctx(): return mine + lax.ppermute(away, 'ctx', FAR).astype(F32)  87.3 us
    ppermute x6, waiting for transfers between devices, gather_tp(): high = lax.ppermute(high, 'tp', down)  87.2 us
    ppermute x9, waiting for transfers between devices, gather_ctx(): far = lax.ppermute(own, 'ctx', FAR)  71.5 us
    pallas_call x2, Pallas kernels, attend_back_call(): pl.pallas_call(attend_back_kernel, grid=(slots,), in_specs=[pl.BlockSpec(...  63.6 us
    ppermute x6, starting transfers between devices, reduce_tp(): going_up = lax.ppermute(high, 'tp', up)  62 us
    pallas_call x2, Pallas kernels, ffn_call(): pl.pallas_call(ffn_kernel, grid=(slots // step,), in_specs=[token, token,...  45 us
    dot_general x10, matrix products, dot_tn(): lax.dot_general(left, right, (((0,), (0,)), ((), ())), preferred_element_...  43.7 us
  transfers between devices with their start and end apart: 79, of which 42 were waited for; matrix products, arithmetic and copies ran while one was open for 15% of the time, Pallas kernels for 13%

profile of v1, /device:TPU:6, one launch (start us, length us, event | category | flops | bytes accessed | tf_op | source)
XLA Modules:
  0.0 957.8 jit_solution(15571136678088434672)
XLA Ops:
  13.6 10.8 %collective-permute-done.3 = bf16[128,768]{1,0:T(8,128)(2,1)S(1)} collective-permute-done((bf16[128,768]{1,0:T(8,128)(2,1)S(1)}, bf16[128,768]{1,0:T(8,128)(2,1)S(1)}, u32[]{:S(2)}, u32[]{:S(2)}) %collective-permute-start.3) | collective-permute-done | bytes 196640 | tf_op jit(solution)/shard_map/ppermute | solution.py:468
  27.6 14.1 %all_to_all.10 = bf16[3,4,288,128]{3,2,0,1:T(8,128)(2,1)S(1)} all-to-all(bf16[3,4,288,128]{3,2,0,1:T(8,128)(2,1)S(1)} %copy.130), channel_id=1, replica_groups=mesh['shard'=2,'ctx'=4,'tp'=4] {'ctx'}, dimensions={1} | all-to-all | bytes 1769472 | tf_op jit(solution)/shard_map/all_to_all | solution.py:472
  62.5 10.8 %collective-permute-done = bf16[256,1024]{1,0:T(8,128)(2,1)} collective-permute-done((bf16[256,1024]{1,0:T(8,128)(2,1)}, bf16[256,1024]{1,0:T(8,128)(2,1)}, u32[]{:S(2)}, u32[]{:S(2)}) %collective-permute-start) | collective-permute-done | bytes 524320 | tf_op jit(solution)/shard_map/ppermute | solution.py:38
  106.5 13.7 %collective-permute-done.27 = bf16[4,256,256]{2,1,0:T(8,128)(2,1)S(1)} collective-permute-done((bf16[4,256,256]{2,1,0:T(8,128)(2,1)}, bf16[4,256,256]{2,1,0:T(8,128)(2,1)S(1)}, u32[]{:S(2)}, u32[]{:S(2)}) %collective-permute-start.27) | collective-permute-done | bytes 524320 | tf_op jit(solution)/shard_map/ppermute | solution.py:58
  138.7 19.3 %collective-permute-done.28 = bf16[4,256,256]{2,1,0:T(8,128)(2,1)} collective-permute-done((bf16[4,256,256]{2,1,0:T(8,128)(2,1)S(1)}, bf16[4,256,256]{2,1,0:T(8,128)(2,1)}, u32[]{:S(2)}, u32[]{:S(2)}) %collective-permute-start.28) | collective-permute-done | bytes 524320 | tf_op jit(solution)/shard_map/ppermute | solution.py:58
  163.8 29.9 %collective-permute-done.9 = bf16[4,256,256]{2,1,0:T(8,128)(2,1)} collective-permute-done((bf16[4,256,256]{2,1,0:T(8,128)(2,1)S(1)}, bf16[4,256,256]{2,1,0:T(8,128)(2,1)}, u32[]{:S(2)}, u32[]{:S(2)}) %collective-permute-start.9) | collective-permute-done | bytes 524320 | tf_op jit(solution)/shard_map/ppermute | solution.py:58
  202.0 19.8 %collective-permute-done.29 = bf16[4,256,256]{2,1,0:T(8,128)(2,1)S(1)} collective-permute-done((bf16[4,256,256]{2,1,0:T(8,128)(2,1)}, bf16[4,256,256]{2,1,0:T(8,128)(2,1)S(1)}, u32[]{:S(2)}, u32[]{:S(2)}) %collective-permute-start.29) | collective-permute-done | bytes 524320 | tf_op jit(solution)/shard_map/ppermute | solution.py:58
  224.5 19.1 %attend.3 = (f32[4,128,1024]{2,1,0:T(8,128)}, f32[4,1,1024]{2,1,0:T(1,128)}, bf16[4,256,256]{2,1,0:T(8,128)(2,1)}, bf16[4,256,1024]{2,1,0:T(8,128)(2,1)}) custom-call(s32[2]{0:T(128)} %pad_add_fusion.place_ref, bf16[4,4,256,128]{3,2,1,0:T(8,128)(2,1)} %get-tuple-element.51.q_ref, bf16[4,4,256,256]{3,2,1,0:T(8,128)(2,1)} %pad_maximum_fusion.6.kv_ref, ...), custom_call_target="tpu_custom_call" | custom-call | tf_op jit(solution)/shard_map/attend/pallas_call | solution.py:222
  247.6 19.1 %attend.2 = (f32[4,128,1024]{2,1,0:T(8,128)}, f32[4,1,1024]{2,1,0:T(1,128)}, bf16[4,256,256]{2,1,0:T(8,128)(2,1)}, bf16[4,256,1024]{2,1,0:T(8,128)(2,1)}) custom-call(s32[2]{0:T(128)} %pad_add_fusion.place_ref, bf16[4,4,256,128]{3,2,1,0:T(8,128)(2,1)} %get-tuple-element.47.q_ref, bf16[4,4,256,256]{3,2,1,0:T(8,128)(2,1)} %pad_maximum_fusion.2.kv_ref, ...), custom_call_target="tpu_custom_call" | custom-call | tf_op jit(solution)/shard_map/attend/pallas_call | solution.py:222
  283.7 11.2 %collective-permute-done.14 = bf16[256,1024]{1,0:T(8,128)(2,1)S(1)} collective-permute-done((bf16[256,1024]{1,0:T(8,128)(2,1)S(1)}, bf16[256,1024]{1,0:T(8,128)(2,1)S(1)}, u32[]{:S(2)}, u32[]{:S(2)}) %collective-permute-start.14) | collective-permute-done | bytes 524320 | tf_op jit(solution)/shard_map/ppermute | solution.py:48
  322.1 27.5 %copy.132 = bf16[3,4,288,2,512]{4,3,2,1,0:T(2,128)(2,1)} copy(bf16[3,4,288,2,512]{4,2,0,1,3:T(8,128)(2,1)} %bitcast.284) | data formatting | bytes 14155776 | tf_op jit(solution)/shard_map/transpose | solution.py:476
  349.5 16.6 %reshape.275.w_ref = bf16[3,1152,1024]{2,1,0:T(8,128)(2,1)} reshape(bf16[3,4,288,2,512]{4,3,2,1,0:T(2,128)(2,1)} %copy.132) | data formatting | bytes 14155776 | tf_op jit(solution)/shard_map/reshape | solution.py:476
  366.1 22.6 %ffn.2 = (bf16[4,256,1152]{2,1,0:T(8,128)(2,1)}, bf16[4,256,1152]{2,1,0:T(8,128)(2,1)}, bf16[4,256,1152]{2,1,0:T(8,128)(2,1)}, bf16[4,256,1024]{2,1,0:T(8,128)(2,1)}, bf16[4,256,1024]{2,1,0:T(8,128)(2,1)}) custom-call(bf16[4,256,1024]{2,1,0:T(8,128)(2,1)} %pad_maximum_fusion.3.x_ref, bf16[4,256,1024]{2,1,0:T(8,128)(2,1)} %pad_maximum_fusion.4.up_ref, ...), custom_call_target="tpu_custom_call" | custom-call | tf_op jit(solution)/shard_map/ffn/pallas_call | solution.py:419
  396.8 11.2 %collective-permute-done.22 = bf16[256,1024]{1,0:T(8,128)(2,1)S(1)} collective-permute-done((bf16[256,1024]{1,0:T(8,128)(2,1)S(1)}, bf16[256,1024]{1,0:T(8,128)(2,1)S(1)}, u32[]{:S(2)}, u32[]{:S(2)}) %collective-permute-start.22) | collective-permute-done | bytes 524320 | tf_op jit(solution)/shard_map/ppermute | solution.py:48
  408.0 11.2 %collective-permute-done.43 = bf16[256,1024]{1,0:T(8,128)(2,1)S(1)} collective-permute-done((bf16[256,1024]{1,0:T(8,128)(2,1)S(1)}, bf16[256,1024]{1,0:T(8,128)(2,1)S(1)}, u32[]{:S(2)}, u32[]{:S(2)}) %collective-permute-start.43) | collective-permute-done | bytes 524320 | tf_op jit(solution)/shard_map/ppermute | solution.py:48
  444.7 22.4 %ffn.3 = (bf16[4,256,1152]{2,1,0:T(8,128)(2,1)}, bf16[4,256,1152]{2,1,0:T(8,128)(2,1)}, bf16[4,256,1152]{2,1,0:T(8,128)(2,1)}, bf16[4,256,1024]{2,1,0:T(8,128)(2,1)}, bf16[4,256,1024]{2,1,0:T(8,128)(2,1)}) custom-call(bf16[4,256,1024]{2,1,0:T(8,128)(2,1)} %pad_maximum_fusion.7.x_ref, bf16[4,256,1024]{2,1,0:T(8,128)(2,1)} %pad_maximum_fusion.8.up_ref, ...), custom_call_target="tpu_custom_call" | custom-call | tf_op jit(solution)/shard_map/ffn/pallas_call | solution.py:419
  474.1 12.2 %collective-permute-done.41 = bf16[256,1024]{1,0:T(8,128)(2,1)S(1)} collective-permute-done((bf16[256,1024]{1,0:T(8,128)(2,1)S(1)}, bf16[256,1024]{1,0:T(8,128)(2,1)S(1)}, u32[]{:S(2)}, u32[]{:S(2)}) %collective-permute-start.41) | collective-permute-done | bytes 524320 | tf_op jit(solution)/shard_map/ppermute | solution.py:48
  503.9 12.8 %collective-permute-done.44 = bf16[256,1024]{1,0:T(8,128)(2,1)S(1)} collective-permute-done((bf16[256,1024]{1,0:T(8,128)(2,1)S(1)}, bf16[256,1024]{1,0:T(8,128)(2,1)S(1)}, u32[]{:S(2)}, u32[]{:S(2)}) %collective-permute-start.44) | collective-permute-done | bytes 524320 | tf_op jit(solution)/shard_map/ppermute | solution.py:38
  528.2 31.9 %attend_back.2 = (f32[4,256,256]{2,1,0:T(8,128)}, bf16[4,4,256,256]{3,2,1,0:T(8,128)(2,1)}) custom-call(s32[2]{0:T(128)} %pad_add_fusion.place_ref, bf16[4,4,256,128]{3,2,1,0:T(8,128)(2,1)} %get-tuple-element.47.q_ref, bf16[4,4,256,256]{3,2,1,0:T(8,128)(2,1)} %pad_maximum_fusion.2.kv_ref, bf16[1024,768]{1,0:T(8,128)(2,1)} %all-gather.3.cloned.1.call-done.w_ref, ...), custom_call_target="tpu_custom_call" | custom-call | tf_op jit(solution)/shard_map/attend_back/pallas_call | solution.py:305
  580.5 31.7 %attend_back.3 = (f32[4,256,256]{2,1,0:T(8,128)}, bf16[4,4,256,256]{3,2,1,0:T(8,128)(2,1)}) custom-call(s32[2]{0:T(128)} %pad_add_fusion.place_ref, bf16[4,4,256,128]{3,2,1,0:T(8,128)(2,1)} %get-tuple-element.51.q_ref, bf16[4,4,256,256]{3,2,1,0:T(8,128)(2,1)} %pad_maximum_fusion.6.kv_ref, bf16[1024,768]{1,0:T(8,128)(2,1)} %all-gather.3.cloned.1.call-done.w_ref, ...), custom_call_target="tpu_custom_call" | custom-call | tf_op jit(solution)/shard_map/attend_back/pallas_call | solution.py:305
  613.7 14.9 %collective-permute-start.60 = (bf16[4,256,256]{2,1,0:T(8,128)(2,1)S(1)}, bf16[4,256,256]{2,1,0:T(8,128)(2,1)S(1)}, u32[]{:S(2)}, u32[]{:S(2)}) collective-permute-start(bf16[4,256,256]{2,1,0:T(8,128)(2,1)S(1)} %get-tuple-element.172), channel_id=1, source_target_pairs={{0,1},{1,2},{2,3},{4,5},{5,6},{6,7},{8,9},{9,10},{10,11},{12,13},{... | collective-permute-start | bytes 1572872 | tf_op jit(solution)/shard_map/ppermute | solution.py:77
  630.1 14.7 %collective-permute-start.48 = (bf16[4,256,256]{2,1,0:T(8,128)(2,1)S(1)}, bf16[4,256,256]{2,1,0:T(8,128)(2,1)S(1)}, u32[]{:S(2)}, u32[]{:S(2)}) collective-permute-start(bf16[4,256,256]{2,1,0:T(8,128)(2,1)S(1)} %get-tuple-element.176), channel_id=1, source_target_pairs={{0,1},{1,2},{2,3},{4,5},{5,6},{6,7},{8,9},{9,10},{10,11},{12,13},{... | collective-permute-start | bytes 1572872 | tf_op jit(solution)/shard_map/ppermute | solution.py:77
  780.7 12.4 %collective-permute-done.67 = bf16[256,1024]{1,0:T(8,128)(2,1)S(1)} collective-permute-done((bf16[256,1024]{1,0:T(8,128)(2,1)S(1)}, bf16[256,1024]{1,0:T(8,128)(2,1)S(1)}, u32[]{:S(2)}, u32[]{:S(2)}) %collective-permute-start.67) | collective-permute-done | bytes 524320 | tf_op jit(solution)/shard_map/ppermute | solution.py:48
  834.2 95.8 %reduce-scatter.5.cloned.1.call-done = bf16[3,288,512]{2,1,0:T(8,128)(2,1)} async-done(((bf16[24,288,512]{2,1,0:T(8,128)(2,1)}), bf16[3,288,512]{2,1,0:T(8,128)(2,1)}) %reduce-scatter.5.cloned.1.call-update) | async-done | bytes 884752 | tf_op jit(solution)/shard_map/reduce_scatter | solution.py:527
  (479 shorter events, 436.4 us)
Async XLA Ops:
  7.2 74.1 %all-gather.3.cloned.1.call-start = ((), (), s32[]{:S(2)}) async-start(), calls=%async_computation.4 | async-start | bytes 1769472 | tf_op jit(solution)/shard_map/all_gather | solution.py:469
  25.0 297.0 %all-gather.5.cloned.1.call-start = ((), (), s32[]{:S(2)}) async-start(), calls=%async_computation.5 | async-start | bytes 7962624 | tf_op jit(solution)/shard_map/all_gather | solution.py:474
  43.5 785.8 %reduce-scatter.7.cloned.1.call-start = ((), (), s32[]{:S(2)}) async-start(), calls=%async_computation.7 | async-start | bytes 1769472
  88.0 32.1 %collective-permute-start.27 = (bf16[4,256,256]{2,1,0:T(8,128)(2,1)}, bf16[4,256,256]{2,1,0:T(8,128)(2,1)S(1)}, u32[]{:S(2)}, u32[]{:S(2)}) collective-permute-start(bf16[4,256,256]{2,1,0:T(8,128)(2,1)} %get-tuple-element.52), channel_id=1, source_target_pairs={{1,0},{2,1},{3,2},{5,4},{6,5},{7,6},{9,8},{10,9},{11,10},{13,12},{... | collective-permute-start | bytes 1572872 | tf_op jit(solution)/shard_map/ppermute | solution.py:58
  89.3 32.1 %collective-permute-start.26 = (bf16[4,256,256]{2,1,0:T(8,128)(2,1)}, bf16[4,256,256]{2,1,0:T(8,128)(2,1)S(1)}, u32[]{:S(2)}, u32[]{:S(2)}) collective-permute-start(bf16[4,256,256]{2,1,0:T(8,128)(2,1)} %get-tuple-element.52), channel_id=1, source_target_pairs={{0,1},{1,2},{2,3},{4,5},{5,6},{6,7},{8,9},{9,10},{10,11},{12,13},{... | collective-permute-start | bytes 1572872 | tf_op jit(solution)/shard_map/ppermute | solution.py:57
  101.9 30.8 %collective-permute-start.7 = (bf16[4,256,256]{2,1,0:T(8,128)(2,1)}, bf16[4,256,256]{2,1,0:T(8,128)(2,1)S(1)}, u32[]{:S(2)}, u32[]{:S(2)}) collective-permute-start(bf16[4,256,256]{2,1,0:T(8,128)(2,1)} %get-tuple-element.48), channel_id=1, source_target_pairs={{0,1},{1,2},{2,3},{4,5},{5,6},{6,7},{8,9},{9,10},{10,11},{12,13},{... | collective-permute-start | bytes 1572872 | tf_op jit(solution)/shard_map/ppermute | solution.py:57
  120.1 37.8 %collective-permute-start.28 = (bf16[4,256,256]{2,1,0:T(8,128)(2,1)S(1)}, bf16[4,256,256]{2,1,0:T(8,128)(2,1)}, u32[]{:S(2)}, u32[]{:S(2)}) collective-permute-start(bf16[4,256,256]{2,1,0:T(8,128)(2,1)S(1)} %collective-permute-done.27), channel_id=1, source_target_pairs={{1,0},{2,1},{3,2},{5,4},{6,5},{7,6},{9,8},{10,9},{11,10},{13,12},{... | collective-permute-start | bytes 1572872 | tf_op jit(solution)/shard_map/ppermute | solution.py:58
  121.4 37.8 %collective-permute-start.30 = (bf16[4,256,256]{2,1,0:T(8,128)(2,1)S(1)}, bf16[4,256,256]{2,1,0:T(8,128)(2,1)}, u32[]{:S(2)}, u32[]{:S(2)}) collective-permute-start(bf16[4,256,256]{2,1,0:T(8,128)(2,1)S(1)} %collective-permute-done.26), channel_id=1, source_target_pairs={{0,1},{1,2},{2,3},{4,5},{5,6},{6,7},{8,9},{9,10},{10,11},{12,13},{... | collective-permute-start | bytes 1572872 | tf_op jit(solution)/shard_map/ppermute | solution.py:57
  131.4 62.4 %collective-permute-start.9 = (bf16[4,256,256]{2,1,0:T(8,128)(2,1)S(1)}, bf16[4,256,256]{2,1,0:T(8,128)(2,1)}, u32[]{:S(2)}, u32[]{:S(2)}) collective-permute-start(bf16[4,256,256]{2,1,0:T(8,128)(2,1)S(1)} %collective-permute-done.8), channel_id=1, source_target_pairs={{1,0},{2,1},{3,2},{5,4},{6,5},{7,6},{9,8},{10,9},{11,10},{13,12},{... | collective-permute-start | bytes 1572872 | tf_op jit(solution)/shard_map/ppermute | solution.py:58
  132.7 62.4 %collective-permute-start.11 = (bf16[4,256,256]{2,1,0:T(8,128)(2,1)S(1)}, bf16[4,256,256]{2,1,0:T(8,128)(2,1)}, u32[]{:S(2)}, u32[]{:S(2)}) collective-permute-start(bf16[4,256,256]{2,1,0:T(8,128)(2,1)S(1)} %collective-permute-done.7), channel_id=1, source_target_pairs={{0,1},{1,2},{2,3},{4,5},{5,6},{6,7},{8,9},{9,10},{10,11},{12,13},{... | collective-permute-start | bytes 1572872 | tf_op jit(solution)/shard_map/ppermute | solution.py:57
  157.9 63.8 %collective-permute-start.29 = (bf16[4,256,256]{2,1,0:T(8,128)(2,1)}, bf16[4,256,256]{2,1,0:T(8,128)(2,1)S(1)}, u32[]{:S(2)}, u32[]{:S(2)}) collective-permute-start(bf16[4,256,256]{2,1,0:T(8,128)(2,1)} %collective-permute-done.28), channel_id=1, source_target_pairs={{1,0},{2,1},{3,2},{5,4},{6,5},{7,6},{9,8},{10,9},{11,10},{13,12},{... | collective-permute-start | bytes 1572872 | tf_op jit(solution)/shard_map/ppermute | solution.py:58
  159.2 62.6 %collective-permute-start.31 = (bf16[4,256,256]{2,1,0:T(8,128)(2,1)}, bf16[4,256,256]{2,1,0:T(8,128)(2,1)S(1)}, u32[]{:S(2)}, u32[]{:S(2)}) collective-permute-start(bf16[4,256,256]{2,1,0:T(8,128)(2,1)} %collective-permute-done.30), channel_id=1, source_target_pairs={{0,1},{1,2},{2,3},{4,5},{5,6},{6,7},{8,9},{9,10},{10,11},{12,13},{... | collective-permute-start | bytes 1572872 | tf_op jit(solution)/shard_map/ppermute | solution.py:57
  193.8 51.4 %collective-permute-start.10 = (bf16[4,256,256]{2,1,0:T(8,128)(2,1)}, bf16[4,256,256]{2,1,0:T(8,128)(2,1)S(1)}, u32[]{:S(2)}, u32[]{:S(2)}) collective-permute-start(bf16[4,256,256]{2,1,0:T(8,128)(2,1)} %collective-permute-done.9), channel_id=1, source_target_pairs={{1,0},{2,1},{3,2},{5,4},{6,5},{7,6},{9,8},{10,9},{11,10},{13,12},{... | collective-permute-start | bytes 1572872 | tf_op jit(solution)/shard_map/ppermute | solution.py:58
  195.1 50.1 %collective-permute-start.12 = (bf16[4,256,256]{2,1,0:T(8,128)(2,1)}, bf16[4,256,256]{2,1,0:T(8,128)(2,1)S(1)}, u32[]{:S(2)}, u32[]{:S(2)}) collective-permute-start(bf16[4,256,256]{2,1,0:T(8,128)(2,1)} %collective-permute-done.11), channel_id=1, source_target_pairs={{0,1},{1,2},{2,3},{4,5},{5,6},{6,7},{8,9},{9,10},{10,11},{12,13},{... | collective-permute-start | bytes 1572872 | tf_op jit(solution)/shard_map/ppermute | solution.py:57
  274.1 32.1 %collective-permute-start.18 = (bf16[256,1024]{1,0:T(8,128)(2,1)S(1)}, bf16[256,1024]{1,0:T(8,128)(2,1)S(1)}, u32[]{:S(2)}, u32[]{:S(2)}) collective-permute-start(bf16[256,1024]{1,0:T(8,128)(2,1)S(1)} %get-tuple-element.188), channel_id=1, source_target_pairs={{0,8},{8,0},{4,12},{12,4},{1,9},{9,1},{5,13},{13,5},{2,10},{10,2},... | collective-permute-start | bytes 1572872 | tf_op jit(solution)/shard_map/ppermute | solution.py:38
  395.5 34.9 %collective-permute-start.37 = (bf16[256,1024]{1,0:T(8,128)(2,1)S(1)}, bf16[256,1024]{1,0:T(8,128)(2,1)S(1)}, u32[]{:S(2)}, u32[]{:S(2)}) collective-permute-start(bf16[256,1024]{1,0:T(8,128)(2,1)S(1)} %copy-done.41), channel_id=1, source_target_pairs={{0,8},{8,0},{4,12},{12,4},{1,9},{9,1},{5,13},{13,5},{2,10},{10,2},... | collective-permute-start | bytes 1572872 | tf_op jit(solution)/shard_map/ppermute | solution.py:38
  521.1 56.8 %collective-permute-start.58 = (bf16[256,1024]{1,0:T(8,128)(2,1)}, bf16[256,1024]{1,0:T(8,128)(2,1)S(1)}, u32[]{:S(2)}, u32[]{:S(2)}) collective-permute-start(bf16[256,1024]{1,0:T(8,128)(2,1)} %get-tuple-element.166), channel_id=1, source_target_pairs={{0,4},{4,0},{8,12},{12,8},{1,5},{5,1},{9,13},{13,9},{2,6},{6,2},{1... | collective-permute-start | bytes 1572872 | tf_op jit(solution)/shard_map/ppermute | solution.py:39
  526.5 51.4 %collective-permute-start.59 = (bf16[256,1024]{1,0:T(8,128)(2,1)S(1)}, bf16[256,1024]{1,0:T(8,128)(2,1)S(1)}, u32[]{:S(2)}, u32[]{:S(2)}) collective-permute-start(bf16[256,1024]{1,0:T(8,128)(2,1)S(1)} %collective-permute-done.57), channel_id=1, source_target_pairs={{0,4},{4,0},{8,12},{12,8},{1,5},{5,1},{9,13},{13,9},{2,6},{6,2},{1... | collective-permute-start | bytes 1572872 | tf_op jit(solution)/shard_map/ppermute | solution.py:40
  561.6 68.3 %collective-permute-start.47 = (bf16[4,256,256]{2,1,0:T(8,128)(2,1)S(1)}, bf16[4,256,256]{2,1,0:T(8,128)(2,1)S(1)}, u32[]{:S(2)}, u32[]{:S(2)}) collective-permute-start(bf16[4,256,256]{2,1,0:T(8,128)(2,1)S(1)} %get-tuple-element.178), channel_id=1, source_target_pairs={{0,1},{1,2},{2,3},{4,5},{5,6},{6,7},{8,9},{9,10},{10,11},{12,13},{... | collective-permute-start | bytes 1572872 | tf_op jit(solution)/shard_map/ppermute | solution.py:77
  570.6 59.3 %collective-permute-start.50 = (bf16[4,256,256]{2,1,0:T(8,128)(2,1)S(1)}, bf16[4,256,256]{2,1,0:T(8,128)(2,1)S(1)}, u32[]{:S(2)}, u32[]{:S(2)}) collective-permute-start(bf16[4,256,256]{2,1,0:T(8,128)(2,1)S(1)} %get-tuple-element.179), channel_id=1, source_target_pairs={{1,0},{2,1},{3,2},{5,4},{6,5},{7,6},{9,8},{10,9},{11,10},{13,12},{... | collective-permute-start | bytes 1572872 | tf_op jit(solution)/shard_map/ppermute | solution.py:78
  613.7 34.5 %collective-permute-start.60 = (bf16[4,256,256]{2,1,0:T(8,128)(2,1)S(1)}, bf16[4,256,256]{2,1,0:T(8,128)(2,1)S(1)}, u32[]{:S(2)}, u32[]{:S(2)}) collective-permute-start(bf16[4,256,256]{2,1,0:T(8,128)(2,1)S(1)} %get-tuple-element.172), channel_id=1, source_target_pairs={{0,1},{1,2},{2,3},{4,5},{5,6},{6,7},{8,9},{9,10},{10,11},{12,13},{... | collective-permute-start | bytes 1572872 | tf_op jit(solution)/shard_map/ppermute | solution.py:77
  630.1 34.5 %collective-permute-start.48 = (bf16[4,256,256]{2,1,0:T(8,128)(2,1)S(1)}, bf16[4,256,256]{2,1,0:T(8,128)(2,1)S(1)}, u32[]{:S(2)}, u32[]{:S(2)}) collective-permute-start(bf16[4,256,256]{2,1,0:T(8,128)(2,1)S(1)} %get-tuple-element.176), channel_id=1, source_target_pairs={{0,1},{1,2},{2,3},{4,5},{5,6},{6,7},{8,9},{9,10},{10,11},{12,13},{... | collective-permute-start | bytes 1572872 | tf_op jit(solution)/shard_map/ppermute | solution.py:77
  715.6 214.4 %reduce-scatter.5.cloned.1.call-start = ((), (), s32[]{:S(2)}) async-start(), calls=%async_computation.6 | async-start | bytes 7962624 | tf_op jit(solution)/shard_map/reduce_scatter | solution.py:527
  830.4 107.0 %collective-permute-start.68 = (bf16[128,768]{0,1:T(8,128)(2,1)S(1)}, bf16[128,768]{0,1:T(8,128)(2,1)S(1)}, u32[]{:S(2)}, u32[]{:S(2)}) collective-permute-start(bf16[128,768]{0,1:T(8,128)(2,1)S(1)} %copy.164), channel_id=1, source_target_pairs={{0,0},{1,4},{2,8},{3,12},{4,1},{5,5},{6,9},{7,13},{8,2},{9,6},{10,... | collective-permute-start | bytes 589832 | tf_op jit(solution)/shard_map/ppermute | solution.py:548
  (150 other events, 1847.3 us)
Sparse Core Ops, SparseCore 0:
  25.2 41.8 all-gather.2
  69.2 162.1 all-gather.4
  715.7 69.6 reduce-scatter.6
  789.4 140.4 reduce-scatter.4

commit v2 on v1

v2 whole, which is shorter than its diff:
```python
import functools
import math

import jax
import jax.numpy as jnp
from jax import lax
from jax.experimental import pallas as pl
from jax.experimental.pallas import tpu as pltpu
from jax.sharding import PartitionSpec as P

EPS = 1e-05
THETA = 1000000.0
LOG2E = 1.4426950408889634
F32 = jnp.float32
BF16 = jnp.bfloat16
NEAR = [(0, 1), (1, 0), (2, 3), (3, 2)]
FAR = [(0, 2), (2, 0), (1, 3), (3, 1)]
CROSS = [(0, 3), (3, 0), (1, 2), (2, 1)]
LIMIT = 56 * 1024 * 1024


def dot_nn(left, right):
    return lax.dot_general(left, right, (((1,), (0,)), ((), ())), preferred_element_type=F32)


def dot_nt(left, right):
    return lax.dot_general(left, right, (((1,), (1,)), ((), ())), preferred_element_type=F32)


def dot_tn(left, right):
    return lax.dot_general(left, right, (((0,), (0,)), ((), ())), preferred_element_type=F32)


def swap_bits(j):
    return ((j & 1) << 1) | (j >> 1)


def gather_ctx(own):
    far = lax.ppermute(own, "ctx", FAR)
    near = lax.ppermute(own, "ctx", NEAR)
    return [own, far, near, lax.ppermute(far, "ctx", NEAR)]


def add_near(own, got):
    return own[0].astype(F32) + got[0].astype(F32), (own[1].astype(F32) + got[1].astype(F32)).astype(BF16)


def reduce_near(own, near):
    return add_near(own, lax.ppermute(near, "ctx", NEAR))


def reduce_far(mine, away):
    return mine + lax.ppermute(away, "ctx", FAR).astype(F32)


def reduce_ctx(own, near):
    got = lax.ppermute(own[1], "ctx", FAR), lax.ppermute(near[0], "ctx", NEAR), lax.ppermute(near[1], "ctx", CROSS)
    return own[0].astype(F32) + got[0].astype(F32) + got[1].astype(F32) + got[2].astype(F32)


def to_tp(value, e):
    return lax.ppermute(value, "tp", [(i, i ^ e) for i in range(4)])


def exchange_tp(blocks):
    return [blocks[0]] + [to_tp(blocks[e], e) for e in range(1, len(blocks))]


def exchange_heads(q_same, q_other, kv):
    return [q_same, to_tp(q_other, 1), kv[0], to_tp(kv[1], 1), to_tp(kv[2], 2), to_tp(kv[3], 3)]


def gather_shard(own, shards):
    if shards == 2:
        return [own, lax.ppermute(own, "shard", [(0, 1), (1, 0)])]
    every = lax.all_gather(own, "shard", axis=0, tiled=False)
    return [every.transpose(1, 2, 0, 3).reshape(*own.shape[:2], -1)]


def send_shard(parts, shards):
    if shards == 2:
        return lax.ppermute(parts[1], "shard", [(0, 1), (1, 0)])
    blocks, units, width = parts[0].shape
    every = parts[0].reshape(blocks, units, shards, width // shards).transpose(2, 0, 1, 3)
    return lax.psum_scatter(every, "shard", scatter_dimension=0, tiled=False)


def add_shard(got, parts):
    return (parts[0].astype(F32) + got.astype(F32)).astype(BF16) if len(parts) == 2 else got


def after(value, *others):
    return lax.optimization_barrier((value, *others))[0]


class Line:
    def __init__(self):
        self.last = ()

    def run(self, call, first, *others):
        result = call(after(first, *self.last), *others)
        self.last = (jax.tree.leaves(result)[0],)
        return result


def trade_tp(own, count):
    got = [own]
    for k in range(1, count):
        got.append(lax.ppermute(own, "tp", [(i, i ^ k) for i in range(count)]))
    index = lax.axis_index("tp")
    slots = []
    for slot in range(count):
        value = got[slot]
        for at in range(1, count):
            value = jnp.where(index == at, got[slot ^ at], value)
        slots.append(value)
    return jnp.stack(slots)


def join_shard(own, shards):
    if shards == 2:
        other = lax.ppermute(own, "shard", [(0, 1), (1, 0)])
        index = lax.axis_index("shard")
        return jnp.concatenate([jnp.where(index == 0, own, other), jnp.where(index == 0, other, own)])
    return lax.all_gather(own, "shard", axis=0, tiled=True)


def sum_all(vector, sizes):
    for name, size in sizes:
        step = 1
        while step < size:
            other = lax.ppermute(vector, name, [(i, i ^ step) for i in range(size)])
            vector = vector + other
            step *= 2
    return vector


def params():
    return pltpu.CompilerParams(vmem_limit_bytes=LIMIT)


def cost(micros):
    return pl.CostEstimate(flops=int(micros * 1.0e9), transcendentals=0, bytes_accessed=int(micros * 1.0e6))


def slot_copies(refs, held, sems):
    return [pltpu.make_async_copy(ref, held.at[k], sems.at[k]) for k, ref in enumerate(refs)]


def start_slots(refs, held, sems):
    @pl.when(pl.program_id(0) == 0)
    def _():
        for copy in slot_copies(refs, held, sems):
            copy.start()


def wait_slot(refs, held, sems, step=1):
    for k, copy in enumerate(slot_copies(refs, held, sems)):

        @pl.when(pl.program_id(0) == k // step)
        def _():
            copy.wait()


def lanes_low(rows):
    return lax.broadcasted_iota(jnp.int32, (rows, 128), 1) < 64


def pack(first, second, low):
    return jnp.where(low, first, second)


def head_sums(values):
    rows = lax.broadcasted_iota(jnp.int32, (128, 128), 0) >> 6
    columns = lax.broadcasted_iota(jnp.int32, (128, 128), 1) >> 6
    ones = jnp.where(rows == columns, 1.0, 0.0).astype(BF16)
    high = values.astype(BF16)
    rest = values - high.astype(F32)
    low = rest.astype(BF16)
    return dot_nn(high, ones) + dot_nn(low, ones)


def qkv_kernel(place_ref, *refs):
    x_refs, (w_ref, cos_ref, sin_ref, gain_ref) = refs[:4], refs[4:8]
    q_same, q_other, kv_same, kv_other, raw_ref, x_ref, q_ref, kv_ref, sems = refs[8:]
    side, j = place_ref[1] & 1, pl.program_id(0)
    rows = x_ref.shape[1]
    start_slots(x_refs, x_ref, sems)
    wait_slot(x_refs, x_ref, sems)
    y = dot_nn(x_ref[j], w_ref[:, :512])
    raw_ref[0] = y[:, :384]
    low = lanes_low(rows)
    early = (lax.broadcasted_iota(jnp.int32, (rows, 128), 1) & 32) == 0
    cosine, sine = cos_ref[0, 0], sin_ref[0, 0]
    turned = []
    for b in range(3):
        u = y[:, b * 128 : (b + 1) * 128]
        r = lax.rsqrt(head_sums(u * u) * (1.0 / 64.0) + EPS)
        n = u * r * gain_ref[:, b * 128 : (b + 1) * 128]
        other = jnp.where(early, -pltpu.roll(n, 96, 1), pltpu.roll(n, 32, 1))
        turned.append(n * cosine + other * sine)
    key, value = turned[2], y[:, 384:512]
    q_ref[0] = (turned[0] * 0.125).astype(BF16)
    q_ref[1] = (turned[1] * 0.125).astype(BF16)
    kv_ref[0] = pack(key, pltpu.roll(value, 64, 1), low).astype(BF16)
    kv_ref[1] = pack(pltpu.roll(key, 64, 1), value, low).astype(BF16)
    q_same[0] = q_ref[side]
    q_other[0] = q_ref[1 - side]
    kv_same[0] = kv_ref[side]
    kv_other[0] = kv_ref[1 - side]


def qkv_call(place, at, xs, w, cosine, sine, gains):
    slots = len(xs)
    rows, width = xs[0].shape
    return pl.pallas_call(
        qkv_kernel,
        grid=(slots,),
        in_specs=[pl.BlockSpec(memory_space=pltpu.SMEM)]
        + [pl.BlockSpec(memory_space=pl.ANY)] * slots
        + [
            pl.BlockSpec(w.shape, lambda j: (0, 0)),
            pl.BlockSpec((1, 1, rows, 128), lambda j: (j, at, 0, 0)),
            pl.BlockSpec((1, 1, rows, 128), lambda j: (j, at, 0, 0)),
            pl.BlockSpec((1, 384), lambda j: (0, 0)),
        ],
        out_specs=[pl.BlockSpec((1, rows, 128), lambda j: (j, 0, 0))] * 4
        + [pl.BlockSpec((1, rows, 384), lambda j: (j, 0, 0))],
        out_shape=[jax.ShapeDtypeStruct((slots, rows, 128), BF16)] * 4
        + [jax.ShapeDtypeStruct((slots, rows, 384), F32)],
        scratch_shapes=[
            pltpu.VMEM((slots, rows, width), BF16),
            pltpu.VMEM((2, rows, 128), BF16),
            pltpu.VMEM((2, rows, 128), BF16),
            pltpu.SemaphoreType.DMA((slots,)),
        ],
        compiler_params=params(),
        cost_estimate=cost(7),
        name="qkv",
    )(place, *xs, w, cosine, sine, gains)


def lay_keys(place_ref, refs, kv_ref):
    c, t = place_ref[0], place_ref[1]
    for e, ref in enumerate(refs):
        for j in range(ref.shape[0]):
            kv_ref[4 * (c ^ swap_bits(j)) + (t ^ e)] = ref[j]


def lay_rows(place_ref, own_ref, got_ref, out_ref, high):
    c, side = place_ref[0], place_ref[1] & 1
    low = lanes_low(own_ref.shape[1])
    for ref, start in ((own_ref, 2 * side), (got_ref, 2 - 2 * side)):
        for j in range(ref.shape[0]):
            g = c ^ swap_bits(j)
            value = ref[j]
            turned = pltpu.roll(value, 64, 1)
            zero = jnp.zeros_like(value)
            if high:
                out_ref[g, start] = jnp.where(low, zero, turned)
                out_ref[g, start + 1] = jnp.where(low, zero, value)
            else:
                out_ref[g, start] = jnp.where(low, value, zero)
                out_ref[g, start + 1] = jnp.where(low, turned, zero)


def diagonal(rows, wide, edge):
    key = lax.broadcasted_iota(jnp.int32, (rows, wide), 0)
    column = lax.broadcasted_iota(jnp.int32, (rows, wide), 1)
    return (key <= (column & (rows - 1))) | (column >= edge)


def whole(shape):
    return pl.BlockSpec(shape, lambda j: (0,) * len(shape))


def attend_kernel(place_ref, *refs):
    q_own, q_got, keys = refs[0], refs[1], refs[2:6]
    own_out, other_out, o_ref, lse_ref, q_ref, kv_ref, acc_ref, sum_ref, ret_ref = refs[6:]
    c, t, g = place_ref[0], place_ref[1], pl.program_id(0)
    side, base = t & 1, t & 2
    rows = kv_ref.shape[1]
    half, wide = 2 * rows, 4 * rows

    @pl.when(g == 0)
    def _():
        lay_keys(place_ref, keys, kv_ref)
        lay_rows(place_ref, q_own, q_got, q_ref, False)

    queries = q_ref[g].reshape(wide, 128)
    acc_ref[...] = jnp.zeros_like(acc_ref)
    sum_ref[...] = jnp.zeros_like(sum_ref)

    def add(pair, skip, allowed):
        weights = jnp.exp2(dot_nt(pair, queries[skip:]) * LOG2E)
        if allowed is not None:
            weights = jnp.where(allowed, weights, 0.0)
        sum_ref[:, skip:] += jnp.sum(weights, axis=0, keepdims=True)
        acc_ref[:, skip:] += dot_tn(pair, weights.astype(BF16))

    def body(n, carry):
        add(kv_ref[pl.ds(2 * n, 2)].reshape(2 * rows, 128), 0, None)
        return carry

    last = 4 * g + base
    lax.fori_loop(0, last >> 1, body, 0)
    add(kv_ref[last], 0, diagonal(rows, wide, half))
    add(kv_ref[last + 1], half, diagonal(rows, half, half))
    total = sum_ref[...]
    out = acc_ref[...] / total
    o_ref[0] = out[64:]
    lse_ref[0] = jnp.log(total) * LOG2E
    flat = jnp.transpose(out)
    low = lanes_low(rows)
    slot = swap_bits(c ^ g)
    for u in range(2):
        first, second = (flat[(2 * u + h) * rows : (2 * u + h + 1) * rows] for h in range(2))
        ret_ref[u, slot] = pack(pltpu.roll(first, 64, 1), second, low).astype(BF16)

    @pl.when(g == pl.num_programs(0) - 1)
    def _():
        own_out[...] = ret_ref[side]
        other_out[...] = ret_ref[1 - side]


def attend_call(place, gets):
    slots, rows, _ = gets[0].shape
    wide = 4 * rows
    return pl.pallas_call(
        attend_kernel,
        grid=(4,),
        in_specs=[pl.BlockSpec(memory_space=pltpu.SMEM)] + [whole(gets[0].shape)] * 6,
        out_specs=[whole(gets[0].shape)] * 2
        + [
            pl.BlockSpec((1, 64, wide), lambda j: (j, 0, 0)),
            pl.BlockSpec((1, 1, wide), lambda j: (j, 0, 0)),
        ],
        out_shape=[jax.ShapeDtypeStruct(gets[0].shape, BF16)] * 2
        + [
            jax.ShapeDtypeStruct((4, 64, wide), F32),
            jax.ShapeDtypeStruct((4, 1, wide), F32),
        ],
        scratch_shapes=[
            pltpu.VMEM((4, 4, rows, 128), BF16),
            pltpu.VMEM((4 * slots, rows, 128), BF16),
            pltpu.VMEM((128, wide), F32),
            pltpu.VMEM((1, wide), F32),
            pltpu.VMEM((2, slots, rows, 128), BF16),
        ],
        compiler_params=params(),
        cost_estimate=cost(17),
        name="attend",
    )(place, *gets)


def out_kernel(place_ref, get_own, get_other, w_ref, mixed_ref, own_ref, near_ref, head_ref):
    side, j = place_ref[1] & 1, pl.program_id(0)
    head_ref[side] = get_own[0]
    head_ref[1 - side] = get_other[0]
    mixed = jnp.concatenate([head_ref[0], head_ref[1]], axis=1)
    mixed_ref[0] = mixed
    part = dot_nt(mixed, w_ref[:, 512:]).astype(BF16)

    @pl.when(j < 2)
    def _():
        own_ref[0] = part

    @pl.when(j >= 2)
    def _():
        near_ref[0] = part


def out_call(place, gets, w):
    slots, rows, _ = gets[0].shape
    width = w.shape[0]
    return pl.pallas_call(
        out_kernel,
        grid=(slots,),
        in_specs=[pl.BlockSpec(memory_space=pltpu.SMEM)]
        + [pl.BlockSpec((1, rows, 128), lambda j: (j, 0, 0))] * 2
        + [whole(w.shape)],
        out_specs=[
            pl.BlockSpec((1, rows, 256), lambda j: (j, 0, 0)),
            pl.BlockSpec((1, rows, width), lambda j: (jnp.minimum(j, 1), 0, 0)),
            pl.BlockSpec((1, rows, width), lambda j: (jnp.maximum(j - 2, 0), 0, 0)),
        ],
        out_shape=[
            jax.ShapeDtypeStruct((slots, rows, 256), BF16),
            jax.ShapeDtypeStruct((2, rows, width), BF16),
            jax.ShapeDtypeStruct((2, rows, width), BF16),
        ],
        scratch_shapes=[pltpu.VMEM((2, rows, 128), BF16)],
        compiler_params=params(),
        cost_estimate=cost(4),
        name="out",
    )(place, *gets, w)


def out_back_kernel(place_ref, *refs):
    x_refs, w_ref, own_out, other_out, x_ref, send_ref, sems = refs[0:4], *refs[4:]
    side, j = place_ref[1] & 1, pl.program_id(0)
    start_slots(x_refs, x_ref, sems)
    wait_slot(x_refs, x_ref, sems)
    back = dot_nn(x_ref[j], w_ref[:, 512:]).astype(BF16)
    send_ref[0] = back[:, :128]
    send_ref[1] = back[:, 128:]
    own_out[0] = send_ref[side]
    other_out[0] = send_ref[1 - side]


def out_back_call(place, xs, w):
    slots = len(xs)
    rows, width = xs[0].shape
    return pl.pallas_call(
        out_back_kernel,
        grid=(slots,),
        in_specs=[pl.BlockSpec(memory_space=pltpu.SMEM)]
        + [pl.BlockSpec(memory_space=pl.ANY)] * slots
        + [whole(w.shape)],
        out_specs=[pl.BlockSpec((1, rows, 128), lambda j: (j, 0, 0))] * 2,
        out_shape=[jax.ShapeDtypeStruct((slots, rows, 128), BF16)] * 2,
        scratch_shapes=[
            pltpu.VMEM((slots, rows, width), BF16),
            pltpu.VMEM((2, rows, 128), BF16),
            pltpu.SemaphoreType.DMA((slots,)),
        ],
        compiler_params=params(),
        cost_estimate=cost(4),
        name="out_back",
    )(place, *xs, w)


def attend_back_kernel(place_ref, *refs):
    q_own, q_got, keys, back_own, back_got = refs[0], refs[1], refs[2:6], refs[6], refs[7]
    o_ref, lse_ref, own_out, other_out, outs = refs[8], refs[9], refs[10], refs[11], refs[12:16]
    q_ref, kv_ref, back_ref, dkv_ref, acc_ref, ret_ref = refs[16:]
    c, t, g = place_ref[0], place_ref[1], pl.program_id(0)
    side, base = t & 1, t & 2
    rows = kv_ref.shape[1]
    half, wide = 2 * rows, 4 * rows

    @pl.when(g == 0)
    def _():
        lay_keys(place_ref, keys, kv_ref)
        lay_rows(place_ref, q_own, q_got, q_ref, False)
        lay_rows(place_ref, back_own, back_got, back_ref, True)
        dkv_ref[...] = jnp.zeros_like(dkv_ref)

    queries = q_ref[g].reshape(wide, 128)
    given = back_ref[g].reshape(wide, 128)
    delta = jnp.sum(jnp.transpose(given.astype(F32))[64:] * o_ref[0], axis=0, keepdims=True)
    lse = lse_ref[0]
    acc_ref[...] = jnp.zeros_like(acc_ref)

    def block(pair, skip, allowed):
        probs = jnp.exp2(dot_nt(pair, queries[skip:]) * LOG2E - lse[:, skip:])
        if allowed is not None:
            probs = jnp.where(allowed, probs, 0.0)
        slopes = dot_nt(pair, given[skip:])
        score_back = (probs * (slopes - delta[:, skip:])).astype(BF16)
        acc_ref[skip:] += dot_tn(score_back, pair)
        return dot_nn(probs.astype(BF16), given[skip:]) + dot_nn(score_back, queries[skip:])

    def body(n, carry):
        pair = kv_ref[pl.ds(2 * n, 2)].reshape(2 * rows, 128)
        dkv_ref[pl.ds(2 * n, 2)] += block(pair, 0, None).reshape(2, rows, 128)
        return carry

    last = 4 * g + base
    lax.fori_loop(0, last >> 1, body, 0)
    dkv_ref[last] += block(kv_ref[last], 0, diagonal(rows, wide, half))
    dkv_ref[last + 1] += block(kv_ref[last + 1], half, diagonal(rows, half, half))
    low = lanes_low(rows)
    slot = swap_bits(c ^ g)
    for u in range(2):
        first, second = (acc_ref[(2 * u + h) * rows : (2 * u + h + 1) * rows] * 0.125 for h in range(2))
        ret_ref[u, slot] = pack(first, pltpu.roll(second, 64, 1), low).astype(BF16)

    @pl.when(g == pl.num_programs(0) - 1)
    def _():
        own_out[...] = ret_ref[side]
        other_out[...] = ret_ref[1 - side]
        for e in range(4):
            for j in range(4):
                outs[e][j] = dkv_ref[4 * (c ^ swap_bits(j)) + (t ^ e)].astype(BF16)


def attend_back_call(place, gets, backs, o, lse):
    slots, rows, _ = gets[0].shape
    wide = 4 * rows
    return pl.pallas_call(
        attend_back_kernel,
        grid=(4,),
        in_specs=[pl.BlockSpec(memory_space=pltpu.SMEM)]
        + [whole(gets[0].shape)] * 8
        + [
            pl.BlockSpec((1, 64, wide), lambda j: (j, 0, 0)),
            pl.BlockSpec((1, 1, wide), lambda j: (j, 0, 0)),
        ],
        out_specs=[whole(gets[0].shape)] * 6,
        out_shape=[jax.ShapeDtypeStruct(gets[0].shape, BF16)] * 6,
        scratch_shapes=[
            pltpu.VMEM((4, 4, rows, 128), BF16),
            pltpu.VMEM((4 * slots, rows, 128), BF16),
            pltpu.VMEM((4, 4, rows, 128), BF16),
            pltpu.VMEM((4 * slots, rows, 128), F32),
            pltpu.VMEM((wide, 128), F32),
            pltpu.VMEM((2, slots, rows, 128), BF16),
        ],
        compiler_params=params(),
        cost_estimate=cost(36),
        name="attend_back",
    )(place, *gets, *backs, o, lse)


def qkv_back_kernel(place_ref, *refs):
    q_own, q_got, keys, (raw_ref, cos_ref, sin_ref, gain_ref, w_ref) = refs[0], refs[1], refs[2:6], refs[6:11]
    back_ref, own_ref, near_ref, share_ref, head_ref, pair_ref = refs[11:]
    side, j = place_ref[1] & 1, pl.program_id(0)
    rows = raw_ref.shape[1]
    head_ref[side] = q_own[0].astype(F32)
    head_ref[1 - side] = q_got[0].astype(F32)
    pair_ref[side] = keys[0][0].astype(F32) + keys[2][0].astype(F32)
    pair_ref[1 - side] = keys[1][0].astype(F32) + keys[3][0].astype(F32)
    low = lanes_low(rows)
    early = (lax.broadcasted_iota(jnp.int32, (rows, 128), 1) & 32) == 0
    cosine, sine = cos_ref[0, 0], sin_ref[0, 0]

    @pl.when(j == 0)
    def _():
        share_ref[...] = jnp.zeros_like(share_ref)

    even, odd = pair_ref[0], pair_ref[1]
    key = pack(even, pltpu.roll(odd, 64, 1), low)
    value = pack(pltpu.roll(even, 64, 1), odd, low)
    outs = []
    for b, given in enumerate((head_ref[0], head_ref[1], key)):
        z = sine * given
        cotangent = given * cosine + jnp.where(early, pltpu.roll(z, 96, 1), -pltpu.roll(z, 32, 1))
        u = raw_ref[0, :, b * 128 : (b + 1) * 128]
        gain = gain_ref[:, b * 128 : (b + 1) * 128]
        r = lax.rsqrt(head_sums(u * u) * (1.0 / 64.0) + EPS)
        mean = head_sums(u * gain * cotangent) * (1.0 / 64.0)
        share_ref[:, b * 128 : (b + 1) * 128] += jnp.sum(cotangent * u * r, axis=0, keepdims=True)
        outs.append((r * gain * cotangent - u * (r * r * r) * mean).astype(BF16))
    outs.append(value.astype(BF16))
    back = jnp.concatenate(outs, axis=1)
    back_ref[0] = back
    part = dot_nt(back, w_ref[:, :512]).astype(BF16)

    @pl.when(j < 2)
    def _():
        own_ref[0] = part

    @pl.when(j >= 2)
    def _():
        near_ref[0] = part


def qkv_back_call(place, at, gets, raw, cosine, sine, gains, w):
    slots, rows, _ = raw.shape
    width = w.shape[0]
    return pl.pallas_call(
        qkv_back_kernel,
        grid=(slots,),
        in_specs=[pl.BlockSpec(memory_space=pltpu.SMEM)]
        + [pl.BlockSpec((1, rows, 128), lambda j: (j, 0, 0))] * 6
        + [
            pl.BlockSpec((1, rows, 384), lambda j: (j, 0, 0)),
            pl.BlockSpec((1, 1, rows, 128), lambda j: (j, at, 0, 0)),
            pl.BlockSpec((1, 1, rows, 128), lambda j: (j, at, 0, 0)),
            whole((1, 384)),
            whole(w.shape),
        ],
        out_specs=[
            pl.BlockSpec((1, rows, 512), lambda j: (j, 0, 0)),
            pl.BlockSpec((1, rows, width), lambda j: (jnp.minimum(j, 1), 0, 0)),
            pl.BlockSpec((1, rows, width), lambda j: (jnp.maximum(j - 2, 0), 0, 0)),
            whole((1, 384)),
        ],
        out_shape=[
            jax.ShapeDtypeStruct((slots, rows, 512), BF16),
            jax.ShapeDtypeStruct((2, rows, width), BF16),
            jax.ShapeDtypeStruct((2, rows, width), BF16),
            jax.ShapeDtypeStruct((1, 384), F32),
        ],
        scratch_shapes=[pltpu.VMEM((2, rows, 128), F32), pltpu.VMEM((2, rows, 128), F32)],
        compiler_params=params(),
        cost_estimate=cost(7),
        name="qkv_back",
    )(place, *gets, raw, cosine, sine, gains, w)


def ffn_kernel(halves, *refs):
    offset_ref, x_refs, given_refs = refs[0], refs[1:5], refs[5:9]
    pieces = refs[9 : 9 + 3 * halves]
    refs = refs[9 + 3 * halves :]
    outs, (w_ref, x_ref, given_ref), held = refs[:7], refs[7:10], refs[10:17]
    sems, x_sems, given_sems, out_sems = refs[17:]
    _, rows, width = x_ref.shape
    count = 2 * rows
    blocks, depth, span = pieces[0].shape

    def copies(j):
        found = []
        for p in range(halves):
            start = pl.multiple_of(offset_ref[p], 128)
            for i in range(blocks):
                found.append(
                    pltpu.make_async_copy(
                        pieces[j * halves + p].at[i],
                        w_ref.at[j, pl.ds(i * depth, depth), pl.ds(start, span)],
                        sems.at[j, p, i],
                    )
                )
        return found

    def start(found):
        for copy in found:
            copy.start()

    def wait(found):
        for copy in found:
            copy.wait()

    tokens, givens = slot_copies(x_refs, x_ref, x_sems), slot_copies(given_refs, given_ref, given_sems)
    for found in (tokens[:2], copies(0), copies(1), copies(2), givens[:2], tokens[2:], givens[2:]):
        start(found)
    leaving = []

    def leave(at, k, value):
        ref, out = held[at], outs[at]
        if at < 3:
            ref[2 * k : 2 * k + 2] = value.reshape(2, rows, -1)
            source, target = ref.at[pl.ds(2 * k, 2)], out.at[pl.ds(2 * k, 2)]
        else:
            ref[...] = value.reshape(2, rows, -1)
            source, target = ref, out
        leaving.append(pltpu.make_async_copy(source, target, out_sems.at[at, k if at < 3 else 0]))
        leaving[-1].start()

    for k in range(2):
        wait(tokens[2 * k : 2 * k + 2])
        x = x_ref[2 * k : 2 * k + 2].reshape(count, width)
        if k == 0:
            wait(copies(0))
        gate = dot_nt(x, w_ref[0])
        if k == 0:
            wait(copies(1))
        up = dot_nt(x, w_ref[1])
        sig = jax.nn.sigmoid(gate)
        swish = gate * sig
        hidden = (swish * up).astype(BF16)
        leave(0, k, hidden)
        if k == 0:
            wait(copies(2))
        wait(givens[2 * k : 2 * k + 2])
        hidden_back = dot_nt(given_ref[2 * k : 2 * k + 2].reshape(count, width), w_ref[2])
        gate_back = (hidden_back * up * (sig * (1.0 + gate * (1.0 - sig)))).astype(BF16)
        leave(1, k, gate_back)
        up_back = (hidden_back * swish).astype(BF16)
        leave(2, k, up_back)
        leave(3 + k, k, dot_nn(hidden, w_ref[2]).astype(BF16))
        leave(5 + k, k, (dot_nn(gate_back, w_ref[0]) + dot_nn(up_back, w_ref[1])).astype(BF16))
    wait(leaving)


def ffn_call(offsets, xs, given, pieces):
    rows, width = xs[0].shape
    halves = len(pieces[0])
    blocks, depth, _ = pieces[0][0].shape
    hidden = blocks * depth
    shapes = [(4, rows, hidden)] * 3 + [(2, rows, width)] * 4
    return pl.pallas_call(
        functools.partial(ffn_kernel, halves),
        in_specs=[pl.BlockSpec(memory_space=pltpu.SMEM)] + [pl.BlockSpec(memory_space=pl.ANY)] * (8 + 3 * halves),
        out_specs=[pl.BlockSpec(memory_space=pl.ANY)] * 7,
        out_shape=[jax.ShapeDtypeStruct(shape, BF16) for shape in shapes],
        scratch_shapes=[
            pltpu.VMEM((3, hidden, width), BF16),
            pltpu.VMEM((4, rows, width), BF16),
            pltpu.VMEM((4, rows, width), BF16),
        ]
        + [pltpu.VMEM(shape, BF16) for shape in shapes]
        + [
            pltpu.SemaphoreType.DMA((3, halves, blocks)),
            pltpu.SemaphoreType.DMA((4,)),
            pltpu.SemaphoreType.DMA((4,)),
            pltpu.SemaphoreType.DMA((7, 2)),
        ],
        compiler_params=params(),
        cost_estimate=cost(22),
        name="ffn",
    )(offsets, *xs, *given, *[piece for row in pieces for piece in row])


def weight_kernel(halves, offset_ref, *refs):
    lefts, rights = refs[0:2], refs[2:10]
    outs, total_ref = refs[10 : 10 + halves], refs[10 + halves]
    blocks, depth, span = outs[0].shape
    total = 0.0
    for s, left in enumerate(lefts):
        a = left[...]
        b = jnp.concatenate([ref[...] for ref in rights[4 * s : 4 * s + 4]])
        total = total + dot_tn(a.reshape(-1, a.shape[-1]), b)
    total_ref[...] = total.astype(BF16)
    for p in range(halves):
        start = pl.multiple_of(offset_ref[p], 128)
        for i in range(blocks):
            outs[p][i] = total_ref[i * depth : (i + 1) * depth, pl.ds(start, span)]


def weight_call(offsets, lefts, rights, halves, blocks):
    units, width = lefts[0].shape[-1], rights[0][0].shape[-1]
    part = (blocks, units // blocks, width // halves)
    return pl.pallas_call(
        functools.partial(weight_kernel, halves),
        in_specs=[pl.BlockSpec(memory_space=pltpu.SMEM)] + [pl.BlockSpec(memory_space=pltpu.VMEM)] * 10,
        out_specs=[pl.BlockSpec(memory_space=pltpu.VMEM)] * halves,
        out_shape=[jax.ShapeDtypeStruct(part, BF16)] * halves,
        scratch_shapes=[pltpu.VMEM((units, width), BF16)],
        compiler_params=params(),
        cost_estimate=cost(10),
        name="weight",
    )(offsets, *lefts, *rights[0], *rights[1])


def small_weight_kernel(halves, near, place_ref, offset_ref, *refs):
    lefts, rights, outs, total_ref = refs[0:2], refs[2:10], refs[10 : 10 + halves], refs[10 + halves]
    t = place_ref[1]
    total = 0.0
    for s, left in enumerate(lefts):
        a = left[...]
        b = jnp.concatenate([ref[...] for ref in rights[4 * s : 4 * s + 4]])
        total = total + dot_tn(a.reshape(-1, a.shape[-1]), b)
    total_ref[...] = total.astype(BF16)
    blocks, _, span = outs[0].shape
    for p in range(halves):
        for e in range(blocks):
            if near:
                outs[p][e] = total_ref[:, pl.ds(pl.multiple_of(offset_ref[p] + (t ^ e) * span, 128), span)]
            else:
                outs[p][e] = total_ref[:, e * span : (e + 1) * span]


def small_weight_call(place, offsets, lefts, rights, halves, blocks, near):
    rows, width = lefts[0].shape[-1], rights[0][0].shape[-1]
    part = (blocks, rows, width // blocks // halves)
    return pl.pallas_call(
        functools.partial(small_weight_kernel, halves, near),
        in_specs=[pl.BlockSpec(memory_space=pltpu.SMEM)] * 2 + [pl.BlockSpec(memory_space=pltpu.VMEM)] * 10,
        out_specs=[pl.BlockSpec(memory_space=pltpu.VMEM)] * halves,
        out_shape=[jax.ShapeDtypeStruct(part, BF16)] * halves,
        scratch_shapes=[pltpu.VMEM((rows, width), BF16)],
        compiler_params=params(),
        cost_estimate=cost(5),
        name="small_weight",
    )(place, offsets, *lefts, *rights[0], *rights[1])


def inverse_root(values):
    return lax.rsqrt(jnp.mean(values * values, axis=-1, keepdims=True) + EPS)


def norm_back(values, root, gain, given):
    mean = jnp.mean(values * gain * given, axis=-1, keepdims=True)
    return root * gain * given - values * (root * root * root) * mean


def per_device(
    sizes,
    tokens,
    positions,
    first_gain,
    query_weight,
    key_weight,
    value_weight,
    query_gain,
    key_gain,
    output_weight,
    second_gain,
    gate_weight,
    up_weight,
    down_weight,
    upstream,
):
    shards, ctx, tp = sizes["shard"], sizes["ctx"], sizes["tp"]
    groups = ("shard", "tp")
    sequences, rows, width = tokens.shape
    head_dim = query_gain.shape[0]
    depth = query_weight.shape[0]
    units = gate_weight.shape[1]
    c, t = lax.axis_index("ctx"), lax.axis_index("tp")
    place = jnp.stack([c, t]).astype(jnp.int32)
    trade = [(i * tp + k, k * ctx + i) for i in range(ctx) for k in range(tp)]

    line = Line()
    small = jnp.concatenate([query_weight, key_weight, value_weight, output_weight.T], axis=1)
    small = lax.ppermute(small, ("ctx", "tp"), trade)
    blocks_attn = trade_tp(small, tp)
    w_attn = join_shard(blocks_attn.reshape(tp * depth, -1), shards)

    large = jnp.stack([gate_weight.T, up_weight.T, down_weight]).reshape(3, ctx, units // ctx, depth)
    large = lax.all_to_all(large, "ctx", 1, 1, tiled=True)
    large = after(large, small).transpose(0, 2, 1, 3).reshape(3, units // ctx, ctx * depth)
    halves = 2 if shards == 2 else 1
    shard = lax.axis_index("shard")
    starts = jnp.stack([shard, 1 - shard])[:halves] if halves == 2 else jnp.zeros((1,), jnp.int32)
    starts = (starts * (width // halves)).astype(jnp.int32)

    mine = lax.dynamic_slice_in_dim(positions, t * rows, rows, 1).astype(F32)
    places = jnp.stack(gather_ctx(mine))
    freqs = jnp.exp(-math.log(THETA) * jnp.arange(0, head_dim, 2).astype(F32) / head_dim)
    angles = places[..., None] * freqs
    cosine, sine = jnp.cos(angles), jnp.sin(angles)
    cosine = jnp.concatenate([cosine] * 4, axis=-1)
    sine = jnp.concatenate([sine] * 4, axis=-1)
    gains = jnp.concatenate([jnp.tile(query_gain, 4), jnp.tile(key_gain, 2)])[None]

    x = tokens.astype(F32)
    root = inverse_root(x)
    first = (x * root * first_gain).astype(BF16)
    given = upstream.astype(F32)

    pair = range(sequences)
    first_all = [gather_ctx(first[s]) for s in pair]
    heads, raw = [], []
    for s in pair:
        one = line.run(qkv_call, place, s, first_all[s], w_attn, cosine, sine, gains)
        heads.append(exchange_heads(one[0], one[1], (one[2], one[3], one[2], one[3])))
        raw.append(one[4])
    lines = [lax.all_gather(after(large[0], blocks_attn), "tp", axis=0, tiled=False)]
    for j in (1, 2):
        lines.append(lax.all_gather(after(large[j], *heads[1]), "tp", axis=0, tiled=False))
    w_ffn = [gather_shard(one, shards) for one in lines]
    upstream_all = [gather_ctx(after(upstream[s], raw[0])) for s in pair]
    heads[0] = after(heads[0], lines[0])
    heads[1] = after(heads[1], w_ffn[0][-1])

    attended, sent = [], []
    for s in pair:
        attended.append(line.run(attend_call, place, heads[s]))
        sent.append([attended[s][0], to_tp(attended[s][1], 1)])

    def middle_of(share, rows_in):
        middle = rows_in + share
        middle_root = inverse_root(middle)
        return (middle * middle_root * second_gain).astype(BF16), middle, middle_root

    mixed, shares_near, shares_far, middles, seconds = [], [], [], [], []
    for s in pair:
        one = line.run(out_call, place, sent[s], w_attn)
        mixed.append(one[0])
        shares_near.append(reduce_near(one[1], one[2]))
    shares_near[0] = after(shares_near[0], lines[1])
    shares_near[1] = after(shares_near[1], lines[2], w_ffn[1][-1])
    for s in pair:
        second, middle, middle_root = line.run(lambda a, b, rows_in: middle_of(reduce_far(a, b), rows_in), *shares_near[s], x[s])
        middles.append((middle, middle_root))
        seconds.append(gather_ctx(second))
    ffn = [line.run(ffn_call, starts, seconds[s], upstream_all[s], w_ffn) for s in pair]

    results, back_rows, mixed_back_all = [], [], []
    sums, backs_sent, got, g_ffn = [], [], [], []

    def turn_back(second_back, s):
        middle, middle_root = middles[s]
        middle_back = given[s] + norm_back(middle, middle_root, second_gain, second_back)
        return middle_back.astype(BF16), middle_back, jnp.sum(second_back * middle * middle_root, axis=0)

    def turn(s, call, *shares):
        low, middle_back, share = line.run(lambda first, *rest: turn_back(call(first, *rest), s), *shares)
        back_rows.append(middle_back)
        mixed_back_all.append(gather_ctx(low))
        return share

    def weight(j):
        at, rights = ((1, seconds), (2, seconds), (0, upstream_all))[j]
        parts = line.run(weight_call, starts, [one[at] for one in ffn], rights, halves, tp)
        sums.append((parts, send_shard(parts, shards)))

    def back_out(s):
        own, other = line.run(out_back_call, place, mixed_back_all[s], w_attn)
        backs_sent.append([own, to_tp(other, 1)])

    def back_attend(s):
        one = line.run(attend_back_call, place, heads[s], backs_sent[s], attended[s][2], attended[s][3])
        got.append(exchange_heads(one[0], one[1], one[2:]))

    def add(j):
        parts, moved = sums[j]
        g_ffn.append(lax.psum_scatter(line.run(add_shard, moved, parts), "tp", scatter_dimension=0, tiled=False))

    shares = ffn[0][5][0], *(
        lax.ppermute(value, "ctx", way) for value, way in ((ffn[0][5][1], FAR), (ffn[0][6][0], NEAR), (ffn[0][6][1], CROSS))
    )
    second_share = turn(0, lambda *parts: sum(part.astype(F32) for part in parts), *shares)
    mine, away = line.run(lambda near, own: add_near(own, near), lax.ppermute(ffn[1][6], "ctx", NEAR), ffn[1][5])
    away = lax.ppermute(away, "ctx", FAR)
    weight(0)
    weight(1)
    back_out(0)
    second_share = second_share + turn(1, lambda far, own: own + far.astype(F32), away, mine)
    weight(2)
    aligned = depth % 128 == 0
    count = shards * tp
    g_out = line.run(small_weight_call, place, starts, mixed, mixed_back_all, 1, count if aligned else 1, False)[0]
    if not aligned:
        g_out = g_out[0].reshape(-1, count, width // count).transpose(1, 0, 2)
    add(0)
    back_out(1)
    g_out = lax.psum_scatter(g_out, groups, scatter_dimension=0, tiled=False)
    back_attend(0)
    add(1)
    add(2)
    back_attend(1)

    for s in pair:
        results.append((middles[s][0] + reduce_far(*reduce_near(ffn[s][3], after(ffn[s][4], got[0][0])))).astype(BF16))

    gradients, shares, head_share, backs, firsts = [], [], 0.0, [], []
    for s in pair:
        back, own, other, share = line.run(qkv_back_call, place, s, got[s], raw[s], cosine, sine, gains, w_attn)
        backs.append(back)
        head_share = head_share + share
        firsts.append(reduce_near(own, other))
    near = aligned and halves == 2
    parts = line.run(small_weight_call, place, starts, backs, first_all, 2 if near else 1, tp if near else 1, near)
    moved = lax.ppermute(parts[1], "shard", [(0, 1), (1, 0)]) if near else None

    def last(mine, away, s):
        first_back = reduce_far(mine, away)
        gradient = back_rows[s] + norm_back(x[s], root[s], first_gain, first_back)
        return jnp.sum(first_back * x[s] * root[s], axis=0), gradient

    for s in pair:
        share, gradient = line.run(lambda a, b: last(a, b, s), *firsts[s])
        shares.append(share)
        gradients.append(gradient)
    shares = jnp.concatenate([shares[0] + shares[1], second_share, head_share[0]])
    shares = sum_all(shares, [(name, sizes[name]) for name in ("ctx", "shard", "tp")])
    if moved is None:
        g_qkv = jnp.concatenate([part[0] for part in parts], axis=1)
        g_qkv = g_qkv.reshape(-1, count, width // count).transpose(1, 0, 2)
        g_qkv = lax.psum_scatter(g_qkv, groups, scatter_dimension=0, tiled=False)
    else:
        g_qkv = line.run(lambda a, b: (a.astype(F32) + b.astype(F32)).astype(BF16), moved, parts[0])
        g_qkv = sum(part.astype(F32) for part in exchange_tp([g_qkv[e] for e in range(tp)])).astype(BF16)

    g_ffn = jnp.stack(g_ffn)
    g_ffn = g_ffn.reshape(3, units // ctx, ctx, depth).transpose(0, 2, 1, 3)
    g_ffn = lax.all_to_all(g_ffn, "ctx", 1, 1, tiled=True)
    g_ffn = g_ffn.reshape(3, units, depth).astype(F32)
    g_out = lax.ppermute(g_out, ("ctx", "tp"), trade).astype(F32)
    g_attn = lax.ppermute(g_qkv, ("ctx", "tp"), trade).astype(F32)
    heads_end = query_weight.shape[1]
    pairs = key_weight.shape[1]

    head_total = shares[2 * width :]
    return (
        jnp.stack(results),
        jnp.stack(gradients),
        g_attn[:heads_end].T,
        g_attn[heads_end : heads_end + pairs].T,
        g_attn[heads_end + pairs : heads_end + 2 * pairs].T,
        g_out,
        g_ffn[0].T,
        g_ffn[1].T,
        g_ffn[2],
        shares[:width],
        shares[width : 2 * width],
        jnp.sum(head_total[: 4 * head_dim].reshape(4, head_dim), axis=0),
        jnp.sum(head_total[4 * head_dim :].reshape(2, head_dim), axis=0),
    )


def solution(mesh):
    rows = P("shard", ("ctx", "tp"), None)
    wide = P(("shard", "ctx"), "tp")
    tall = P("tp", ("shard", "ctx"))
    none = P()
    in_specs = (
        rows, P("shard", "ctx"), none, wide, wide, wide, none, none, tall, none, wide, wide, tall, rows,
    )
    out_specs = (rows, rows, wide, wide, wide, tall, wide, wide, tall, none, none, none, none)
    sizes = {name: mesh.shape[name] for name in ("shard", "ctx", "tp")}
    return jax.shard_map(
        functools.partial(per_device, sizes), mesh=mesh, in_specs=in_specs, out_specs=out_specs, check_vma=False
    )
```

time: 972 us -> 685 us (0.70)
  the two profiles are of different devices: /device:TPU:6 before, /device:TPU:0 now
where the time goes in v2:
time: 685 us; the launch traced here: 675 us
  Pallas kernels  230 us (34%)
  waiting for transfers between devices  213 us (31%)
  starting transfers between devices  134 us (20%)
  other arithmetic  55 us (8%)
  local copies, waits for them, and re-layouts  27.2 us (4%)
  between operations  15.5 us (2%)
    ppermute x23, waiting for transfers between devices, to_tp(): return lax.ppermute(value, 'tp', [(i, i ^ e) for i in range(4)])  73.2 us
    ppermute x23, starting transfers between devices, to_tp(): return lax.ppermute(value, 'tp', [(i, i ^ e) for i in range(4)])  64 us
    pallas_call x2, Pallas kernels, attend_back_call(): pl.pallas_call(attend_back_kernel, grid=(4,), in_specs=[pl.BlockSpec(memo...  58.7 us
    pallas_call x2, Pallas kernels, ffn_call(): pl.pallas_call(functools.partial(ffn_kernel, halves), in_specs=[pl.BlockS...  50.1 us
    ppermute x9, waiting for transfers between devices, gather_ctx(): far = lax.ppermute(own, 'ctx', FAR)  42.3 us
    ppermute x6, waiting for transfers between devices, reduce_far(): return mine + lax.ppermute(away, 'ctx', FAR).astype(F32)  36.1 us
    pallas_call x3, Pallas kernels, weight_call(): pl.pallas_call(functools.partial(weight_kernel, halves), in_specs=[pl.Blo...  31.1 us
    pallas_call x2, Pallas kernels, attend_call(): pl.pallas_call(attend_kernel, grid=(4,), in_specs=[pl.BlockSpec(memory_sp...  28.4 us
  transfers between devices with their start and end apart: 95, of which 28 were waited for; matrix products, arithmetic and copies ran while one was open for 10% of the time, Pallas kernels for 34%

profile of v2, /device:TPU:0, one launch (start us, length us, event | category | flops | bytes accessed | tf_op | source)
XLA Modules:
  0.0 674.9 jit_solution(542617709356151856)
XLA Ops:
  39.0 10.4 %collective-permute-done.5 = bf16[128,768]{0,1:T(8,128)(2,1)S(1)} collective-permute-done((bf16[128,768]{0,1:T(8,128)(2,1)S(1)}, bf16[128,768]{0,1:T(8,128)(2,1)S(1)}, u32[]{:S(2)}, u32[]{:S(2)}) %collective-permute-start.5) | collective-permute-done | bytes 196640 | tf_op jit(solution)/shard_map/ppermute | solution.py:109
  95.9 9.6 %collective-permute-done.18.refs_1_ = bf16[4,256,128]{2,1,0:T(8,128)(2,1)S(1)} collective-permute-done((bf16[4,256,128]{2,1,0:T(8,128)(2,1)}, bf16[4,256,128]{2,1,0:T(8,128)(2,1)S(1)}, u32[]{:S(2)}, u32[]{:S(2)}) %collective-permute-start.18) | collective-permute-done | bytes 262176 | tf_op jit(solution)/shard_map/ppermute | solution.py:62
  133.7 13.3 %collective-permute-done.17.refs_5_ = bf16[4,256,128]{2,1,0:T(8,128)(2,1)} collective-permute-done((bf16[4,256,128]{2,1,0:T(8,128)(2,1)}, bf16[4,256,128]{2,1,0:T(8,128)(2,1)}, u32[]{:S(2)}, u32[]{:S(2)}) %collective-permute-start.17) | collective-permute-done | bytes 262176 | tf_op jit(solution)/shard_map/ppermute | solution.py:62
  147.0 14.0 %attend.2 = (bf16[4,256,128]{2,1,0:T(8,128)(2,1)}, bf16[4,256,128]{2,1,0:T(8,128)(2,1)}, f32[4,64,1024]{2,1,0:T(8,128)}, f32[4,1,1024]{2,1,0:T(1,128)}) custom-call(s32[2]{0:T(128)} %pad_add_fusion.place_ref, bf16[4,256,128]{2,1,0:T(8,128)(2,1)} %get-tuple-element.145.refs_0_, bf16[4,256,128]{2,1,0:T(8,128)(2,1)} %collective-permute-done.14.refs_1_, ...), custom_call_target="tpu_custom_call" | custom-call | flops 16999999488 | bytes 17000000 | tf_op jit(solution)/shard_map/attend/pallas_call | solution.py:329
  161.1 14.4 %attend.3 = (bf16[4,256,128]{2,1,0:T(8,128)(2,1)}, bf16[4,256,128]{2,1,0:T(8,128)(2,1)}, f32[4,64,1024]{2,1,0:T(8,128)}, f32[4,1,1024]{2,1,0:T(1,128)}) custom-call(s32[2]{0:T(128)} %pad_add_fusion.place_ref, bf16[4,256,128]{2,1,0:T(8,128)(2,1)} %get-tuple-element.156.refs_0_, bf16[4,256,128]{2,1,0:T(8,128)(2,1)} %copy-done.39, ...), custom_call_target="tpu_custom_call" | custom-call | flops 16999999488 | bytes 17000000 | tf_op jit(solution)/shard_map/attend/pallas_call | solution.py:329
  198.3 10.0 %collective-permute-done.33.refs_6_.refs_3_ = bf16[256,1024]{1,0:T(8,128)(2,1)} collective-permute-done((bf16[256,1024]{1,0:T(8,128)(2,1)}, bf16[256,1024]{1,0:T(8,128)(2,1)}, u32[]{:S(2)}, u32[]{:S(2)}) %collective-permute-start.33) | collective-permute-done | bytes 524320 | tf_op jit(solution)/shard_map/ppermute | solution.py:39
  213.1 10.0 %all-gather.11.cloned.1.call-done = bf16[1152,512]{1,0:T(8,128)(2,1)} async-done(((bf16[288,512]{1,0:T(8,128)(2,1)}), bf16[1152,512]{1,0:T(8,128)(2,1)}) %all-gather.11.cloned.1.call-update) | async-done | bytes 1179664 | tf_op jit(solution)/shard_map/all_gather | solution.py:834
  228.6 12.3 %collective-permute-done.29 = bf16[256,1024]{1,0:T(8,128)(2,1)S(1)} collective-permute-done((bf16[256,1024]{1,0:T(8,128)(2,1)}, bf16[256,1024]{1,0:T(8,128)(2,1)S(1)}, u32[]{:S(2)}, u32[]{:S(2)}) %collective-permute-start.29) | collective-permute-done | bytes 524320 | tf_op jit(solution)/shard_map/ppermute | solution.py:53
  244.6 11.5 %collective-permute-done.30.refs_2_.refs_3_ = bf16[256,1024]{1,0:T(8,128)(2,1)} collective-permute-done((bf16[256,1024]{1,0:T(8,128)(2,1)}, bf16[256,1024]{1,0:T(8,128)(2,1)}, u32[]{:S(2)}, u32[]{:S(2)}) %collective-permute-start.30) | collective-permute-done | bytes 524320 | tf_op jit(solution)/shard_map/ppermute | solution.py:39
  266.5 25.1 %ffn.2 = (bf16[4,256,1152]{2,1,0:T(8,128)(2,1)}, bf16[4,256,1152]{2,1,0:T(8,128)(2,1)}, bf16[4,256,1152]{2,1,0:T(8,128)(2,1)}, bf16[2,256,1024]{2,1,0:T(8,128)(2...) custom-call(s32[2]{0:T(128)} %add_multiply_fusion.refs_0_.offset_ref, ...), custom_call_target="tpu_custom_call" | custom-call | flops 22000001024 | bytes 22000000 | tf_op jit(solution)/shard_map/ffn/pallas_call | solution.py:674
  296.6 24.9 %ffn.3 = (bf16[4,256,1152]{2,1,0:T(8,128)(2,1)}, bf16[4,256,1152]{2,1,0:T(8,128)(2,1)}, bf16[4,256,1152]{2,1,0:T(8,128)(2,1)}, bf16[2,256,1024]{2,1,0:T(8,128)(2...) custom-call(s32[2]{0:T(128)} %add_multiply_fusion.refs_0_.offset_ref, ...), custom_call_target="tpu_custom_call" | custom-call | flops 22000001024 | bytes 22000000 | tf_op jit(solution)/shard_map/ffn/pallas_call | solution.py:674
  325.5 10.6 %weight.3 = (bf16[4,288,512]{2,1,0:T(8,128)(2,1)}, bf16[4,288,512]{2,1,0:T(8,128)(2,1)}) custom-call(s32[2]{0:T(128)} %add_multiply_fusion.refs_0_.offset_ref, bf16[4,256,1152]{2,1,0:T(8,128)(2,1)} %get-tuple-element.197.refs_0_, bf16[4,256,1152]{2,1,0:T(8,128)(2,1)} %get-tuple-element.198.refs_1_, bf16[256,1024]{1,0:T(8,128)(2,1)} %multiply_convert_fusion.2.refs_1_.refs_2_, ...), custom_call_target="tpu_custom_call" | custom-call | flops 10000000000 | bytes 10000000 | tf_op jit(solution)/shard_map/weight/pallas_call | solution.py:716
  340.0 10.1 %weight.4 = (bf16[4,288,512]{2,1,0:T(8,128)(2,1)}, bf16[4,288,512]{2,1,0:T(8,128)(2,1)}) custom-call(s32[2]{0:T(128)} %add_multiply_fusion.refs_0_.offset_ref, bf16[4,256,1152]{2,1,0:T(8,128)(2,1)} %get-tuple-element.202.refs_0_, bf16[4,256,1152]{2,1,0:T(8,128)(2,1)} %get-tuple-element.203.refs_1_, bf16[256,1024]{1,0:T(8,128)(2,1)} %multiply_convert_fusion.2.refs_1_.refs_2_, ...), custom_call_target="tpu_custom_call" | custom-call | flops 10000000000 | bytes 10000000 | tf_op jit(solution)/shard_map/weight/pallas_call | solution.py:716
  361.5 9.6 %collective-permute-done.52.refs_7_.refs_1_ = bf16[256,1024]{1,0:T(8,128)(2,1)S(1)} collective-permute-done((bf16[256,1024]{1,0:T(8,128)(2,1)}, bf16[256,1024]{1,0:T(8,128)(2,1)S(1)}, u32[]{:S(2)}, u32[]{:S(2)}) %collective-permute-start.52) | collective-permute-done | bytes 524320 | tf_op jit(solution)/shard_map/ppermute | solution.py:39
  371.2 10.3 %weight.5 = (bf16[4,288,512]{2,1,0:T(8,128)(2,1)}, bf16[4,288,512]{2,1,0:T(8,128)(2,1)}) custom-call(s32[2]{0:T(128)} %add_multiply_fusion.refs_0_.offset_ref, bf16[4,256,1152]{2,1,0:T(8,128)(2,1)} %get-tuple-element.186.refs_0_, bf16[4,256,1152]{2,1,0:T(8,128)(2,1)} %get-tuple-element.192.refs_1_, bf16[256,1024]{1,0:T(8,128)(2,1)} %get-tuple-element.183.refs_5_.refs_2_, ...), custom_call_target="tpu_custom_call" | custom-call | flops 10000000000 | bytes 10000000 | tf_op jit(solution)/shard_map/weight/pallas_call | solution.py:716
  395.8 29.4 %attend_back.2 = (bf16[4,256,128]{2,1,0:T(8,128)(2,1)}, bf16[4,256,128]{2,1,0:T(8,128)(2,1)}, bf16[4,256,128]{2,1,0:T(8,128)(2,1)}, bf16[4,256,128]{2,1,0:T(8,12...) custom-call(s32[2]{0:T(128)} %pad_add_fusion.place_ref, ...), custom_call_target="tpu_custom_call" | custom-call | flops 35999997952 | bytes 36000000 | tf_op jit(solution)/shard_map/attend_back/pallas_call | solution.py:491
  434.1 13.5 %collective-permute-start.65 = (bf16[4,256,128]{2,1,0:T(8,128)(2,1)}, bf16[4,256,128]{2,1,0:T(8,128)(2,1)}, u32[]{:S(2)}, u32[]{:S(2)}) collective-permute-start(bf16[4,256,128]{2,1,0:T(8,128)(2,1)} %get-tuple-element.236), channel_id=1, source_target_pairs={{0,2},{1,3},{2,0},{3,1},{4,6},{5,7},{6,4},{7,5},{8,10},{9,11},{10,... | collective-permute-start | bytes 786440 | tf_op jit(solution)/shard_map/ppermute | solution.py:62
  447.7 10.3 %collective-permute-done.60 = bf16[4,288,512]{2,1,0:T(8,128)(2,1)S(1)} collective-permute-done((bf16[4,288,512]{2,1,0:T(8,128)(2,1)}, bf16[4,288,512]{2,1,0:T(8,128)(2,1)S(1)}, u32[]{:S(2)}, u32[]{:S(2)}) %collective-permute-start.60) | collective-permute-done | bytes 1179680 | tf_op jit(solution)/shard_map/ppermute | solution.py:82
  458.0 15.5 %collective-permute-start.66 = (bf16[4,256,128]{2,1,0:T(8,128)(2,1)S(1)}, bf16[4,256,128]{2,1,0:T(8,128)(2,1)}, u32[]{:S(2)}, u32[]{:S(2)}) collective-permute-start(bf16[4,256,128]{2,1,0:T(8,128)(2,1)S(1)} %copy-done.43), channel_id=1, source_target_pairs={{0,3},{1,2},{2,1},{3,0},{4,7},{5,6},{6,5},{7,4},{8,11},{9,10},{10,... | collective-permute-start | bytes 786440 | tf_op jit(solution)/shard_map/ppermute | solution.py:62
  476.3 29.4 %attend_back.3 = (bf16[4,256,128]{2,1,0:T(8,128)(2,1)}, bf16[4,256,128]{2,1,0:T(8,128)(2,1)}, bf16[4,256,128]{2,1,0:T(8,128)(2,1)}, bf16[4,256,128]{2,1,0:T(8,12...) custom-call(s32[2]{0:T(128)} %pad_add_fusion.place_ref, ...), custom_call_target="tpu_custom_call" | custom-call | flops 35999997952 | bytes 36000000 | tf_op jit(solution)/shard_map/attend_back/pallas_call | solution.py:491
  527.4 15.4 %collective-permute-done.69.refs_3_ = bf16[4,256,128]{2,1,0:T(8,128)(2,1)S(1)} collective-permute-done((bf16[4,256,128]{2,1,0:T(8,128)(2,1)}, bf16[4,256,128]{2,1,0:T(8,128)(2,1)S(1)}, u32[]{:S(2)}, u32[]{:S(2)}) %collective-permute-start.69) | collective-permute-done | bytes 262176 | tf_op jit(solution)/shard_map/ppermute | solution.py:62
  542.7 12.1 %collective-permute-done.71.refs_5_ = bf16[4,256,128]{2,1,0:T(8,128)(2,1)S(1)} collective-permute-done((bf16[4,256,128]{2,1,0:T(8,128)(2,1)}, bf16[4,256,128]{2,1,0:T(8,128)(2,1)S(1)}, u32[]{:S(2)}, u32[]{:S(2)}) %collective-permute-start.71) | collective-permute-done | bytes 262176 | tf_op jit(solution)/shard_map/ppermute | solution.py:62
  611.1 9.5 %collective-permute-done.74 = bf16[256,1024]{1,0:T(8,128)(2,1)S(1)} collective-permute-done((bf16[256,1024]{1,0:T(8,128)(2,1)S(1)}, bf16[256,1024]{1,0:T(8,128)(2,1)S(1)}, u32[]{:S(2)}, u32[]{:S(2)}) %collective-permute-start.74) | collective-permute-done | bytes 524320 | tf_op jit(solution)/shard_map/ppermute | solution.py:53
  654.4 10.3 %all-to-all-done.1 = bf16[3,4,288,128]{3,2,0,1:T(8,128)(2,1)S(1)} async-done(((bf16[3,4,288,128]{3,2,0,1:T(8,128)(2,1)}), bf16[3,4,288,128]{3,2,0,1:T(8,128)(2,1)S(1)}, u32[]{:S(2)}, u32[]{:S(2)}) %all-to-all-start.1) | async-done | bytes 884768 | tf_op jit(solution)/shard_map/all_to_all | solution.py:952
  (404 shorter events, 317.7 us)
Async XLA Ops:
  10.8 41.3 %collective-permute-start.9 = (f32[2,256]{1,0:T(2,128)S(1)}, f32[2,256]{1,0:T(2,128)S(1)}, u32[]{:S(2)}, u32[]{:S(2)}) collective-permute-start(f32[2,256]{1,0:T(2,128)S(1)} %dynamic-slice_convert_fusion), channel_id=1, source_target_pairs={{0,4},{4,0},{8,12},{12,8},{1,5},{5,1},{9,13},{13,9},{2,6},{6,2},{1... | collective-permute-start | bytes 6152 | tf_op jit(solution)/shard_map/ppermute | solution.py:40
  19.5 44.3 %all-to-all-start = ((bf16[3,4,288,128]{3,2,0,1:T(8,128)(2,1)}), bf16[3,4,288,128]{3,2,0,1:T(8,128)(2,1)S(1)}, u32[]{:S(2)}, u32[]{:S(2)}) async-start(bf16[3,4,288,128]{3,2,0,1:T(8,128)(2,1)} %copy.92), calls=%async_computation | async-start | bytes 1769472 | tf_op jit(solution)/shard_map/all_to_all | solution.py:804
  26.8 93.4 %all-gather.7.cloned.1.call-start = ((), (), s32[]{:S(2)}) async-start(), calls=%async_computation.10 | async-start | bytes 1474560 | tf_op jit(solution)/shard_map/all_gather | solution.py:832
  64.8 125.8 %all-gather.9.cloned.1.call-start = ((), (), s32[]{:S(2)}) async-start(), calls=%async_computation.11 | async-start | bytes 1474560 | tf_op jit(solution)/shard_map/all_gather | solution.py:834
  119.9 103.2 %all-gather.11.cloned.1.call-start = ((), (), s32[]{:S(2)}) async-start(), calls=%async_computation.12 | async-start | bytes 1474560 | tf_op jit(solution)/shard_map/all_gather | solution.py:834
  120.6 40.4 %collective-permute-start.22 = (bf16[4,288,512]{2,1,0:T(8,128)(2,1)}, bf16[4,288,512]{2,1,0:T(8,128)(2,1)S(1)}, u32[]{:S(2)}, u32[]{:S(2)}) collective-permute-start(bf16[4,288,512]{2,1,0:T(8,128)(2,1)} %bitcast.208), channel_id=1, source_target_pairs={{0,16},{16,0},{1,17},{17,1},{2,18},{18,2},{3,19},{19,3},{4,20},{20... | collective-permute-start | bytes 3538952 | tf_op jit(solution)/shard_map/ppermute | solution.py:75
  184.3 389.6 %reduce-scatter.5.cloned.1.call-start = ((), (), s32[]{:S(2)}) async-start(), calls=%async_computation.6 | async-start | bytes 589824 | tf_op jit(solution)/shard_map/reduce_scatter | solution.py:912
  198.2 45.9 %collective-permute-start.34 = (bf16[256,1024]{1,0:T(8,128)(2,1)}, bf16[256,1024]{1,0:T(8,128)(2,1)}, u32[]{:S(2)}, u32[]{:S(2)}) collective-permute-start(bf16[256,1024]{1,0:T(8,128)(2,1)} %get-tuple-element.183.refs_5_.refs_2_), channel_id=1, source_target_pairs={{0,4},{4,0},{8,12},{12,8},{1,5},{5,1},{9,13},{13,9},{2,6},{6,2},{1... | collective-permute-start | bytes 1572872 | tf_op jit(solution)/shard_map/ppermute | solution.py:40
  210.3 47.9 %collective-permute-start.35 = (bf16[256,1024]{1,0:T(8,128)(2,1)}, bf16[256,1024]{1,0:T(8,128)(2,1)}, u32[]{:S(2)}, u32[]{:S(2)}) collective-permute-start(bf16[256,1024]{1,0:T(8,128)(2,1)} %collective-permute-done.33.refs_6_.refs_3_), channel_id=1, source_target_pairs={{0,4},{4,0},{8,12},{12,8},{1,5},{5,1},{9,13},{13,9},{2,6},{6,2},{1... | collective-permute-start | bytes 1572872 | tf_op jit(solution)/shard_map/ppermute | solution.py:41
  258.8 37.8 %collective-permute-start.38 = (bf16[256,1024]{1,0:T(8,128)(2,1)S(1)}, bf16[256,1024]{1,0:T(8,128)(2,1)}, u32[]{:S(2)}, u32[]{:S(2)}) collective-permute-start(bf16[256,1024]{1,0:T(8,128)(2,1)S(1)} %multiply_convert_fusion.1.refs_1_.refs_6_), channel_id=1, source_target_pairs={{0,4},{4,0},{8,12},{12,8},{1,5},{5,1},{9,13},{13,9},{2,6},{6,2},{1... | collective-permute-start | bytes 1572872 | tf_op jit(solution)/shard_map/ppermute | solution.py:40
  358.9 66.3 %collective-permute-start.61 = (bf16[4,288,512]{2,1,0:T(8,128)(2,1)}, bf16[4,288,512]{2,1,0:T(8,128)(2,1)}, u32[]{:S(2)}, u32[]{:S(2)}) collective-permute-start(bf16[4,288,512]{2,1,0:T(8,128)(2,1)} %get-tuple-element.224), channel_id=1, source_target_pairs={{0,16},{16,0},{1,17},{17,1},{2,18},{18,2},{3,19},{19,3},{4,20},{20... | collective-permute-start | bytes 3538952 | tf_op jit(solution)/shard_map/ppermute | solution.py:82
  387.7 256.4 %reduce-scatter.9.cloned.1.call-start = ((), (), s32[]{:S(2)}) async-start(), calls=%async_computation.8 | async-start | bytes 1474560 | tf_op jit(solution)/shard_map/reduce_scatter | solution.py:892
  427.9 216.2 %reduce-scatter.7.cloned.1.call-start = ((), (), s32[]{:S(2)}) async-start(), calls=%async_computation.7 | async-start | bytes 1474560 | tf_op jit(solution)/shard_map/reduce_scatter | solution.py:892
  428.5 215.6 %reduce-scatter.11.cloned.1.call-start = ((), (), s32[]{:S(2)}) async-start(), calls=%async_computation.9 | async-start | bytes 1474560 | tf_op jit(solution)/shard_map/reduce_scatter | solution.py:892
  430.0 46.2 %collective-permute-start.62 = (bf16[4,256,128]{2,1,0:T(8,128)(2,1)}, bf16[4,256,128]{2,1,0:T(8,128)(2,1)}, u32[]{:S(2)}, u32[]{:S(2)}) collective-permute-start(bf16[4,256,128]{2,1,0:T(8,128)(2,1)} %get-tuple-element.228), channel_id=1, source_target_pairs={{0,1},{1,0},{2,3},{3,2},{4,5},{5,4},{6,7},{7,6},{8,9},{9,8},{10,11... | collective-permute-start | bytes 786440 | tf_op jit(solution)/shard_map/ppermute | solution.py:62
  432.1 73.5 %collective-permute-start.63 = (bf16[4,256,128]{2,1,0:T(8,128)(2,1)}, bf16[4,256,128]{2,1,0:T(8,128)(2,1)}, u32[]{:S(2)}, u32[]{:S(2)}) collective-permute-start(bf16[4,256,128]{2,1,0:T(8,128)(2,1)} %get-tuple-element.233), channel_id=1, source_target_pairs={{0,1},{1,0},{2,3},{3,2},{4,5},{5,4},{6,7},{7,6},{8,9},{9,8},{10,11... | collective-permute-start | bytes 786440 | tf_op jit(solution)/shard_map/ppermute | solution.py:62
  432.2 74.3 %collective-permute-start.64 = (bf16[4,256,128]{2,1,0:T(8,128)(2,1)}, bf16[4,256,128]{2,1,0:T(8,128)(2,1)}, u32[]{:S(2)}, u32[]{:S(2)}) collective-permute-start(bf16[4,256,128]{2,1,0:T(8,128)(2,1)} %get-tuple-element.235), channel_id=1, source_target_pairs={{0,1},{1,0},{2,3},{3,2},{4,5},{5,4},{6,7},{7,6},{8,9},{9,8},{10,11... | collective-permute-start | bytes 786440 | tf_op jit(solution)/shard_map/ppermute | solution.py:62
  434.1 73.6 %collective-permute-start.65 = (bf16[4,256,128]{2,1,0:T(8,128)(2,1)}, bf16[4,256,128]{2,1,0:T(8,128)(2,1)}, u32[]{:S(2)}, u32[]{:S(2)}) collective-permute-start(bf16[4,256,128]{2,1,0:T(8,128)(2,1)} %get-tuple-element.236), channel_id=1, source_target_pairs={{0,2},{1,3},{2,0},{3,1},{4,6},{5,7},{6,4},{7,5},{8,10},{9,11},{10,... | collective-permute-start | bytes 786440 | tf_op jit(solution)/shard_map/ppermute | solution.py:62
  458.0 56.3 %collective-permute-start.66 = (bf16[4,256,128]{2,1,0:T(8,128)(2,1)S(1)}, bf16[4,256,128]{2,1,0:T(8,128)(2,1)}, u32[]{:S(2)}, u32[]{:S(2)}) collective-permute-start(bf16[4,256,128]{2,1,0:T(8,128)(2,1)S(1)} %copy-done.43), channel_id=1, source_target_pairs={{0,3},{1,2},{2,1},{3,0},{4,7},{5,6},{6,5},{7,4},{8,11},{9,10},{10,... | collective-permute-start | bytes 786440 | tf_op jit(solution)/shard_map/ppermute | solution.py:62
  476.2 94.9 %collective-permute-start.56 = (bf16[2,256,1024]{2,1,0:T(8,128)(2,1)}, bf16[2,256,1024]{2,1,0:T(8,128)(2,1)S(1)}, u32[]{:S(2)}, u32[]{:S(2)}) collective-permute-start(bf16[2,256,1024]{2,1,0:T(8,128)(2,1)} %get-tuple-element.219), channel_id=1, source_target_pairs={{0,4},{4,0},{8,12},{12,8},{1,5},{5,1},{9,13},{13,9},{2,6},{6,2},{1... | collective-permute-start | bytes 3145736 | tf_op jit(solution)/shard_map/ppermute | solution.py:49
  514.3 40.5 %collective-permute-start.71 = (bf16[4,256,128]{2,1,0:T(8,128)(2,1)}, bf16[4,256,128]{2,1,0:T(8,128)(2,1)S(1)}, u32[]{:S(2)}, u32[]{:S(2)}) collective-permute-start(bf16[4,256,128]{2,1,0:T(8,128)(2,1)} %get-tuple-element.246), channel_id=1, source_target_pairs={{0,3},{1,2},{2,1},{3,0},{4,7},{5,6},{6,5},{7,4},{8,11},{9,10},{10,... | collective-permute-start | bytes 786440 | tf_op jit(solution)/shard_map/ppermute | solution.py:62
  527.3 46.6 %collective-permute-start.58 = (bf16[2,256,1024]{2,1,0:T(8,128)(2,1)S(1)}, bf16[2,256,1024]{2,1,0:T(8,128)(2,1)}, u32[]{:S(2)}, u32[]{:S(2)}) collective-permute-start(bf16[2,256,1024]{2,1,0:T(8,128)(2,1)S(1)} %copy-done.32), channel_id=1, source_target_pairs={{0,4},{4,0},{8,12},{12,8},{1,5},{5,1},{9,13},{13,9},{2,6},{6,2},{1... | collective-permute-start | bytes 3145736 | tf_op jit(solution)/shard_map/ppermute | solution.py:49
  542.7 44.5 %collective-permute-start.67 = (bf16[2,256,1024]{2,1,0:T(8,128)(2,1)}, bf16[2,256,1024]{2,1,0:T(8,128)(2,1)}, u32[]{:S(2)}, u32[]{:S(2)}) collective-permute-start(bf16[2,256,1024]{2,1,0:T(8,128)(2,1)} %get-tuple-element.239), channel_id=1, source_target_pairs={{0,4},{4,0},{8,12},{12,8},{1,5},{5,1},{9,13},{13,9},{2,6},{6,2},{1... | collective-permute-start | bytes 3145736 | tf_op jit(solution)/shard_map/ppermute | solution.py:49
  569.7 51.7 %collective-permute-start.75 = (bf16[4,512,128]{2,1,0:T(8,128)(2,1)}, bf16[4,512,128]{2,1,0:T(8,128)(2,1)}, u32[]{:S(2)}, u32[]{:S(2)}) collective-permute-start(bf16[4,512,128]{2,1,0:T(8,128)(2,1)} %get-tuple-element.255), channel_id=1, source_target_pairs={{0,16},{16,0},{1,17},{17,1},{2,18},{18,2},{3,19},{19,3},{4,20},{20... | collective-permute-start | bytes 1572872 | tf_op jit(solution)/shard_map/ppermute | solution.py:929
  (123 other events, 2037.9 us)
Sparse Core Ops, SparseCore 0:
  64.9 29.1 all-gather.6
  120.1 39.7 all-gather.8
  184.4 38.6 all-gather.10
  387.8 70.4 reduce-scatter.4
  460.6 41.2 reduce-scatter.8
  504.2 45.2 reduce-scatter.6
  552.0 33.1 reduce-scatter.10

commit v3 on v2

v3 whole, which is shorter than its diff:
```python
import functools
import math

import jax
import jax.numpy as jnp
from jax import lax
from jax.experimental import pallas as pl
from jax.experimental.pallas import tpu as pltpu
from jax.sharding import PartitionSpec as P

EPS = 1e-05
THETA = 1000000.0
LOG2E = 1.4426950408889634
F32 = jnp.float32
BF16 = jnp.bfloat16
NEAR = [(0, 1), (1, 0), (2, 3), (3, 2)]
FAR = [(0, 2), (2, 0), (1, 3), (3, 1)]
CROSS = [(0, 3), (3, 0), (1, 2), (2, 1)]
LIMIT = 56 * 1024 * 1024


def dot_nn(left, right):
    return lax.dot_general(left, right, (((1,), (0,)), ((), ())), preferred_element_type=F32)


def dot_nt(left, right):
    return lax.dot_general(left, right, (((1,), (1,)), ((), ())), preferred_element_type=F32)


def dot_tn(left, right):
    return lax.dot_general(left, right, (((0,), (0,)), ((), ())), preferred_element_type=F32)


def swap_bits(j):
    return ((j & 1) << 1) | (j >> 1)


def gather_ctx(own):
    far = lax.ppermute(own, "ctx", FAR)
    near = lax.ppermute(own, "ctx", NEAR)
    return [own, far, near, lax.ppermute(far, "ctx", NEAR)]


def add_near(own, got):
    return own[0].astype(F32) + got[0].astype(F32), (own[1].astype(F32) + got[1].astype(F32)).astype(BF16)


def reduce_near(own, near):
    return add_near(own, lax.ppermute(near, "ctx", NEAR))


def reduce_far(mine, away):
    return mine + lax.ppermute(away, "ctx", FAR).astype(F32)


def reduce_ctx(own, near):
    got = lax.ppermute(own[1], "ctx", FAR), lax.ppermute(near[0], "ctx", NEAR), lax.ppermute(near[1], "ctx", CROSS)
    return own[0].astype(F32) + got[0].astype(F32) + got[1].astype(F32) + got[2].astype(F32)


def to_tp(value, e):
    return lax.ppermute(value, "tp", [(i, i ^ e) for i in range(4)])


def exchange_tp(blocks):
    return [blocks[0]] + [to_tp(blocks[e], e) for e in range(1, len(blocks))]


def exchange_heads(q_same, kv):
    return [q_same, *exchange_tp(kv)]


def gather_shard(own, shards):
    if shards == 2:
        return [own, lax.ppermute(own, "shard", [(0, 1), (1, 0)])]
    every = lax.all_gather(own, "shard", axis=0, tiled=False)
    return [every.transpose(1, 2, 0, 3).reshape(*own.shape[:2], -1)]


def send_shard(parts, shards):
    if shards == 2:
        return lax.ppermute(parts[1], "shard", [(0, 1), (1, 0)])
    blocks, units, width = parts[0].shape
    every = parts[0].reshape(blocks, units, shards, width // shards).transpose(2, 0, 1, 3)
    return lax.psum_scatter(every, "shard", scatter_dimension=0, tiled=False)


def add_shard(got, parts):
    return (parts[0].astype(F32) + got.astype(F32)).astype(BF16) if len(parts) == 2 else got


def after(value, *others):
    return lax.optimization_barrier((value, *others))[0]


class Line:
    def __init__(self):
        self.last = ()

    def run(self, call, first, *others):
        result = call(after(first, *self.last), *others)
        self.last = (jax.tree.leaves(result)[0],)
        return result


def trade_tp(own, count):
    got = [own]
    for k in range(1, count):
        got.append(lax.ppermute(own, "tp", [(i, i ^ k) for i in range(count)]))
    index = lax.axis_index("tp")
    slots = []
    for slot in range(count):
        value = got[slot]
        for at in range(1, count):
            value = jnp.where(index == at, got[slot ^ at], value)
        slots.append(value)
    return jnp.stack(slots)


def join_shard(own, shards):
    if shards == 2:
        other = lax.ppermute(own, "shard", [(0, 1), (1, 0)])
        index = lax.axis_index("shard")
        return jnp.concatenate([jnp.where(index == 0, own, other), jnp.where(index == 0, other, own)])
    return lax.all_gather(own, "shard", axis=0, tiled=True)


def sum_all(vector, sizes):
    for name, size in sizes:
        step = 1
        while step < size:
            other = lax.ppermute(vector, name, [(i, i ^ step) for i in range(size)])
            vector = vector + other
            step *= 2
    return vector


def params():
    return pltpu.CompilerParams(vmem_limit_bytes=LIMIT)


def cost(micros):
    return pl.CostEstimate(flops=int(micros * 1.0e9), transcendentals=0, bytes_accessed=int(micros * 1.0e6))


def slot_copies(refs, held, sems):
    return [pltpu.make_async_copy(ref, held.at[k], sems.at[k]) for k, ref in enumerate(refs)]


def start_slots(refs, held, sems):
    @pl.when(pl.program_id(0) == 0)
    def _():
        for copy in slot_copies(refs, held, sems):
            copy.start()


def wait_slot(refs, held, sems, step=1):
    for k, copy in enumerate(slot_copies(refs, held, sems)):

        @pl.when(pl.program_id(0) == k // step)
        def _():
            copy.wait()


def lanes_low(rows):
    return lax.broadcasted_iota(jnp.int32, (rows, 128), 1) < 64


def pack(first, second, low):
    return jnp.where(low, first, second)


def head_sums(values):
    rows = lax.broadcasted_iota(jnp.int32, (128, 128), 0) >> 6
    columns = lax.broadcasted_iota(jnp.int32, (128, 128), 1) >> 6
    ones = jnp.where(rows == columns, 1.0, 0.0).astype(BF16)
    high = values.astype(BF16)
    rest = values - high.astype(F32)
    low = rest.astype(BF16)
    return dot_nn(high, ones) + dot_nn(low, ones)


def qkv_kernel(place_ref, *refs):
    x_refs, (w_ref, cos_ref, sin_ref, gain_ref) = refs[:4], refs[4:8]
    q_same, kv_same, beside, kv_other, raw_ref, x_ref, q_ref, kv_ref, sems = refs[8:]
    side, s, j = place_ref[1] & 1, pl.program_id(0), pl.program_id(1)
    rows = x_ref.shape[2]
    copies = slot_copies(x_refs, x_ref, sems)

    @pl.when((s == 0) & (j == 0))
    def _():
        for copy in copies:
            copy.start()

    for k, copy in enumerate(copies):

        @pl.when((s == 0) & (j == k))
        def _():
            copy.wait()

    y = dot_nn(x_ref[j, s], w_ref[:, :512])
    raw_ref[0, 0] = y[:, :384]
    low = lanes_low(rows)
    early = (lax.broadcasted_iota(jnp.int32, (rows, 128), 1) & 32) == 0
    cosine, sine = cos_ref[0, 0], sin_ref[0, 0]
    turned = []
    for b in range(3):
        u = y[:, b * 128 : (b + 1) * 128]
        r = lax.rsqrt(head_sums(u * u) * (1.0 / 64.0) + EPS)
        n = u * r * gain_ref[:, b * 128 : (b + 1) * 128]
        other = jnp.where(early, -pltpu.roll(n, 96, 1), pltpu.roll(n, 32, 1))
        turned.append(n * cosine + other * sine)
    key, value = turned[2], y[:, 384:512]
    q_ref[0] = (turned[0] * 0.125).astype(BF16)
    q_ref[1] = (turned[1] * 0.125).astype(BF16)
    kv_ref[0] = pack(key, pltpu.roll(value, 64, 1), low).astype(BF16)
    kv_ref[1] = pack(pltpu.roll(key, 64, 1), value, low).astype(BF16)
    q_same[0, 0] = q_ref[side]
    kv_same[0, 0] = kv_ref[side]
    beside[0, 0, :rows] = q_ref[1 - side]
    beside[0, 0, rows:] = kv_ref[1 - side]
    kv_other[0, 0] = kv_ref[1 - side]


def step_block(*shape):
    return pl.BlockSpec((1, 1, *shape), lambda s, j: (s, j, 0, 0))


def table_block(*shape):
    return pl.BlockSpec((1, 1, *shape), lambda s, j: (j, s, 0, 0))


def whole2(shape):
    return pl.BlockSpec(shape, lambda s, j: (0,) * len(shape))


def qkv_call(place, xs, w, cosine, sine, gains):
    slots = len(xs)
    pair, rows, width = xs[0].shape
    talls = (rows, rows, 2 * rows, rows)
    return pl.pallas_call(
        qkv_kernel,
        grid=(pair, slots),
        in_specs=[pl.BlockSpec(memory_space=pltpu.SMEM)]
        + [pl.BlockSpec(memory_space=pl.ANY)] * slots
        + [whole2(w.shape), table_block(rows, 128), table_block(rows, 128), whole2((1, 384))],
        out_specs=[step_block(tall, 128) for tall in talls] + [step_block(rows, 384)],
        out_shape=[jax.ShapeDtypeStruct((pair, slots, tall, 128), BF16) for tall in talls]
        + [jax.ShapeDtypeStruct((pair, slots, rows, 384), F32)],
        scratch_shapes=[
            pltpu.VMEM((slots, pair, rows, width), BF16),
            pltpu.VMEM((2, rows, 128), BF16),
            pltpu.VMEM((2, rows, 128), BF16),
            pltpu.SemaphoreType.DMA((slots,)),
        ],
        compiler_params=params(),
        cost_estimate=cost(15),
        name="qkv",
    )(place, *xs, w, cosine, sine, gains)


def lay_keys(place_ref, refs, kv_ref):
    c, t = place_ref[0], place_ref[1]
    for e, ref in enumerate(refs):
        for j in range(ref.shape[1]):
            kv_ref[4 * (c ^ swap_bits(j)) + (t ^ e)] = ref[0, j, ref.shape[2] - kv_ref.shape[1] :]


def lay_rows(place_ref, own_ref, got_ref, out_ref, high):
    c, side = place_ref[0], place_ref[1] & 1
    rows = out_ref.shape[2]
    low = lanes_low(rows)
    for ref, start in ((own_ref, 2 * side), (got_ref, 2 - 2 * side)):
        for j in range(4):
            g = c ^ swap_bits(j)
            value = ref[0, j, :rows] if len(ref.shape) == 4 else ref[j, :rows]
            turned = pltpu.roll(value, 64, 1)
            zero = jnp.zeros_like(value)
            if high:
                out_ref[g, start] = jnp.where(low, zero, turned)
                out_ref[g, start + 1] = jnp.where(low, zero, value)
            else:
                out_ref[g, start] = jnp.where(low, value, zero)
                out_ref[g, start + 1] = jnp.where(low, turned, zero)


def diagonal(rows, wide, edge):
    key = lax.broadcasted_iota(jnp.int32, (rows, wide), 0)
    column = lax.broadcasted_iota(jnp.int32, (rows, wide), 1)
    return (key <= (column & (rows - 1))) | (column >= edge)


def whole(shape):
    return pl.BlockSpec(shape, lambda j: (0,) * len(shape))


def attend_kernel(place_ref, *refs):
    q_own, keys = refs[0], refs[1:5]
    own_out, other_out, o_ref, lse_ref, q_ref, kv_ref, acc_ref, sum_ref, ret_ref = refs[5:]
    c, t, g = place_ref[0], place_ref[1], pl.program_id(1)
    side, base = t & 1, t & 2
    rows = kv_ref.shape[1]
    half, wide = 2 * rows, 4 * rows

    @pl.when(g == 0)
    def _():
        lay_keys(place_ref, keys, kv_ref)
        lay_rows(place_ref, q_own, keys[1], q_ref, False)

    queries = q_ref[g].reshape(wide, 128)
    acc_ref[...] = jnp.zeros_like(acc_ref)
    sum_ref[...] = jnp.zeros_like(sum_ref)

    def add(pair, skip, allowed):
        weights = jnp.exp2(dot_nt(pair, queries[skip:]) * LOG2E)
        if allowed is not None:
            weights = jnp.where(allowed, weights, 0.0)
        sum_ref[:, skip:] += jnp.sum(weights, axis=0, keepdims=True)
        acc_ref[:, skip:] += dot_tn(pair, weights.astype(BF16))

    def body(n, carry):
        add(kv_ref[pl.ds(2 * n, 2)].reshape(2 * rows, 128), 0, None)
        return carry

    last = 4 * g + base
    lax.fori_loop(0, last >> 1, body, 0)
    add(kv_ref[last], 0, diagonal(rows, wide, half))
    add(kv_ref[last + 1], half, diagonal(rows, half, half))
    total = sum_ref[...]
    out = acc_ref[...] / total
    o_ref[0, 0] = out[64:]
    lse_ref[0, 0] = jnp.log(total) * LOG2E
    flat = jnp.transpose(out)
    low = lanes_low(rows)
    slot = swap_bits(c ^ g)
    for u in range(2):
        first, second = (flat[(2 * u + h) * rows : (2 * u + h + 1) * rows] for h in range(2))
        ret_ref[u, slot] = pack(pltpu.roll(first, 64, 1), second, low).astype(BF16)

    @pl.when(g == 3)
    def _():
        own_out[0] = ret_ref[side]
        other_out[0] = ret_ref[1 - side]


def sequence_block(shape):
    return pl.BlockSpec((1, *shape[1:]), lambda s, j: (s, 0, 0, 0))


def attend_call(place, gets):
    pair, slots, rows, _ = gets[0].shape
    wide = 4 * rows
    return pl.pallas_call(
        attend_kernel,
        grid=(pair, 4),
        in_specs=[pl.BlockSpec(memory_space=pltpu.SMEM)] + [sequence_block(one.shape) for one in gets],
        out_specs=[sequence_block(gets[0].shape)] * 2 + [step_block(64, wide), step_block(1, wide)],
        out_shape=[jax.ShapeDtypeStruct(gets[0].shape, BF16)] * 2
        + [
            jax.ShapeDtypeStruct((pair, 4, 64, wide), F32),
            jax.ShapeDtypeStruct((pair, 4, 1, wide), F32),
        ],
        scratch_shapes=[
            pltpu.VMEM((4, 4, rows, 128), BF16),
            pltpu.VMEM((4 * slots, rows, 128), BF16),
            pltpu.VMEM((128, wide), F32),
            pltpu.VMEM((1, wide), F32),
            pltpu.VMEM((2, slots, rows, 128), BF16),
        ],
        compiler_params=params(),
        cost_estimate=cost(32),
        name="attend",
    )(place, *gets)


def own_block(rows, width):
    return pl.BlockSpec((1, 1, rows, width), lambda s, j: (jnp.minimum(j, 1), s, 0, 0))


def near_block(rows, width):
    return pl.BlockSpec((1, 1, rows, width), lambda s, j: (jnp.maximum(j - 2, 0), s, 0, 0))


def store_share(j, own_ref, near_ref, part):
    @pl.when(j < 2)
    def _():
        own_ref[0, 0] = part

    @pl.when(j >= 2)
    def _():
        near_ref[0, 0] = part


def out_kernel(place_ref, get_own, get_other, w_ref, mixed_ref, own_ref, near_ref, head_ref):
    side, j = place_ref[1] & 1, pl.program_id(1)
    head_ref[side] = get_own[0, 0]
    head_ref[1 - side] = get_other[0, 0]
    mixed = jnp.concatenate([head_ref[0], head_ref[1]], axis=1)
    mixed_ref[0, 0] = mixed
    store_share(j, own_ref, near_ref, dot_nt(mixed, w_ref[:, 512:]).astype(BF16))


def out_call(place, gets, w):
    pair, slots, rows, _ = gets[0].shape
    width = w.shape[0]
    return pl.pallas_call(
        out_kernel,
        grid=(pair, slots),
        in_specs=[pl.BlockSpec(memory_space=pltpu.SMEM)] + [step_block(rows, 128)] * 2 + [whole2(w.shape)],
        out_specs=[step_block(rows, 256), own_block(rows, width), near_block(rows, width)],
        out_shape=[
            jax.ShapeDtypeStruct((pair, slots, rows, 256), BF16),
            jax.ShapeDtypeStruct((2, pair, rows, width), BF16),
            jax.ShapeDtypeStruct((2, pair, rows, width), BF16),
        ],
        scratch_shapes=[pltpu.VMEM((2, rows, 128), BF16)],
        compiler_params=params(),
        cost_estimate=cost(9),
        name="out",
    )(place, *gets, w)


def out_back_kernel(place_ref, *refs):
    x_refs, w_ref, own_out, other_out, x_ref, send_ref, sems = refs[0:4], *refs[4:]
    side, j = place_ref[1] & 1, pl.program_id(0)
    start_slots(x_refs, x_ref, sems)
    wait_slot(x_refs, x_ref, sems)
    back = dot_nn(x_ref[j], w_ref[:, 512:]).astype(BF16)
    send_ref[0] = back[:, :128]
    send_ref[1] = back[:, 128:]
    own_out[0] = send_ref[side]
    other_out[0] = send_ref[1 - side]


def out_back_call(place, xs, w):
    slots = len(xs)
    rows, width = xs[0].shape
    return pl.pallas_call(
        out_back_kernel,
        grid=(slots,),
        in_specs=[pl.BlockSpec(memory_space=pltpu.SMEM)]
        + [pl.BlockSpec(memory_space=pl.ANY)] * slots
        + [whole(w.shape)],
        out_specs=[pl.BlockSpec((1, rows, 128), lambda j: (j, 0, 0))] * 2,
        out_shape=[jax.ShapeDtypeStruct((slots, rows, 128), BF16)] * 2,
        scratch_shapes=[
            pltpu.VMEM((slots, rows, width), BF16),
            pltpu.VMEM((2, rows, 128), BF16),
            pltpu.SemaphoreType.DMA((slots,)),
        ],
        compiler_params=params(),
        cost_estimate=cost(4),
        name="out_back",
    )(place, *xs, w)


def attend_back_kernel(place_ref, *refs):
    q_own, keys, back_own, back_got = refs[0], refs[1:5], refs[5], refs[6]
    o_ref, lse_ref = refs[7], refs[8]
    own_out, outs = refs[-11], refs[-10:-6]
    q_ref, kv_ref, back_ref, dkv_ref, acc_ref, ret_ref = refs[-6:]
    c, t, g = place_ref[0], place_ref[1], pl.program_id(0)
    side, base = t & 1, t & 2
    rows = kv_ref.shape[1]
    half, wide = 2 * rows, 4 * rows

    @pl.when(g == 0)
    def _():
        lay_keys(place_ref, keys, kv_ref)
        lay_rows(place_ref, q_own, keys[1], q_ref, False)
        lay_rows(place_ref, back_own, back_got, back_ref, True)
        dkv_ref[...] = jnp.zeros_like(dkv_ref)

    queries = q_ref[g].reshape(wide, 128)
    given = back_ref[g].reshape(wide, 128)
    delta = jnp.sum(jnp.transpose(given.astype(F32))[64:] * o_ref[0, 0], axis=0, keepdims=True)
    lse = lse_ref[0, 0]
    acc_ref[...] = jnp.zeros_like(acc_ref)

    def block(pair, skip, allowed):
        probs = jnp.exp2(dot_nt(pair, queries[skip:]) * LOG2E - lse[:, skip:])
        if allowed is not None:
            probs = jnp.where(allowed, probs, 0.0)
        slopes = dot_nt(pair, given[skip:])
        score_back = (probs * (slopes - delta[:, skip:])).astype(BF16)
        acc_ref[skip:] += dot_tn(score_back, pair)
        return dot_nn(probs.astype(BF16), given[skip:]) + dot_nn(score_back, queries[skip:])

    def body(n, carry):
        pair = kv_ref[pl.ds(2 * n, 2)].reshape(2 * rows, 128)
        dkv_ref[pl.ds(2 * n, 2)] += block(pair, 0, None).reshape(2, rows, 128)
        return carry

    last = 4 * g + base
    lax.fori_loop(0, last >> 1, body, 0)
    dkv_ref[last] += block(kv_ref[last], 0, diagonal(rows, wide, half))
    dkv_ref[last + 1] += block(kv_ref[last + 1], half, diagonal(rows, half, half))
    low = lanes_low(rows)
    slot = swap_bits(c ^ g)
    for u in range(2):
        first, second = (acc_ref[(2 * u + h) * rows : (2 * u + h + 1) * rows] * 0.125 for h in range(2))
        ret_ref[u, slot] = pack(first, pltpu.roll(second, 64, 1), low).astype(BF16)

    @pl.when(g == pl.num_programs(0) - 1)
    def _():
        own_out[0] = ret_ref[side]
        outs[1][0, :, :rows] = ret_ref[1 - side]
        for e in range(4):
            for j in range(4):
                outs[e][0, j, outs[e].shape[2] - rows :] = dkv_ref[4 * (c ^ swap_bits(j)) + (t ^ e)].astype(BF16)


def attend_back_call(place, at, gets, backs, o, lse):
    _, slots, rows, _ = gets[0].shape
    wide = 4 * rows
    block = lambda one: pl.BlockSpec((1, *one.shape[1:]), lambda g: (at, 0, 0, 0))
    return pl.pallas_call(
        attend_back_kernel,
        grid=(4,),
        in_specs=[pl.BlockSpec(memory_space=pltpu.SMEM)]
        + [block(one) for one in gets]
        + [whole(one.shape) for one in backs]
        + [pl.BlockSpec((1, 1, tall, wide), lambda g: (at, g, 0, 0)) for tall in (64, 1)],
        out_specs=[whole((1, *one.shape[1:])) for one in gets],
        out_shape=[jax.ShapeDtypeStruct((1, *one.shape[1:]), BF16) for one in gets],
        scratch_shapes=[
            pltpu.VMEM((4, 4, rows, 128), BF16),
            pltpu.VMEM((4 * slots, rows, 128), BF16),
            pltpu.VMEM((4, 4, rows, 128), BF16),
            pltpu.VMEM((4 * slots, rows, 128), F32),
            pltpu.VMEM((wide, 128), F32),
            pltpu.VMEM((2, slots, rows, 128), BF16),
        ],
        compiler_params=params(),
        cost_estimate=cost(8),
        name="attend_back",
    )(place, *gets, *backs, o, lse)


def qkv_back_kernel(place_ref, *refs):
    q_own, keys, (raw_ref, cos_ref, sin_ref, gain_ref, w_ref) = refs[0], refs[1:5], refs[5:10]
    back_ref, own_ref, near_ref, share_ref, head_ref, pair_ref = refs[10:]
    side, j = place_ref[1] & 1, pl.program_id(0)
    rows = raw_ref.shape[2]
    head_ref[side] = q_own[0, 0].astype(F32)
    head_ref[1 - side] = keys[1][0, 0, :rows].astype(F32)
    pair_ref[side] = keys[0][0, 0].astype(F32) + keys[2][0, 0].astype(F32)
    pair_ref[1 - side] = keys[1][0, 0, rows:].astype(F32) + keys[3][0, 0].astype(F32)
    low = lanes_low(rows)
    early = (lax.broadcasted_iota(jnp.int32, (rows, 128), 1) & 32) == 0
    cosine, sine = cos_ref[0, 0], sin_ref[0, 0]

    @pl.when(j == 0)
    def _():
        share_ref[...] = jnp.zeros_like(share_ref)

    even, odd = pair_ref[0], pair_ref[1]
    key = pack(even, pltpu.roll(odd, 64, 1), low)
    value = pack(pltpu.roll(even, 64, 1), odd, low)
    outs = []
    for b, given in enumerate((head_ref[0], head_ref[1], key)):
        z = sine * given
        cotangent = given * cosine + jnp.where(early, pltpu.roll(z, 96, 1), -pltpu.roll(z, 32, 1))
        u = raw_ref[0, 0, :, b * 128 : (b + 1) * 128]
        gain = gain_ref[:, b * 128 : (b + 1) * 128]
        r = lax.rsqrt(head_sums(u * u) * (1.0 / 64.0) + EPS)
        mean = head_sums(u * gain * cotangent) * (1.0 / 64.0)
        share_ref[:, b * 128 : (b + 1) * 128] += jnp.sum(cotangent * u * r, axis=0, keepdims=True)
        outs.append((r * gain * cotangent - u * (r * r * r) * mean).astype(BF16))
    outs.append(value.astype(BF16))
    back = jnp.concatenate(outs, axis=1)
    back_ref[0, 0] = back
    store_share(j, own_ref, near_ref, dot_nt(back, w_ref[:, :512]).astype(BF16))


def qkv_back_call(place, at, gets, raw, cosine, sine, gains, w):
    _, slots, rows, _ = raw.shape
    width = w.shape[0]
    here = lambda *shape: pl.BlockSpec((1, 1, *shape), lambda j: (0, j, 0, 0))
    table = pl.BlockSpec((1, 1, rows, 128), lambda j: (j, at, 0, 0))
    return pl.pallas_call(
        qkv_back_kernel,
        grid=(slots,),
        in_specs=[pl.BlockSpec(memory_space=pltpu.SMEM)]
        + [here(*one.shape[2:]) for one in gets]
        + [pl.BlockSpec((1, 1, rows, 384), lambda j: (at, j, 0, 0)), table, table, whole((1, 384)), whole(w.shape)],
        out_specs=[
            here(rows, 512),
            pl.BlockSpec((1, 1, rows, width), lambda j: (jnp.minimum(j, 1), 0, 0, 0)),
            pl.BlockSpec((1, 1, rows, width), lambda j: (jnp.maximum(j - 2, 0), 0, 0, 0)),
            whole((1, 384)),
        ],
        out_shape=[
            jax.ShapeDtypeStruct((1, slots, rows, 512), BF16),
            jax.ShapeDtypeStruct((2, 1, rows, width), BF16),
            jax.ShapeDtypeStruct((2, 1, rows, width), BF16),
            jax.ShapeDtypeStruct((1, 384), F32),
        ],
        scratch_shapes=[pltpu.VMEM((2, rows, 128), F32), pltpu.VMEM((2, rows, 128), F32)],
        compiler_params=params(),
        cost_estimate=cost(8),
        name="qkv_back",
    )(place, *gets, raw, cosine, sine, gains, w)


def ffn_kernel(at, halves, *refs):
    offset_ref, x_refs, given_refs, pieces = refs[0], refs[1:5], refs[5:9], refs[9 : 9 + 3 * halves]
    refs = refs[-18:]
    act_out, outs = refs[0], refs[1:5]
    w_ref, x_ref, given_ref, act_ref, held = *refs[5:9], refs[9:13]
    sems, x_sems, given_sems, act_sems, out_sems = refs[13:]
    _, rows, width = x_ref.shape
    count = 2 * rows
    blocks, depth, span = pieces[0].shape

    def copies(j):
        return [
            pltpu.make_async_copy(
                pieces[j * halves + p].at[i],
                w_ref.at[j, pl.ds(i * depth, depth), pl.ds(pl.multiple_of(offset_ref[p], 128), span)],
                sems.at[j, p, i],
            )
            for p in range(halves)
            for i in range(blocks)
        ]

    def start(found):
        for copy in found:
            copy.start()

    def wait(found):
        for copy in found:
            copy.wait()

    tokens = slot_copies([ref.at[at] for ref in x_refs], x_ref, x_sems)
    givens = slot_copies([ref.at[at] for ref in given_refs], given_ref, given_sems)
    for found in (tokens[:2], copies(0), copies(1), copies(2), givens[:2], tokens[2:], givens[2:]):
        start(found)
    leaving = []

    def leave(source, target, sem):
        leaving.append(pltpu.make_async_copy(source, target, sem))
        leaving[-1].start()

    def leave_act(kind, k, value):
        act_ref[kind, 2 * k : 2 * k + 2] = value.reshape(2, rows, -1)
        leave(act_ref.at[kind, pl.ds(2 * k, 2)], act_out.at[kind, pl.ds(2 * k, 2)], act_sems.at[kind, k])

    def leave_part(n, value):
        held[n][...] = value.astype(BF16).reshape(2, rows, width)
        leave(held[n], outs[n].at[:, at] if n < 2 else outs[n], out_sems.at[n])

    for k in range(2):
        wait(tokens[2 * k : 2 * k + 2])
        x = x_ref[2 * k : 2 * k + 2].reshape(count, width)
        if k == 0:
            wait(copies(0))
        gate = dot_nt(x, w_ref[0])
        if k == 0:
            wait(copies(1))
        up = dot_nt(x, w_ref[1])
        sig = jax.nn.sigmoid(gate)
        swish = gate * sig
        hidden = (swish * up).astype(BF16)
        leave_act(2, k, hidden)
        if k == 0:
            wait(copies(2))
        wait(givens[2 * k : 2 * k + 2])
        hidden_back = dot_nt(given_ref[2 * k : 2 * k + 2].reshape(count, width), w_ref[2])
        gate_back = (hidden_back * up * (sig * (1.0 + gate * (1.0 - sig)))).astype(BF16)
        leave_act(0, k, gate_back)
        up_back = (hidden_back * swish).astype(BF16)
        leave_act(1, k, up_back)
        leave_part(2 + k, dot_nn(gate_back, w_ref[0]) + dot_nn(up_back, w_ref[1]))
        leave_part(k, dot_nn(hidden, w_ref[2]))
    wait(leaving)


def ffn_call(offsets, at, xs, given, pieces, before):
    pair, rows, width = xs[0].shape
    halves = len(pieces[0])
    blocks, depth, _ = pieces[0][0].shape
    hidden = blocks * depth
    part, act = (2, rows, width), (3, 4, rows, hidden)
    both = (2, pair, rows, width)
    parts = [piece for row in pieces for piece in row]
    first = 9 + len(parts)
    before = before or []
    return pl.pallas_call(
        functools.partial(ffn_kernel, at, halves),
        in_specs=[pl.BlockSpec(memory_space=pltpu.SMEM)] + [pl.BlockSpec(memory_space=pl.ANY)] * (8 + len(parts) + len(before)),
        out_specs=[pl.BlockSpec(memory_space=pl.ANY)] * 5,
        out_shape=[jax.ShapeDtypeStruct(shape, BF16) for shape in (act, both, both, part, part)],
        input_output_aliases={first + i: 1 + i for i in range(len(before))},
        scratch_shapes=[
            pltpu.VMEM((3, hidden, width), BF16),
            pltpu.VMEM((4, rows, width), BF16),
            pltpu.VMEM((4, rows, width), BF16),
            pltpu.VMEM(act, BF16),
        ]
        + [pltpu.VMEM(part, BF16)] * 4
        + [
            pltpu.SemaphoreType.DMA((3, halves, blocks)),
            pltpu.SemaphoreType.DMA((4,)),
            pltpu.SemaphoreType.DMA((4,)),
            pltpu.SemaphoreType.DMA((3, 2)),
            pltpu.SemaphoreType.DMA((4,)),
        ],
        compiler_params=params(),
        cost_estimate=cost(22),
        name="ffn",
    )(offsets, *xs, *given, *parts, *before)


def weight_kernel(halves, offset_ref, *refs):
    lefts, rights = refs[0:2], refs[2:6]
    outs, total_ref = refs[6 : 6 + halves], refs[6 + halves]
    total = 0.0
    for s, left in enumerate(lefts):
        a = left[0]
        total = total + dot_tn(a.reshape(-1, a.shape[-1]), jnp.concatenate([ref[s] for ref in rights]))
    total_ref[...] = total.astype(BF16)
    blocks, depth, span = outs[0].shape
    for p in range(halves):
        start = pl.multiple_of(offset_ref[p], 128)
        for i in range(blocks):
            outs[p][i] = total_ref[i * depth : (i + 1) * depth, pl.ds(start, span)]


def weight_call(offsets, kind, acts, rights, halves, blocks):
    units, width = acts[0].shape[-1], rights[0].shape[-1]
    unit = (1, *acts[0].shape[1:])
    part = (blocks, units // blocks, width // halves)
    return pl.pallas_call(
        functools.partial(weight_kernel, halves),
        grid=(1,),
        in_specs=[pl.BlockSpec(memory_space=pltpu.SMEM)]
        + [pl.BlockSpec(unit, lambda j: (kind, 0, 0, 0))] * 2
        + [whole(one.shape) for one in rights],
        out_specs=[whole(part)] * halves,
        out_shape=[jax.ShapeDtypeStruct(part, BF16)] * halves,
        scratch_shapes=[pltpu.VMEM((units, width), BF16)],
        compiler_params=params(),
        cost_estimate=cost(10),
        name="weight",
    )(offsets, *acts, *rights)


def small_weight_kernel(halves, near, count, place_ref, offset_ref, *refs):
    lefts, rights, outs, total_ref = refs[:count], refs[count : -halves - 1], refs[-halves - 1 : -1], refs[-1]
    t = place_ref[1]
    total = 0.0
    for s in range(2):
        a = lefts[0][s] if count == 1 else lefts[s][0]
        pieces = [ref[s] for ref in rights] if len(rights) == 4 else [ref[...] for ref in rights[4 * s : 4 * s + 4]]
        total = total + dot_tn(a.reshape(-1, a.shape[-1]), jnp.concatenate(pieces))
    total_ref[...] = total.astype(BF16)
    blocks, _, span = outs[0].shape
    for p in range(halves):
        for e in range(blocks):
            if near:
                outs[p][e] = total_ref[:, pl.ds(pl.multiple_of(offset_ref[p] + (t ^ e) * span, 128), span)]
            else:
                outs[p][e] = total_ref[:, e * span : (e + 1) * span]


def small_weight_call(place, offsets, lefts, rights, halves, blocks, near):
    rows, width = lefts[0].shape[-1], rights[0].shape[-1]
    part = (blocks, rows, width // blocks // halves)
    return pl.pallas_call(
        functools.partial(small_weight_kernel, halves, near, len(lefts)),
        in_specs=[pl.BlockSpec(memory_space=pltpu.SMEM)] * 2
        + [pl.BlockSpec(memory_space=pltpu.VMEM)] * (len(lefts) + len(rights)),
        out_specs=[pl.BlockSpec(memory_space=pltpu.VMEM)] * halves,
        out_shape=[jax.ShapeDtypeStruct(part, BF16)] * halves,
        scratch_shapes=[pltpu.VMEM((rows, width), BF16)],
        compiler_params=params(),
        cost_estimate=cost(5),
        name="small_weight",
    )(place, offsets, *lefts, *rights)


def inverse_root(values):
    return lax.rsqrt(jnp.mean(values * values, axis=-1, keepdims=True) + EPS)


def norm_back(values, root, gain, given):
    mean = jnp.mean(values * gain * given, axis=-1, keepdims=True)
    return root * gain * given - values * (root * root * root) * mean


def per_device(
    sizes,
    tokens,
    positions,
    first_gain,
    query_weight,
    key_weight,
    value_weight,
    query_gain,
    key_gain,
    output_weight,
    second_gain,
    gate_weight,
    up_weight,
    down_weight,
    upstream,
):
    shards, ctx, tp = sizes["shard"], sizes["ctx"], sizes["tp"]
    groups = ("shard", "tp")
    sequences, rows, width = tokens.shape
    head_dim = query_gain.shape[0]
    depth = query_weight.shape[0]
    units = gate_weight.shape[1]
    c, t = lax.axis_index("ctx"), lax.axis_index("tp")
    place = jnp.stack([c, t]).astype(jnp.int32)
    trade = [(i * tp + k, k * ctx + i) for i in range(ctx) for k in range(tp)]

    line = Line()
    shard = lax.axis_index("shard")
    small = jnp.concatenate([query_weight, key_weight, value_weight, output_weight.T], axis=1)
    small = lax.ppermute(small, ("ctx", "tp"), trade)
    blocks_attn = trade_tp(small, tp)
    w_attn = join_shard(blocks_attn.reshape(tp * depth, -1), shards)

    large = jnp.stack([gate_weight.T, up_weight.T, down_weight]).reshape(3, ctx, units // ctx, depth)
    large = lax.all_to_all(large, "ctx", 1, 1, tiled=True)
    large = after(large, small).transpose(0, 2, 1, 3).reshape(3, units // ctx, ctx * depth)
    aligned = depth % 128 == 0
    starts = jnp.stack([shard, 1 - shard]) if shards == 2 else jnp.zeros((2,), jnp.int32)
    starts = (starts * (width // 2)).astype(jnp.int32)

    mine = lax.dynamic_slice_in_dim(positions, t * rows, rows, 1).astype(F32)
    places = jnp.stack(gather_ctx(mine))
    freqs = jnp.exp(-math.log(THETA) * jnp.arange(0, head_dim, 2).astype(F32) / head_dim)
    angles = places[..., None] * freqs
    cosine, sine = jnp.cos(angles), jnp.sin(angles)
    cosine = jnp.concatenate([cosine] * 4, axis=-1)
    sine = jnp.concatenate([sine] * 4, axis=-1)
    gains = jnp.concatenate([jnp.tile(query_gain, 4), jnp.tile(key_gain, 2)])[None]

    x = tokens.astype(F32)
    root = inverse_root(x)
    first = (x * root * first_gain).astype(BF16)
    given = upstream.astype(F32)

    pair = range(sequences)
    first_all = gather_ctx(first)
    one = line.run(qkv_call, place, first_all, w_attn, cosine, sine, gains)
    heads, raw = exchange_heads(one[0], (one[1], one[2], one[1], one[3])), one[4]
    lines = [lax.all_gather(after(large[0], blocks_attn), "tp", axis=0, tiled=False)]
    for j in (1, 2):
        lines.append(lax.all_gather(after(large[j], *heads), "tp", axis=0, tiled=False))
    w_ffn = [gather_shard(one, shards) for one in lines]
    upstream_all = gather_ctx(after(upstream, raw))
    heads = after(heads, w_ffn[0][-1], *upstream_all)
    own, other, o, lse = line.run(attend_call, place, heads)
    own = after(own, lines[1])
    mixed, own, near = line.run(out_call, place, [own, to_tp(other, 1)], w_attn)
    mine, away = line.run(lambda got, own: add_near(own, got), lax.ppermute(near, "ctx", NEAR), own)

    def middle_of(far, mine):
        middle = x + (mine + far.astype(F32))
        middle_root = inverse_root(middle)
        return (middle * middle_root * second_gain).astype(BF16), middle, middle_root

    mine = after(mine, lines[2], w_ffn[1][-1])
    second, middle, middle_root = line.run(middle_of, lax.ppermute(away, "ctx", FAR), mine)
    seconds = gather_ctx(second)
    ffn = []
    for s in pair:
        before = ffn[-1][1:3] if ffn else None
        ffn.append(line.run(ffn_call, starts, s, seconds, upstream_all, w_ffn, before))
    out_shares = ffn[-1][1:3]

    back_rows, mixed_back_all, backs_sent = [], [], []

    def turn_back(second_back, s):
        middle_back = given[s] + norm_back(middle[s], middle_root[s], second_gain, second_back)
        return middle_back.astype(BF16), middle_back, jnp.sum(second_back * middle[s] * middle_root[s], axis=0)

    def turn(s, call, *shares):
        low, middle_back, share = line.run(lambda first, *rest: turn_back(call(first, *rest), s), *shares)
        back_rows.append(middle_back)
        mixed_back_all.append(gather_ctx(low))
        return share

    def back_out(s):
        own, other = line.run(out_back_call, place, mixed_back_all[s], w_attn)
        backs_sent.append([own, to_tp(other, 1)])

    own, near = ffn[0][3], ffn[0][4]
    shares = own[0], *(
        lax.ppermute(value, "ctx", way) for value, way in ((own[1], FAR), (near[0], NEAR), (near[1], CROSS))
    )
    second_share = turn(0, lambda *parts: sum(part.astype(F32) for part in parts), *shares)
    mine, away = line.run(lambda got, own: add_near(own, got), lax.ppermute(ffn[1][4], "ctx", NEAR), ffn[1][3])
    away = lax.ppermute(away, "ctx", FAR)
    near = aligned and shards == 2
    count = shards * tp
    small = 2 if near else 1, tp if near else 1, near
    halves = 2 if shards == 2 else 1
    sums, g_ffn = [], []

    def weight(kind):
        rights = upstream_all if kind == 2 else seconds
        sums.append(line.run(weight_call, starts, kind, [one[0] for one in ffn], rights, halves, tp))

    def send(kind):
        parts = sums[kind]
        return send_shard(after(parts, g_ffn[-1]) if g_ffn else parts, shards)

    def add(kind, moved):
        added = line.run(add_shard, moved, sums[kind])
        sums[kind] = added
        g_ffn.append(added)

    def scatter(kind):
        return lax.psum_scatter(g_ffn[kind], "tp", scatter_dimension=0, tiled=False)

    weight(0)
    moved = send(0)
    weight(1)
    back_out(0)
    second_share = second_share + turn(1, lambda far, own: own + far.astype(F32), away, mine)
    weight(2)
    back_out(1)
    add(0, moved)
    moved = send(1)
    near_sum, away = line.run(
        lambda got, own: add_near(own, got), lax.ppermute(after(out_shares[1], backs_sent[0]), "ctx", NEAR), out_shares[0]
    )
    far_sum = lax.ppermute(away, "ctx", FAR)
    half = line.run(attend_back_call, after(place, *backs_sent[1]), 0, heads, backs_sent[0], o, lse)
    got = [exchange_heads(half[0], half[1:])]
    given_all = [*mixed_back_all[0], *mixed_back_all[1]]
    out_parts = line.run(small_weight_call, place, starts, [mixed], given_all, *small)
    out_moved = lax.ppermute(out_parts[1], "shard", [(0, 1), (1, 0)]) if near else None
    add(1, moved)
    moved = send(2)
    result = line.run(lambda far, mine: ((middle + mine) + far.astype(F32)).astype(BF16), far_sum, near_sum)
    full = line.run(attend_back_call, place, 1, heads, backs_sent[1], o, lse)
    got.append(exchange_heads(full[0], full[1:]))
    add(2, moved)
    g_ffn = [scatter(kind) for kind in range(3)]
    def last(far, mine, s):
        first_back = mine[0] + far[0].astype(F32)
        gradient = back_rows[s] + norm_back(x[s], root[s], first_gain, first_back)
        return jnp.sum(first_back * x[s] * root[s], axis=0), gradient

    backs, firsts, head_share, first_share, gradients = [], [], 0.0, 0.0, []
    for s in pair:
        back, own, other, share = line.run(qkv_back_call, place, s, got[s], raw, cosine, sine, gains, w_attn)
        backs.append(back)
        head_share = head_share + share
        other = lax.ppermute(other, "ctx", NEAR)
        if s == 0:
            mine, away = line.run(lambda got, own: add_near(own, got), other, own)
            firsts.append((lax.ppermute(away, "ctx", FAR), mine))
    parts = line.run(small_weight_call, place, starts, backs, first_all, *small)
    moved = lax.ppermute(parts[1], "shard", [(0, 1), (1, 0)]) if near else None
    mine, away = line.run(lambda got, own: add_near(own, got), other, own)
    firsts.append((lax.ppermute(away, "ctx", FAR), mine))
    for s in pair:
        share, gradient = line.run(lambda a, b: last(a, b, s), *firsts[s])
        first_share = first_share + share
        gradients.append(gradient)
    shares = jnp.concatenate([first_share, second_share, head_share[0]])
    shares = sum_all(shares, [(name, sizes[name]) for name in ("ctx", "shard", "tp")])

    if near:
        both = lambda a, b: (a.astype(F32) + b.astype(F32)).astype(BF16)
        g_attn = line.run(
            lambda a, b: jnp.concatenate([both(a, b), both(out_moved, out_parts[0])], axis=1), moved, parts[0]
        )
        g_attn = exchange_tp([g_attn[e] for e in range(tp)])
    else:
        g_attn = jnp.concatenate([parts[0][0], out_parts[0][0]])
        g_attn = g_attn.reshape(-1, count, width // count).transpose(1, 0, 2)
        g_attn = lax.psum_scatter(g_attn, groups, scatter_dimension=0, tiled=False)
    def settle(g):
        g = g.reshape(3, units, depth).astype(F32)
        return g[0].T, g[1].T, g[2]

    g_ffn = jnp.stack(g_ffn).reshape(3, units // ctx, ctx, depth).transpose(0, 2, 1, 3)
    g_ffn = lax.all_to_all(g_ffn, "ctx", 1, 1, tiled=True)
    g_ffn = line.run(settle, g_ffn)

    if near:
        g_attn = line.run(lambda *parts: sum(part.astype(F32) for part in parts).astype(BF16), *g_attn)
    g_attn = lax.ppermute(g_attn, ("ctx", "tp"), trade).astype(F32)
    heads_end = query_weight.shape[1]
    pairs = key_weight.shape[1]

    head_total = shares[2 * width :]
    return (
        result,
        jnp.stack(gradients),
        g_attn[:heads_end].T,
        g_attn[heads_end : heads_end + pairs].T,
        g_attn[heads_end + pairs : heads_end + 2 * pairs].T,
        g_attn[heads_end + 2 * pairs :],
        *g_ffn,
        shares[:width],
        shares[width : 2 * width],
        jnp.sum(head_total[: 4 * head_dim].reshape(4, head_dim), axis=0),
        jnp.sum(head_total[4 * head_dim :].reshape(2, head_dim), axis=0),
    )


def solution(mesh):
    rows = P("shard", ("ctx", "tp"), None)
    wide = P(("shard", "ctx"), "tp")
    tall = P("tp", ("shard", "ctx"))
    none = P()
    in_specs = (
        rows, P("shard", "ctx"), none, wide, wide, wide, none, none, tall, none, wide, wide, tall, rows,
    )
    out_specs = (rows, rows, wide, wide, wide, tall, wide, wide, tall, none, none, none, none)
    sizes = {name: mesh.shape[name] for name in ("shard", "ctx", "tp")}
    return jax.shard_map(
        functools.partial(per_device, sizes), mesh=mesh, in_specs=in_specs, out_specs=out_specs, check_vma=False
    )
```

time: 685 us -> 621 us (0.907)
  the two profiles are of different devices: /device:TPU:0 before, /device:TPU:6 now
where the time goes in v3:
time: 621 us; the launch traced here: 616 us
  Pallas kernels  222 us (36%)
  waiting for transfers between devices  193 us (31%)
  starting transfers between devices  97.3 us (16%)
  other arithmetic  66.1 us (11%)
  local copies, waits for them, and re-layouts  22.2 us (4%)
  between operations  15.1 us (2%)
    pallas_call x2, Pallas kernels, attend_back_call(): pl.pallas_call(attend_back_kernel, grid=(4,), in_specs=[pl.BlockSpec(memo...  58.8 us
    ppermute x15, waiting for transfers between devices, to_tp(): return lax.ppermute(value, 'tp', [(i, i ^ e) for i in range(4)])  56.7 us
    pallas_call x2, Pallas kernels, ffn_call(): pl.pallas_call(functools.partial(ffn_kernel, at, halves), in_specs=[pl.Bl...  50.2 us
    ppermute x6, waiting for transfers between devices, gather_ctx(): far = lax.ppermute(own, 'ctx', FAR)  45.9 us
    ppermute x15, starting transfers between devices, to_tp(): return lax.ppermute(value, 'tp', [(i, i ^ e) for i in range(4)])  39.4 us
    pallas_call x3, Pallas kernels, weight_call(): pl.pallas_call(functools.partial(weight_kernel, halves), grid=(1,), in_sp...  30.8 us
    all_gather x2, waiting for transfers between devices, per_device(): lax.all_gather(after(large[j], *heads), 'tp', axis=0, tiled=False)  27.7 us
    pallas_call x1, Pallas kernels, attend_call(): pl.pallas_call(attend_kernel, grid=(pair, 4), in_specs=[pl.BlockSpec(memo...  26 us
  transfers between devices with their start and end apart: 73, of which 27 were waited for; matrix products, arithmetic and copies ran while one was open for 11% of the time, Pallas kernels for 31%

profile of v3, /device:TPU:6, one launch (start us, length us, event | category | flops | bytes accessed | tf_op | source)
XLA Modules:
  0.0 616.1 jit_solution(4527907642347350277)
XLA Ops:
  37.3 10.0 %collective-permute-done.5 = bf16[128,768]{0,1:T(8,128)(2,1)S(1)} collective-permute-done((bf16[128,768]{0,1:T(8,128)(2,1)S(1)}, bf16[128,768]{0,1:T(8,128)(2,1)S(1)}, u32[]{:S(2)}, u32[]{:S(2)}) %collective-permute-start.5) | collective-permute-done | bytes 196640 | tf_op jit(solution)/shard_map/ppermute | solution.py:109
  57.9 10.0 %collective-permute-done.7 = bf16[512,768]{1,0:T(8,128)(2,1)} collective-permute-done((bf16[512,768]{1,0:T(8,128)(2,1)S(1)}, bf16[512,768]{1,0:T(8,128)(2,1)}, u32[]{:S(2)}, u32[]{:S(2)}) %collective-permute-start.7) | collective-permute-done | bytes 786464 | tf_op jit(solution)/shard_map/ppermute | solution.py:122
  70.4 12.5 %qkv.1 = (bf16[2,4,256,128]{3,2,1,0:T(8,128)(2,1)}, bf16[2,4,256,128]{3,2,1,0:T(8,128)(2,1)}, bf16[2,4,512,128]{3,2,1,0:T(8,128)(2,1)}, bf16[2,4,256,128]{3,2,1,0:T(8,128)(2,1)}, f32[2,4,256,384]{3,2,1,0:T(8,128)}) custom-call(s32[2]{0:T(128)} %pad_add_fusion.place_ref, bf16[2,256,1024]{2,1,0:T(8,128)(2,1)} %multiply_convert_fusion.1.refs_0_.refs_2_, ...), custom_call_target="tpu_custom_call" | custom-call | flops 15000000512 | bytes 15000000 | tf_op jit(solution)/shard_map/qkv/pallas_call | solution.py:241
  89.9 17.9 %collective-permute-done.15.refs_6_.refs_3_ = bf16[2,256,1024]{2,1,0:T(8,128)(2,1)} collective-permute-done((bf16[2,256,1024]{2,1,0:T(8,128)(2,1)S(1)}, bf16[2,256,1024]{2,1,0:T(8,128)(2,1)}, u32[]{:S(2)}, u32[]{:S(2)}) %collective-permute-start.15) | collective-permute-done | bytes 1048608 | tf_op jit(solution)/shard_map/ppermute | solution.py:39
  116.3 20.2 %collective-permute-done.13.refs_4_ = bf16[2,4,256,128]{3,2,1,0:T(8,128)(2,1)} collective-permute-done((bf16[2,4,256,128]{3,2,1,0:T(8,128)(2,1)}, bf16[2,4,256,128]{3,2,1,0:T(8,128)(2,1)}, u32[]{:S(2)}, u32[]{:S(2)}) %collective-permute-start.13) | collective-permute-done | bytes 524320 | tf_op jit(solution)/shard_map/ppermute | solution.py:62
  136.5 10.4 %all-gather.11.cloned.1.call-start = ((), (), s32[]{:S(2)}) async-start(), calls=%async_computation.10 | async-start | bytes 1474560 | tf_op jit(solution)/shard_map/all_gather | solution.py:853
  147.0 26.0 %attend.1 = (bf16[2,4,256,128]{3,2,1,0:T(8,128)(2,1)}, bf16[2,4,256,128]{3,2,1,0:T(8,128)(2,1)}, f32[2,4,64,1024]{3,2,1,0:T(8,128)}, f32[2,4,1,1024]{3,2,1,0:T(1,128)}) custom-call(s32[2]{0:T(128)} %pad_add_fusion.place_ref, bf16[2,4,256,128]{3,2,1,0:T(8,128)(2,1)} %get-tuple-element.122.refs_0_, bf16[2,4,256,128]{3,2,1,0:T(8,128)(2,1)} %get-tuple-element.123.refs_1_, ...), custom_call_target="tpu_custom_call" | custom-call | flops 32000000000 | bytes 32000000 | tf_op jit(solution)/shard_map/attend/pallas_call | solution.py:353
  173.7 11.7 %collective-permute-done.18.get_other = bf16[2,4,256,128]{3,2,1,0:T(8,128)(2,1)S(1)} collective-permute-done((bf16[2,4,256,128]{3,2,1,0:T(8,128)(2,1)}, bf16[2,4,256,128]{3,2,1,0:T(8,128)(2,1)S(1)}, u32[]{:S(2)}, u32[]{:S(2)}) %collective-permute-start.18) | collective-permute-done | bytes 524320 | tf_op jit(solution)/shard_map/ppermute | solution.py:62
  186.2 8.1 %out.1 = (bf16[2,4,256,256]{3,2,1,0:T(8,128)(2,1)}, bf16[2,2,256,1024]{3,2,1,0:T(8,128)(2,1)}, bf16[2,2,256,1024]{3,2,1,0:T(8,128)(2,1)}) custom-call(s32[2]{0:T(128)} %pad_add_fusion.place_ref, bf16[2,4,256,128]{3,2,1,0:T(8,128)(2,1)} %get-tuple-element.130.get_own, bf16[2,4,256,128]{3,2,1,0:T(8,128)(2,1)} %copy-done.32, ...), custom_call_target="tpu_custom_call" | custom-call | flops 8999999488 | bytes 9000000 | tf_op jit(solution)/shard_map/out/pallas_call | solution.py:406
  203.3 27.7 %all-gather.11.cloned.1.call-done = bf16[1152,512]{1,0:T(8,128)(2,1)} async-done(((bf16[288,512]{1,0:T(8,128)(2,1)}), bf16[1152,512]{1,0:T(8,128)(2,1)}) %all-gather.11.cloned.1.call-update) | async-done | bytes 1179664 | tf_op jit(solution)/shard_map/all_gather | solution.py:853
  235.6 23.5 %collective-permute-done.22.refs_2_.refs_3_ = bf16[2,256,1024]{2,1,0:T(8,128)(2,1)} collective-permute-done((bf16[2,256,1024]{2,1,0:T(8,128)(2,1)}, bf16[2,256,1024]{2,1,0:T(8,128)(2,1)}, u32[]{:S(2)}, u32[]{:S(2)}) %collective-permute-start.22) | collective-permute-done | bytes 1048608 | tf_op jit(solution)/shard_map/ppermute | solution.py:39
  262.3 25.4 %ffn.2 = (bf16[3,4,256,1152]{3,2,1,0:T(8,128)(2,1)}, bf16[2,2,256,1024]{3,2,1,0:T(8,128)(2,1)}, bf16[2,2,256,1024]{3,2,1,0:T(8,128)(2,1)}, bf16[2,256,1024]{2,1,0:T(8,128)(2,1)}, bf16[2,256,1024]{2,1,0:T(8,128)(2,1)}) custom-call(s32[2]{0:T(128)} %add_multiply_fusion.refs_0_.offset_ref, bf16[2,256,1024]{2,1,0:T(8,128)(2,1)} %multiply_convert_fusion.refs_1_.refs_2_, ...), custom_call_target="tpu_custom_call" | custom-call | flops 22000001024 | bytes 22000000 | tf_op jit(solution)/shard_map/ffn/pallas_call | solution.py:689
  293.0 24.9 %ffn.3 = (bf16[3,4,256,1152]{3,2,1,0:T(8,128)(2,1)}, bf16[2,2,256,1024]{3,2,1,0:T(8,128)(2,1)}, bf16[2,2,256,1024]{3,2,1,0:T(8,128)(2,1)}, bf16[2,256,1024]{2,1,0:T(8,128)(2,1)}, bf16[2,256,1024]{2,1,0:T(8,128)(2,1)}) custom-call(s32[2]{0:T(128)} %add_multiply_fusion.refs_0_.offset_ref, ...), custom_call_target="tpu_custom_call", output_to_operand_aliasing={{1}: (15, {}), {2}: (16, {})} | custom-call | flops 22000001024 | bytes 22000000 | tf_op jit(solution)/shard_map/ffn/pallas_call | solution.py:689
  323.7 10.3 %weight.3 = (bf16[4,288,512]{2,1,0:T(8,128)(2,1)}, bf16[4,288,512]{2,1,0:T(8,128)(2,1)}) custom-call(s32[2]{0:T(128)} %add_multiply_fusion.refs_0_.offset_ref, bf16[3,4,256,1152]{3,2,1,0:T(8,128)(2,1)} %get-tuple-element.140.refs_0_, bf16[3,4,256,1152]{3,2,1,0:T(8,128)(2,1)} %get-tuple-element.149.refs_1_, ...), custom_call_target="tpu_custom_call" | custom-call | flops 10000000000 | bytes 10000000 | tf_op jit(solution)/shard_map/weight/pallas_call | solution.py:734
  336.9 10.1 %weight.4 = (bf16[4,288,512]{2,1,0:T(8,128)(2,1)}, bf16[4,288,512]{2,1,0:T(8,128)(2,1)}) custom-call(s32[2]{0:T(128)} %add_multiply_fusion.refs_0_.offset_ref, bf16[3,4,256,1152]{3,2,1,0:T(8,128)(2,1)} %get-tuple-element.140.refs_0_, bf16[3,4,256,1152]{3,2,1,0:T(8,128)(2,1)} %get-tuple-element.149.refs_1_, ...), custom_call_target="tpu_custom_call" | custom-call | flops 10000000000 | bytes 10000000 | tf_op jit(solution)/shard_map/weight/pallas_call | solution.py:734
  368.5 10.4 %weight.5 = (bf16[4,288,512]{2,1,0:T(8,128)(2,1)}, bf16[4,288,512]{2,1,0:T(8,128)(2,1)}) custom-call(s32[2]{0:T(128)} %add_multiply_fusion.refs_0_.offset_ref, bf16[3,4,256,1152]{3,2,1,0:T(8,128)(2,1)} %get-tuple-element.140.refs_0_, bf16[3,4,256,1152]{3,2,1,0:T(8,128)(2,1)} %get-tuple-element.149.refs_1_, bf16[2,256,1024]{2,1,0:T(8,128)(2,1)} %refs_2_, ...), custom_call_target="tpu_custom_call" | custom-call | flops 10000000000 | bytes 10000000 | tf_op jit(solution)/shard_map/weight/pallas_call | solution.py:734
  385.4 7.1 %collective-permute-done.35 = bf16[4,288,512]{2,1,0:T(8,128)(2,1)S(1)} collective-permute-done((bf16[4,288,512]{2,1,0:T(8,128)(2,1)}, bf16[4,288,512]{2,1,0:T(8,128)(2,1)S(1)}, u32[]{:S(2)}, u32[]{:S(2)}) %collective-permute-start.35) | collective-permute-done | bytes 1179680 | tf_op jit(solution)/shard_map/ppermute | solution.py:82
  405.5 29.2 %attend_back.2 = (bf16[1,4,256,128]{3,2,1,0:T(8,128)(2,1)}, bf16[1,4,256,128]{3,2,1,0:T(8,128)(2,1)}, bf16[1,4,512,128]{3,2,1,0:T(8,128)(2,1)}, bf16[1,4,256,128]{3,2,1,0:T(8,128)(2,1)}, bf16[1,4,256,128]{3,2,1,0:T(8,128)(2,1)}) custom-call(s32[2]{0:T(128)} %pad_add_fusion.place_ref, bf16[2,4,256,128]{3,2,1,0:T(8,128)(2,1)} %get-tuple-element.122.refs_0_, ...), custom_call_target="tpu_custom_call" | custom-call | flops 8000000000 | bytes 8000000 | tf_op jit(solution)/shard_map/attend_back/pallas_call | solution.py:517
  442.8 13.6 %collective-permute-start.45 = (bf16[1,4,256,128]{3,2,1,0:T(8,128)(2,1)}, bf16[1,4,256,128]{3,2,1,0:T(8,128)(2,1)}, u32[]{:S(2)}, u32[]{:S(2)}) collective-permute-start(bf16[1,4,256,128]{3,2,1,0:T(8,128)(2,1)} %get-tuple-element.189), channel_id=1, source_target_pairs={{0,2},{1,3},{2,0},{3,1},{4,6},{5,7},{6,4},{7,5},{8,10},{9,11},{10,... | collective-permute-start | bytes 786440 | tf_op jit(solution)/shard_map/ppermute | solution.py:62
  460.1 29.5 %attend_back.3 = (bf16[1,4,256,128]{3,2,1,0:T(8,128)(2,1)}, bf16[1,4,256,128]{3,2,1,0:T(8,128)(2,1)}, bf16[1,4,512,128]{3,2,1,0:T(8,128)(2,1)}, bf16[1,4,256,128]{3,2,1,0:T(8,128)(2,1)}, bf16[1,4,256,128]{3,2,1,0:T(8,128)(2,1)}) custom-call(s32[2]{0:T(128)} %pad_add_fusion.place_ref, bf16[2,4,256,128]{3,2,1,0:T(8,128)(2,1)} %get-tuple-element.122.refs_0_, ...), custom_call_target="tpu_custom_call" | custom-call | flops 8000000000 | bytes 8000000 | tf_op jit(solution)/shard_map/attend_back/pallas_call | solution.py:517
  492.9 10.2 %collective-permute-start.50 = (bf16[1,4,256,128]{3,2,1,0:T(8,128)(2,1)S(1)}, bf16[1,4,256,128]{3,2,1,0:T(8,128)(2,1)S(1)}, u32[]{:S(2)}, u32[]{:S(2)}) collective-permute-start(bf16[1,4,256,128]{3,2,1,0:T(8,128)(2,1)S(1)} %copy-done.36), channel_id=1, source_target_pairs={{0,2},{1,3},{2,0},{3,1},{4,6},{5,7},{6,4},{7,5},{8,10},{9,11},{10,... | collective-permute-start | bytes 786440 | tf_op jit(solution)/shard_map/ppermute | solution.py:62
  503.1 7.7 %qkv_back.2 = (bf16[1,4,256,512]{3,2,1,0:T(8,128)(2,1)}, bf16[2,1,256,1024]{3,2,1,0:T(8,128)(2,1)}, bf16[2,1,256,1024]{3,2,1,0:T(8,128)(2,1)}, f32[1,384]{1,0:T(1,128)}) custom-call(s32[2]{0:T(128)} %pad_add_fusion.place_ref, bf16[1,4,256,128]{3,2,1,0:T(8,128)(2,1)} %get-tuple-element.176.refs_0_, bf16[1,4,256,128]{3,2,1,0:T(8,128)(2,1)} %get-tuple-element.187.refs_1_, ...), custom_call_target="tpu_custom_call" | custom-call | flops 8000000000 | bytes 8000000 | tf_op jit(solution)/shard_map/qkv_back/pallas_call | solution.py:581
  518.7 7.6 %qkv_back.3 = (bf16[1,4,256,512]{3,2,1,0:T(8,128)(2,1)}, bf16[2,1,256,1024]{3,2,1,0:T(8,128)(2,1)}, bf16[2,1,256,1024]{3,2,1,0:T(8,128)(2,1)}, f32[1,384]{1,0:T(1,128)}) custom-call(s32[2]{0:T(128)} %pad_add_fusion.place_ref, bf16[1,4,256,128]{3,2,1,0:T(8,128)(2,1)} %get-tuple-element.184.refs_0_, bf16[1,4,256,128]{3,2,1,0:T(8,128)(2,1)} %get-tuple-element.195.refs_1_, ...), custom_call_target="tpu_custom_call" | custom-call | flops 8000000000 | bytes 8000000 | tf_op jit(solution)/shard_map/qkv_back/pallas_call | solution.py:581
  546.1 9.4 %collective-permute-done.53 = bf16[1,256,1024]{2,1,0:T(8,128)(2,1)S(1)} collective-permute-done((bf16[1,256,1024]{2,1,0:T(8,128)(2,1)S(1)}, bf16[1,256,1024]{2,1,0:T(8,128)(2,1)S(1)}, u32[]{:S(2)}, u32[]{:S(2)}) %collective-permute-start.53) | collective-permute-done | bytes 524320 | tf_op jit(solution)/shard_map/ppermute | solution.py:963
  (329 shorter events, 227.7 us)
Async XLA Ops:
  19.6 28.8 %collective-permute-start = (bf16[2,256,1024]{2,1,0:T(8,128)(2,1)}, bf16[2,256,1024]{2,1,0:T(8,128)(2,1)}, u32[]{:S(2)}, u32[]{:S(2)}) collective-permute-start(bf16[2,256,1024]{2,1,0:T(8,128)(2,1)} %multiply_convert_fusion.1.refs_0_.refs_2_), channel_id=1, source_target_pairs={{0,8},{8,0},{4,12},{12,4},{1,9},{9,1},{5,13},{13,5},{2,10},{10,2},... | collective-permute-start | bytes 3145736 | tf_op jit(solution)/shard_map/ppermute | solution.py:39
  23.2 33.7 %all-to-all-start = ((bf16[3,4,288,128]{3,2,0,1:T(8,128)(2,1)}), bf16[3,4,288,128]{3,2,0,1:T(8,128)(2,1)S(1)}, u32[]{:S(2)}, u32[]{:S(2)}) async-start(bf16[3,4,288,128]{3,2,0,1:T(8,128)(2,1)} %copy.94), calls=%async_computation | async-start | bytes 1769472 | tf_op jit(solution)/shard_map/all_to_all | solution.py:827
  26.7 60.6 %all-gather.7.cloned.1.call-start = ((), (), s32[]{:S(2)}) async-start(), calls=%async_computation.8 | async-start | bytes 1474560 | tf_op jit(solution)/shard_map/all_gather | solution.py:851
  37.3 33.1 %collective-permute-start.1 = (bf16[2,256,1024]{2,1,0:T(8,128)(2,1)}, bf16[2,256,1024]{2,1,0:T(8,128)(2,1)}, u32[]{:S(2)}, u32[]{:S(2)}) collective-permute-start(bf16[2,256,1024]{2,1,0:T(8,128)(2,1)} %multiply_convert_fusion.1.refs_0_.refs_2_), channel_id=1, source_target_pairs={{0,4},{4,0},{8,12},{12,8},{1,5},{5,1},{9,13},{13,9},{2,6},{6,2},{1... | collective-permute-start | bytes 3145736 | tf_op jit(solution)/shard_map/ppermute | solution.py:40
  57.8 115.8 %all-gather.9.cloned.1.call-start = ((), (), s32[]{:S(2)}) async-start(), calls=%async_computation.9 | async-start | bytes 1474560 | tf_op jit(solution)/shard_map/all_gather | solution.py:853
  87.3 59.7 %collective-permute-start.14 = (bf16[4,288,512]{2,1,0:T(8,128)(2,1)}, bf16[4,288,512]{2,1,0:T(8,128)(2,1)}, u32[]{:S(2)}, u32[]{:S(2)}) collective-permute-start(bf16[4,288,512]{2,1,0:T(8,128)(2,1)} %bitcast.224), channel_id=1, source_target_pairs={{0,16},{16,0},{1,17},{17,1},{2,18},{18,2},{3,19},{19,3},{4,20},{20... | collective-permute-start | bytes 3538952 | tf_op jit(solution)/shard_map/ppermute | solution.py:75
  89.3 47.1 %collective-permute-start.11 = (bf16[2,4,512,128]{3,2,1,0:T(8,128)(2,1)}, bf16[2,4,512,128]{3,2,1,0:T(8,128)(2,1)}, u32[]{:S(2)}, u32[]{:S(2)}) collective-permute-start(bf16[2,4,512,128]{3,2,1,0:T(8,128)(2,1)} %get-tuple-element.116), channel_id=1, source_target_pairs={{0,1},{1,0},{2,3},{3,2},{4,5},{5,4},{6,7},{7,6},{8,9},{9,8},{10,11... | collective-permute-start | bytes 3145736 | tf_op jit(solution)/shard_map/ppermute | solution.py:62
  89.9 57.0 %collective-permute-start.16 = (bf16[2,256,1024]{2,1,0:T(8,128)(2,1)S(1)}, bf16[2,256,1024]{2,1,0:T(8,128)(2,1)}, u32[]{:S(2)}, u32[]{:S(2)}) collective-permute-start(bf16[2,256,1024]{2,1,0:T(8,128)(2,1)S(1)} %copy-done.11), channel_id=1, source_target_pairs={{0,4},{4,0},{8,12},{12,8},{1,5},{5,1},{9,13},{13,9},{2,6},{6,2},{1... | collective-permute-start | bytes 3145736 | tf_op jit(solution)/shard_map/ppermute | solution.py:40
  107.8 39.1 %collective-permute-start.17 = (bf16[2,256,1024]{2,1,0:T(8,128)(2,1)}, bf16[2,256,1024]{2,1,0:T(8,128)(2,1)}, u32[]{:S(2)}, u32[]{:S(2)}) collective-permute-start(bf16[2,256,1024]{2,1,0:T(8,128)(2,1)} %collective-permute-done.15.refs_6_.refs_3_), channel_id=1, source_target_pairs={{0,4},{4,0},{8,12},{12,8},{1,5},{5,1},{9,13},{13,9},{2,6},{6,2},{1... | collective-permute-start | bytes 3145736 | tf_op jit(solution)/shard_map/ppermute | solution.py:41
  136.5 94.4 %all-gather.11.cloned.1.call-start = ((), (), s32[]{:S(2)}) async-start(), calls=%async_computation.10 | async-start | bytes 1474560 | tf_op jit(solution)/shard_map/all_gather | solution.py:853
  195.2 374.8 %reduce-scatter.4.cloned.1.call-start = ((), (), s32[]{:S(2)}) async-start(), calls=%async_computation.5 | async-start | bytes 1474560 | tf_op jit(solution)/shard_map/reduce_scatter | solution.py:919
  195.3 35.7 %collective-permute-start.20 = (bf16[4,288,512]{2,1,0:T(8,128)(2,1)}, bf16[4,288,512]{2,1,0:T(8,128)(2,1)}, u32[]{:S(2)}, u32[]{:S(2)}) collective-permute-start(bf16[4,288,512]{2,1,0:T(8,128)(2,1)} %bitcast.227), channel_id=1, source_target_pairs={{0,16},{16,0},{1,17},{17,1},{2,18},{18,2},{3,19},{19,3},{4,20},{20... | collective-permute-start | bytes 3538952 | tf_op jit(solution)/shard_map/ppermute | solution.py:75
  202.7 28.2 %collective-permute-start.21 = (bf16[2,256,1024]{2,1,0:T(8,128)(2,1)}, bf16[2,256,1024]{2,1,0:T(8,128)(2,1)}, u32[]{:S(2)}, u32[]{:S(2)}) collective-permute-start(bf16[2,256,1024]{2,1,0:T(8,128)(2,1)} %get-tuple-element.292), channel_id=1, source_target_pairs={{0,8},{8,0},{4,12},{12,4},{1,9},{9,1},{5,13},{13,5},{2,10},{10,2},... | collective-permute-start | bytes 3145736 | tf_op jit(solution)/shard_map/ppermute | solution.py:868
  363.9 37.9 %collective-permute-start.34 = (bf16[2,2,256,1024]{3,2,1,0:T(8,128)(2,1)}, bf16[2,2,256,1024]{3,2,1,0:T(8,128)(2,1)}, u32[]{:S(2)}, u32[]{:S(2)}) collective-permute-start(bf16[2,2,256,1024]{3,2,1,0:T(8,128)(2,1)} %get-tuple-element.160), channel_id=1, source_target_pairs={{0,4},{4,0},{8,12},{12,8},{1,5},{5,1},{9,13},{13,9},{2,6},{6,2},{1... | collective-permute-start | bytes 6291464 | tf_op jit(solution)/shard_map/ppermute | solution.py:931
  393.9 176.2 %reduce-scatter.6.cloned.1.call-start = ((), (), s32[]{:S(2)}) async-start(), calls=%async_computation.6 | async-start | bytes 1474560 | tf_op jit(solution)/shard_map/reduce_scatter | solution.py:919
  395.8 43.7 %collective-permute-start.41 = (bf16[4,288,512]{2,1,0:T(8,128)(2,1)}, bf16[4,288,512]{2,1,0:T(8,128)(2,1)S(1)}, u32[]{:S(2)}, u32[]{:S(2)}) collective-permute-start(bf16[4,288,512]{2,1,0:T(8,128)(2,1)} %get-tuple-element.170), channel_id=1, source_target_pairs={{0,16},{16,0},{1,17},{17,1},{2,18},{18,2},{3,19},{19,3},{4,20},{20... | collective-permute-start | bytes 3538952 | tf_op jit(solution)/shard_map/ppermute | solution.py:82
  404.9 51.5 %collective-permute-start.40 = (bf16[2,256,1024]{2,1,0:T(8,128)(2,1)}, bf16[2,256,1024]{2,1,0:T(8,128)(2,1)}, u32[]{:S(2)}, u32[]{:S(2)}) collective-permute-start(bf16[2,256,1024]{2,1,0:T(8,128)(2,1)} %fusion.1), channel_id=1, source_target_pairs={{0,8},{8,0},{4,12},{12,4},{1,9},{9,1},{5,13},{13,5},{2,10},{10,2},... | collective-permute-start | bytes 3145736 | tf_op jit(solution)/shard_map/ppermute | solution.py:933
  440.9 48.8 %collective-permute-start.43 = (bf16[4,288,512]{2,1,0:T(8,128)(2,1)}, bf16[4,288,512]{2,1,0:T(8,128)(2,1)}, u32[]{:S(2)}, u32[]{:S(2)}) collective-permute-start(bf16[4,288,512]{2,1,0:T(8,128)(2,1)} %get-tuple-element.182), channel_id=1, source_target_pairs={{0,16},{16,0},{1,17},{17,1},{2,18},{18,2},{3,19},{19,3},{4,20},{20... | collective-permute-start | bytes 3538952 | tf_op jit(solution)/shard_map/ppermute | solution.py:82
  441.3 61.8 %collective-permute-start.44 = (bf16[1,4,512,128]{3,2,1,0:T(8,128)(2,1)}, bf16[1,4,512,128]{3,2,1,0:T(8,128)(2,1)}, u32[]{:S(2)}, u32[]{:S(2)}) collective-permute-start(bf16[1,4,512,128]{3,2,1,0:T(8,128)(2,1)} %get-tuple-element.188), channel_id=1, source_target_pairs={{0,1},{1,0},{2,3},{3,2},{4,5},{5,4},{6,7},{7,6},{8,9},{9,8},{10,11... | collective-permute-start | bytes 1572872 | tf_op jit(solution)/shard_map/ppermute | solution.py:62
  442.8 50.1 %collective-permute-start.45 = (bf16[1,4,256,128]{3,2,1,0:T(8,128)(2,1)}, bf16[1,4,256,128]{3,2,1,0:T(8,128)(2,1)}, u32[]{:S(2)}, u32[]{:S(2)}) collective-permute-start(bf16[1,4,256,128]{3,2,1,0:T(8,128)(2,1)} %get-tuple-element.189), channel_id=1, source_target_pairs={{0,2},{1,3},{2,0},{3,1},{4,6},{5,7},{6,4},{7,5},{8,10},{9,11},{10,... | collective-permute-start | bytes 786440 | tf_op jit(solution)/shard_map/ppermute | solution.py:62
  456.4 46.7 %collective-permute-start.46 = (bf16[1,4,256,128]{3,2,1,0:T(8,128)(2,1)}, bf16[1,4,256,128]{3,2,1,0:T(8,128)(2,1)}, u32[]{:S(2)}, u32[]{:S(2)}) collective-permute-start(bf16[1,4,256,128]{3,2,1,0:T(8,128)(2,1)} %get-tuple-element.190), channel_id=1, source_target_pairs={{0,3},{1,2},{2,1},{3,0},{4,7},{5,6},{6,5},{7,4},{8,11},{9,10},{10,... | collective-permute-start | bytes 786440 | tf_op jit(solution)/shard_map/ppermute | solution.py:62
  456.4 113.6 %reduce-scatter.8.cloned.1.call-start = ((), (), s32[]{:S(2)}) async-start(), calls=%async_computation.7 | async-start | bytes 1474560 | tf_op jit(solution)/shard_map/reduce_scatter | solution.py:919
  456.5 70.8 %collective-permute-start.55 = (bf16[4,256,128]{2,1,0:T(8,128)(2,1)}, bf16[4,256,128]{2,1,0:T(8,128)(2,1)}, u32[]{:S(2)}, u32[]{:S(2)}) collective-permute-start(bf16[4,256,128]{2,1,0:T(8,128)(2,1)} %get-tuple-element.208), channel_id=1, source_target_pairs={{0,16},{16,0},{1,17},{17,1},{2,18},{18,2},{3,19},{19,3},{4,20},{20... | collective-permute-start | bytes 786440 | tf_op jit(solution)/shard_map/ppermute | solution.py:938
  489.7 28.2 %collective-permute-start.49 = (bf16[1,4,512,128]{3,2,1,0:T(8,128)(2,1)}, bf16[1,4,512,128]{3,2,1,0:T(8,128)(2,1)S(1)}, u32[]{:S(2)}, u32[]{:S(2)}) collective-permute-start(bf16[1,4,512,128]{3,2,1,0:T(8,128)(2,1)} %get-tuple-element.196), channel_id=1, source_target_pairs={{0,1},{1,0},{2,3},{3,2},{4,5},{5,4},{6,7},{7,6},{8,9},{9,8},{10,11... | collective-permute-start | bytes 1572872 | tf_op jit(solution)/shard_map/ppermute | solution.py:62
  (90 other events, 1258.6 us)
Sparse Core Ops, SparseCore 0:
  58.0 29.2 all-gather.6
  136.6 30.1 all-gather.8
  195.3 35.5 all-gather.10
  394.0 31.5 reduce-scatter.3
  456.5 37.4 reduce-scatter.5
  528.5 31.2 reduce-scatter.7

commit v4 on v3

--- a/solution.py
+++ b/solution.py
@@ -605,10 +605,10 @@
 
 def ffn_kernel(at, halves, *refs):
     offset_ref, x_refs, given_refs, pieces = refs[0], refs[1:5], refs[5:9], refs[9 : 9 + 3 * halves]
-    refs = refs[-18:]
+    refs = refs[-16:]
     act_out, outs = refs[0], refs[1:5]
-    w_ref, x_ref, given_ref, act_ref, held = *refs[5:9], refs[9:13]
-    sems, x_sems, given_sems, act_sems, out_sems = refs[13:]
+    w_ref, x_ref, given_ref, act_ref, held = *refs[5:9], refs[9:11]
+    sems, x_sems, given_sems, act_sems, out_sems = refs[11:]
     _, rows, width = x_ref.shape
     count = 2 * rows
     blocks, depth, span = pieces[0].shape
@@ -636,44 +636,70 @@
     givens = slot_copies([ref.at[at] for ref in given_refs], given_ref, given_sems)
     for found in (tokens[:2], copies(0), copies(1), copies(2), givens[:2], tokens[2:], givens[2:]):
         start(found)
-    leaving = []
-
-    def leave(source, target, sem):
-        leaving.append(pltpu.make_async_copy(source, target, sem))
-        leaving[-1].start()
+
+    def act_copy(kind, k):
+        rows_of = pl.ds(2 * k, 2)
+        return pltpu.make_async_copy(act_ref.at[kind, rows_of], act_out.at[kind, rows_of], act_sems.at[kind, k])
+
+    def part_copy(n, k):
+        out = outs[k].at[:, at] if n == 0 else outs[2 + k]
+        return pltpu.make_async_copy(held[n].at[k], out, out_sems.at[n, k])
 
     def leave_act(kind, k, value):
-        act_ref[kind, 2 * k : 2 * k + 2] = value.reshape(2, rows, -1)
-        leave(act_ref.at[kind, pl.ds(2 * k, 2)], act_out.at[kind, pl.ds(2 * k, 2)], act_sems.at[kind, k])
-
-    def leave_part(n, value):
-        held[n][...] = value.astype(BF16).reshape(2, rows, width)
-        leave(held[n], outs[n].at[:, at] if n < 2 else outs[n], out_sems.at[n])
-
-    for k in range(2):
-        wait(tokens[2 * k : 2 * k + 2])
-        x = x_ref[2 * k : 2 * k + 2].reshape(count, width)
-        if k == 0:
-            wait(copies(0))
+        act_ref[kind, pl.ds(2 * k, 2)] = value.reshape(2, rows, -1)
+        act_copy(kind, k).start()
+
+    def leave_part(n, k, value):
+        held[n][k] = value.astype(BF16).reshape(2, rows, width)
+        for turn in range(2):
+
+            @pl.when(k == turn)
+            def _():
+                part_copy(n, turn).start()
+
+    def arrive(k, found):
+        @pl.when(k == 0)
+        def _():
+            wait(found)
+
+    def step(k, carry):
+        for turn in range(2):
+
+            @pl.when(k == turn)
+            def _():
+                wait(tokens[2 * turn : 2 * turn + 2])
+
+        x = x_ref[pl.ds(2 * k, 2)].reshape(count, width)
+        arrive(k, copies(0))
         gate = dot_nt(x, w_ref[0])
-        if k == 0:
-            wait(copies(1))
+        arrive(k, copies(1))
         up = dot_nt(x, w_ref[1])
         sig = jax.nn.sigmoid(gate)
         swish = gate * sig
         hidden = (swish * up).astype(BF16)
         leave_act(2, k, hidden)
-        if k == 0:
-            wait(copies(2))
-        wait(givens[2 * k : 2 * k + 2])
-        hidden_back = dot_nt(given_ref[2 * k : 2 * k + 2].reshape(count, width), w_ref[2])
+        arrive(k, copies(2))
+        for turn in range(2):
+
+            @pl.when(k == turn)
+            def _():
+                wait(givens[2 * turn : 2 * turn + 2])
+
+        hidden_back = dot_nt(given_ref[pl.ds(2 * k, 2)].reshape(count, width), w_ref[2])
         gate_back = (hidden_back * up * (sig * (1.0 + gate * (1.0 - sig)))).astype(BF16)
         leave_act(0, k, gate_back)
         up_back = (hidden_back * swish).astype(BF16)
         leave_act(1, k, up_back)
-        leave_part(2 + k, dot_nn(gate_back, w_ref[0]) + dot_nn(up_back, w_ref[1]))
-        leave_part(k, dot_nn(hidden, w_ref[2]))
-    wait(leaving)
+        leave_part(1, k, dot_nn(gate_back, w_ref[0]) + dot_nn(up_back, w_ref[1]))
+        leave_part(0, k, dot_nn(hidden, w_ref[2]))
+        return carry
+
+    lax.fori_loop(0, 2, step, 0)
+    for k in range(2):
+        for kind in range(3):
+            act_copy(kind, k).wait()
+        for n in range(2):
+            part_copy(n, k).wait()
 
 
 def ffn_call(offsets, at, xs, given, pieces, before):
@@ -698,13 +724,13 @@
             pltpu.VMEM((4, rows, width), BF16),
             pltpu.VMEM(act, BF16),
         ]
-        + [pltpu.VMEM(part, BF16)] * 4
+        + [pltpu.VMEM((2, *part), BF16)] * 2
         + [
             pltpu.SemaphoreType.DMA((3, halves, blocks)),
             pltpu.SemaphoreType.DMA((4,)),
             pltpu.SemaphoreType.DMA((4,)),
             pltpu.SemaphoreType.DMA((3, 2)),
-            pltpu.SemaphoreType.DMA((4,)),
+            pltpu.SemaphoreType.DMA((2, 2)),
         ],
         compiler_params=params(),
         cost_estimate=cost(22),
@@ -948,7 +974,7 @@
         gradient = back_rows[s] + norm_back(x[s], root[s], first_gain, first_back)
         return jnp.sum(first_back * x[s] * root[s], axis=0), gradient
 
-    backs, firsts, head_share, first_share, gradients = [], [], 0.0, 0.0, []
+    backs, firsts, head_share, gradients = [], [], 0.0, []
     for s in pair:
         back, own, other, share = line.run(qkv_back_call, place, s, got[s], raw, cosine, sine, gains, w_attn)
         backs.append(back)
@@ -961,13 +987,12 @@
     moved = lax.ppermute(parts[1], "shard", [(0, 1), (1, 0)]) if near else None
     mine, away = line.run(lambda got, own: add_near(own, got), other, own)
     firsts.append((lax.ppermute(away, "ctx", FAR), mine))
-    for s in pair:
+    def finish(s):
         share, gradient = line.run(lambda a, b: last(a, b, s), *firsts[s])
-        first_share = first_share + share
         gradients.append(gradient)
-    shares = jnp.concatenate([first_share, second_share, head_share[0]])
-    shares = sum_all(shares, [(name, sizes[name]) for name in ("ctx", "shard", "tp")])
-
+        return share
+
+    first_share = finish(0)
     if near:
         both = lambda a, b: (a.astype(F32) + b.astype(F32)).astype(BF16)
         g_attn = line.run(
@@ -978,6 +1003,10 @@
         g_attn = jnp.concatenate([parts[0][0], out_parts[0][0]])
         g_attn = g_attn.reshape(-1, count, width // count).transpose(1, 0, 2)
         g_attn = lax.psum_scatter(g_attn, groups, scatter_dimension=0, tiled=False)
+    first_share = first_share + finish(1)
+    shares = jnp.concatenate([first_share, second_share, head_share[0]])
+    shares = sum_all(shares, [(name, sizes[name]) for name in ("ctx", "shard", "tp")])
+
     def settle(g):
         g = g.reshape(3, units, depth).astype(F32)
         return g[0].T, g[1].T, g[2]

time: 621 us -> 622 us (level)
  starting transfers between devices: 97.3 us -> 89.4 us
    all_gather x2, starting transfers between devices: 10.5 us -> 0.3 us  [per_device(): lax.all_gather(after(large[j], *heads), 'tp', axis=0, tiled=False)]
    ppermute x3, waiting for transfers between devices: 7.11 us -> 0.01 us  [send_shard(): return lax.ppermute(parts[1], 'shard', [(0, 1), (1, 0)])]
    unnamed x95 -> x97, local copies, waits for them, and re-layouts: 14.1 us -> 13.9 us
  transfers between devices with their start and end apart: 73 -> 73, of which waited for: 27 -> 25; matrix products, arithmetic and copies ran while one was open for 11% -> 11% of each run, Pallas kernels for 31% -> 31%
where the time goes in v4:
time: 622 us; the launch traced here: 612 us
  Pallas kernels  223 us (36%)
  waiting for transfers between devices  198 us (32%)
  starting transfers between devices  89.4 us (14%)
  other arithmetic  64.4 us (10%)
  local copies, waits for them, and re-layouts  22 us (4%)
  between operations  15.1 us (2%)
    pallas_call x2, Pallas kernels, attend_back_call(): pl.pallas_call(attend_back_kernel, grid=(4,), in_specs=[pl.BlockSpec(memo...  58.8 us
    ppermute x15, waiting for transfers between devices, to_tp(): return lax.ppermute(value, 'tp', [(i, i ^ e) for i in range(4)])  57.1 us
    pallas_call x2, Pallas kernels, ffn_call(): pl.pallas_call(functools.partial(ffn_kernel, at, halves), in_specs=[pl.Bl...  50.3 us
    ppermute x6, waiting for transfers between devices, gather_ctx(): far = lax.ppermute(own, 'ctx', FAR)  47.4 us
    ppermute x15, starting transfers between devices, to_tp(): return lax.ppermute(value, 'tp', [(i, i ^ e) for i in range(4)])  43.8 us
    pallas_call x3, Pallas kernels, weight_call(): pl.pallas_call(functools.partial(weight_kernel, halves), grid=(1,), in_sp...  30.6 us
    all_gather x2, waiting for transfers between devices, per_device(): lax.all_gather(after(large[j], *heads), 'tp', axis=0, tiled=False)  28.9 us
    pallas_call x1, Pallas kernels, attend_call(): pl.pallas_call(attend_kernel, grid=(pair, 4), in_specs=[pl.BlockSpec(memo...  26 us
  transfers between devices with their start and end apart: 73, of which 25 were waited for; matrix products, arithmetic and copies ran while one was open for 11% of the time, Pallas kernels for 31%

profile of v4, /device:TPU:6, one launch (start us, length us, event | category | flops | bytes accessed | tf_op | source)
XLA Modules:
  0.0 612.0 jit_solution(1852777864385263603)
XLA Ops:
  37.3 10.0 %collective-permute-done.5 = bf16[128,768]{0,1:T(8,128)(2,1)S(1)} collective-permute-done((bf16[128,768]{0,1:T(8,128)(2,1)S(1)}, bf16[128,768]{0,1:T(8,128)(2,1)S(1)}, u32[]{:S(2)}, u32[]{:S(2)}) %collective-permute-start.5) | collective-permute-done | bytes 196640 | tf_op jit(solution)/shard_map/ppermute | solution.py:109
  57.9 10.0 %collective-permute-done.7 = bf16[512,768]{1,0:T(8,128)(2,1)} collective-permute-done((bf16[512,768]{1,0:T(8,128)(2,1)S(1)}, bf16[512,768]{1,0:T(8,128)(2,1)}, u32[]{:S(2)}, u32[]{:S(2)}) %collective-permute-start.7) | collective-permute-done | bytes 786464 | tf_op jit(solution)/shard_map/ppermute | solution.py:122
  70.4 12.5 %qkv.1 = (bf16[2,4,256,128]{3,2,1,0:T(8,128)(2,1)}, bf16[2,4,256,128]{3,2,1,0:T(8,128)(2,1)}, bf16[2,4,512,128]{3,2,1,0:T(8,128)(2,1)}, bf16[2,4,256,128]{3,2,1,0:T(8,128)(2,1)}, f32[2,4,256,384]{3,2,1,0:T(8,128)}) custom-call(s32[2]{0:T(128)} %pad_add_fusion.place_ref, bf16[2,256,1024]{2,1,0:T(8,128)(2,1)} %multiply_convert_fusion.1.refs_0_.refs_2_, ...), custom_call_target="tpu_custom_call" | custom-call | flops 15000000512 | bytes 15000000 | tf_op jit(solution)/shard_map/qkv/pallas_call | solution.py:241
  89.9 18.0 %collective-permute-done.15.refs_6_.refs_3_ = bf16[2,256,1024]{2,1,0:T(8,128)(2,1)} collective-permute-done((bf16[2,256,1024]{2,1,0:T(8,128)(2,1)S(1)}, bf16[2,256,1024]{2,1,0:T(8,128)(2,1)}, u32[]{:S(2)}, u32[]{:S(2)}) %collective-permute-start.15) | collective-permute-done | bytes 1048608 | tf_op jit(solution)/shard_map/ppermute | solution.py:39
  116.2 20.2 %collective-permute-done.13.refs_4_ = bf16[2,4,256,128]{3,2,1,0:T(8,128)(2,1)} collective-permute-done((bf16[2,4,256,128]{3,2,1,0:T(8,128)(2,1)}, bf16[2,4,256,128]{3,2,1,0:T(8,128)(2,1)}, u32[]{:S(2)}, u32[]{:S(2)}) %collective-permute-start.13) | collective-permute-done | bytes 524320 | tf_op jit(solution)/shard_map/ppermute | solution.py:62
  136.8 26.0 %attend.1 = (bf16[2,4,256,128]{3,2,1,0:T(8,128)(2,1)}, bf16[2,4,256,128]{3,2,1,0:T(8,128)(2,1)}, f32[2,4,64,1024]{3,2,1,0:T(8,128)}, f32[2,4,1,1024]{3,2,1,0:T(1,128)}) custom-call(s32[2]{0:T(128)} %pad_add_fusion.place_ref, bf16[2,4,256,128]{3,2,1,0:T(8,128)(2,1)} %get-tuple-element.122.refs_0_, bf16[2,4,256,128]{3,2,1,0:T(8,128)(2,1)} %get-tuple-element.123.refs_1_, ...), custom_call_target="tpu_custom_call" | custom-call | flops 32000000000 | bytes 32000000 | tf_op jit(solution)/shard_map/attend/pallas_call | solution.py:353
  166.4 10.4 %collective-permute-done.18.get_other = bf16[2,4,256,128]{3,2,1,0:T(8,128)(2,1)S(1)} collective-permute-done((bf16[2,4,256,128]{3,2,1,0:T(8,128)(2,1)}, bf16[2,4,256,128]{3,2,1,0:T(8,128)(2,1)S(1)}, u32[]{:S(2)}, u32[]{:S(2)}) %collective-permute-start.18) | collective-permute-done | bytes 524320 | tf_op jit(solution)/shard_map/ppermute | solution.py:62
  177.7 8.1 %out.1 = (bf16[2,4,256,256]{3,2,1,0:T(8,128)(2,1)}, bf16[2,2,256,1024]{3,2,1,0:T(8,128)(2,1)}, bf16[2,2,256,1024]{3,2,1,0:T(8,128)(2,1)}) custom-call(s32[2]{0:T(128)} %pad_add_fusion.place_ref, bf16[2,4,256,128]{3,2,1,0:T(8,128)(2,1)} %get-tuple-element.130.get_own, bf16[2,4,256,128]{3,2,1,0:T(8,128)(2,1)} %copy-done.32, ...), custom_call_target="tpu_custom_call" | custom-call | flops 8999999488 | bytes 9000000 | tf_op jit(solution)/shard_map/out/pallas_call | solution.py:406
  194.8 26.0 %all-gather.11.cloned.1.call-done = bf16[1152,512]{1,0:T(8,128)(2,1)} async-done(((bf16[288,512]{1,0:T(8,128)(2,1)}), bf16[1152,512]{1,0:T(8,128)(2,1)}) %all-gather.11.cloned.1.call-update) | async-done | bytes 1179664 | tf_op jit(solution)/shard_map/all_gather | solution.py:879
  225.5 23.5 %collective-permute-done.22.refs_2_.refs_3_ = bf16[2,256,1024]{2,1,0:T(8,128)(2,1)} collective-permute-done((bf16[2,256,1024]{2,1,0:T(8,128)(2,1)}, bf16[2,256,1024]{2,1,0:T(8,128)(2,1)}, u32[]{:S(2)}, u32[]{:S(2)}) %collective-permute-start.22) | collective-permute-done | bytes 1048608 | tf_op jit(solution)/shard_map/ppermute | solution.py:39
  252.1 25.3 %ffn.2 = (bf16[3,4,256,1152]{3,2,1,0:T(8,128)(2,1)}, bf16[2,2,256,1024]{3,2,1,0:T(8,128)(2,1)}, bf16[2,2,256,1024]{3,2,1,0:T(8,128)(2,1)}, bf16[2,256,1024]{2,1,0:T(8,128)(2,1)}, bf16[2,256,1024]{2,1,0:T(8,128)(2,1)}) custom-call(s32[2]{0:T(128)} %add_multiply_fusion.refs_0_.offset_ref, bf16[2,256,1024]{2,1,0:T(8,128)(2,1)} %multiply_convert_fusion.refs_1_.refs_2_, ...), custom_call_target="tpu_custom_call" | custom-call | flops 22000001024 | bytes 22000000 | tf_op jit(solution)/shard_map/ffn/pallas_call | solution.py:715
  282.7 25.0 %ffn.3 = (bf16[3,4,256,1152]{3,2,1,0:T(8,128)(2,1)}, bf16[2,2,256,1024]{3,2,1,0:T(8,128)(2,1)}, bf16[2,2,256,1024]{3,2,1,0:T(8,128)(2,1)}, bf16[2,256,1024]{2,1,0:T(8,128)(2,1)}, bf16[2,256,1024]{2,1,0:T(8,128)(2,1)}) custom-call(s32[2]{0:T(128)} %add_multiply_fusion.refs_0_.offset_ref, ...), custom_call_target="tpu_custom_call", output_to_operand_aliasing={{1}: (15, {}), {2}: (16, {})} | custom-call | flops 22000001024 | bytes 22000000 | tf_op jit(solution)/shard_map/ffn/pallas_call | solution.py:715
  313.5 10.1 %weight.3 = (bf16[4,288,512]{2,1,0:T(8,128)(2,1)}, bf16[4,288,512]{2,1,0:T(8,128)(2,1)}) custom-call(s32[2]{0:T(128)} %add_multiply_fusion.refs_0_.offset_ref, bf16[3,4,256,1152]{3,2,1,0:T(8,128)(2,1)} %get-tuple-element.140.refs_0_, bf16[3,4,256,1152]{3,2,1,0:T(8,128)(2,1)} %get-tuple-element.149.refs_1_, ...), custom_call_target="tpu_custom_call" | custom-call | flops 10000000000 | bytes 10000000 | tf_op jit(solution)/shard_map/weight/pallas_call | solution.py:760
  326.7 10.1 %weight.4 = (bf16[4,288,512]{2,1,0:T(8,128)(2,1)}, bf16[4,288,512]{2,1,0:T(8,128)(2,1)}) custom-call(s32[2]{0:T(128)} %add_multiply_fusion.refs_0_.offset_ref, bf16[3,4,256,1152]{3,2,1,0:T(8,128)(2,1)} %get-tuple-element.140.refs_0_, bf16[3,4,256,1152]{3,2,1,0:T(8,128)(2,1)} %get-tuple-element.149.refs_1_, ...), custom_call_target="tpu_custom_call" | custom-call | flops 10000000000 | bytes 10000000 | tf_op jit(solution)/shard_map/weight/pallas_call | solution.py:760
  358.8 10.4 %weight.5 = (bf16[4,288,512]{2,1,0:T(8,128)(2,1)}, bf16[4,288,512]{2,1,0:T(8,128)(2,1)}) custom-call(s32[2]{0:T(128)} %add_multiply_fusion.refs_0_.offset_ref, bf16[3,4,256,1152]{3,2,1,0:T(8,128)(2,1)} %get-tuple-element.140.refs_0_, bf16[3,4,256,1152]{3,2,1,0:T(8,128)(2,1)} %get-tuple-element.149.refs_1_, bf16[2,256,1024]{2,1,0:T(8,128)(2,1)} %refs_2_, ...), custom_call_target="tpu_custom_call" | custom-call | flops 10000000000 | bytes 10000000 | tf_op jit(solution)/shard_map/weight/pallas_call | solution.py:760
  390.5 29.3 %attend_back.2 = (bf16[1,4,256,128]{3,2,1,0:T(8,128)(2,1)}, bf16[1,4,256,128]{3,2,1,0:T(8,128)(2,1)}, bf16[1,4,512,128]{3,2,1,0:T(8,128)(2,1)}, bf16[1,4,256,128]{3,2,1,0:T(8,128)(2,1)}, bf16[1,4,256,128]{3,2,1,0:T(8,128)(2,1)}) custom-call(s32[2]{0:T(128)} %pad_add_fusion.place_ref, bf16[2,4,256,128]{3,2,1,0:T(8,128)(2,1)} %get-tuple-element.122.refs_0_, ...), custom_call_target="tpu_custom_call" | custom-call | flops 8000000000 | bytes 8000000 | tf_op jit(solution)/shard_map/attend_back/pallas_call | solution.py:517
  428.3 18.9 %collective-permute-start.45 = (bf16[1,4,256,128]{3,2,1,0:T(8,128)(2,1)}, bf16[1,4,256,128]{3,2,1,0:T(8,128)(2,1)}, u32[]{:S(2)}, u32[]{:S(2)}) collective-permute-start(bf16[1,4,256,128]{3,2,1,0:T(8,128)(2,1)} %get-tuple-element.189), channel_id=1, source_target_pairs={{0,2},{1,3},{2,0},{3,1},{4,6},{5,7},{6,4},{7,5},{8,10},{9,11},{10,... | collective-permute-start | bytes 786440 | tf_op jit(solution)/shard_map/ppermute | solution.py:62
  450.9 29.5 %attend_back.3 = (bf16[1,4,256,128]{3,2,1,0:T(8,128)(2,1)}, bf16[1,4,256,128]{3,2,1,0:T(8,128)(2,1)}, bf16[1,4,512,128]{3,2,1,0:T(8,128)(2,1)}, bf16[1,4,256,128]{3,2,1,0:T(8,128)(2,1)}, bf16[1,4,256,128]{3,2,1,0:T(8,128)(2,1)}) custom-call(s32[2]{0:T(128)} %pad_add_fusion.place_ref, bf16[2,4,256,128]{3,2,1,0:T(8,128)(2,1)} %get-tuple-element.122.refs_0_, ...), custom_call_target="tpu_custom_call" | custom-call | flops 8000000000 | bytes 8000000 | tf_op jit(solution)/shard_map/attend_back/pallas_call | solution.py:517
  481.0 10.2 %collective-permute-start.50 = (bf16[1,4,256,128]{3,2,1,0:T(8,128)(2,1)}, bf16[1,4,256,128]{3,2,1,0:T(8,128)(2,1)S(1)}, u32[]{:S(2)}, u32[]{:S(2)}) collective-permute-start(bf16[1,4,256,128]{3,2,1,0:T(8,128)(2,1)} %get-tuple-element.197), channel_id=1, source_target_pairs={{0,2},{1,3},{2,0},{3,1},{4,6},{5,7},{6,4},{7,5},{8,10},{9,11},{10,... | collective-permute-start | bytes 786440 | tf_op jit(solution)/shard_map/ppermute | solution.py:62
  501.6 7.9 %collective-permute-done.51.refs_4_ = bf16[1,4,256,128]{3,2,1,0:T(8,128)(2,1)S(1)} collective-permute-done((bf16[1,4,256,128]{3,2,1,0:T(8,128)(2,1)S(1)}, bf16[1,4,256,128]{3,2,1,0:T(8,128)(2,1)S(1)}, u32[]{:S(2)}, u32[]{:S(2)}) %collective-permute-start.51) | collective-permute-done | bytes 262176 | tf_op jit(solution)/shard_map/ppermute | solution.py:62
  510.4 7.7 %qkv_back.3 = (bf16[1,4,256,512]{3,2,1,0:T(8,128)(2,1)}, bf16[2,1,256,1024]{3,2,1,0:T(8,128)(2,1)}, bf16[2,1,256,1024]{3,2,1,0:T(8,128)(2,1)}, f32[1,384]{1,0:T(1,128)}) custom-call(s32[2]{0:T(128)} %pad_add_fusion.place_ref, bf16[1,4,256,128]{3,2,1,0:T(8,128)(2,1)} %get-tuple-element.184.refs_0_, bf16[1,4,256,128]{3,2,1,0:T(8,128)(2,1)} %get-tuple-element.195.refs_1_, ...), custom_call_target="tpu_custom_call" | custom-call | flops 8000000000 | bytes 8000000 | tf_op jit(solution)/shard_map/qkv_back/pallas_call | solution.py:581
  533.1 9.0 %collective-permute-done.48 = bf16[1,256,1024]{2,1,0:T(8,128)(2,1)S(1)} collective-permute-done((bf16[1,256,1024]{2,1,0:T(8,128)(2,1)S(1)}, bf16[1,256,1024]{2,1,0:T(8,128)(2,1)S(1)}, u32[]{:S(2)}, u32[]{:S(2)}) %collective-permute-start.48) | collective-permute-done | bytes 524320 | tf_op jit(solution)/shard_map/ppermute | solution.py:985
  542.0 10.0 %collective-permute-done.53 = bf16[1,256,1024]{2,1,0:T(8,128)(2,1)S(1)} collective-permute-done((bf16[1,256,1024]{2,1,0:T(8,128)(2,1)S(1)}, bf16[1,256,1024]{2,1,0:T(8,128)(2,1)S(1)}, u32[]{:S(2)}, u32[]{:S(2)}) %collective-permute-start.53) | collective-permute-done | bytes 524320 | tf_op jit(solution)/shard_map/ppermute | solution.py:989
  593.8 8.2 %collective-permute-done.59 = bf16[768,128]{1,0:T(8,128)(2,1)S(1)} collective-permute-done((bf16[768,128]{1,0:T(8,128)(2,1)S(1)}, bf16[768,128]{1,0:T(8,128)(2,1)S(1)}, u32[]{:S(2)}, u32[]{:S(2)}) %collective-permute-start.59) | collective-permute-done | bytes 196640 | tf_op jit(solution)/shard_map/ppermute | solution.py:1020
  (329 shorter events, 220.8 us)
Async XLA Ops:
  19.6 28.8 %collective-permute-start = (bf16[2,256,1024]{2,1,0:T(8,128)(2,1)}, bf16[2,256,1024]{2,1,0:T(8,128)(2,1)}, u32[]{:S(2)}, u32[]{:S(2)}) collective-permute-start(bf16[2,256,1024]{2,1,0:T(8,128)(2,1)} %multiply_convert_fusion.1.refs_0_.refs_2_), channel_id=1, source_target_pairs={{0,8},{8,0},{4,12},{12,4},{1,9},{9,1},{5,13},{13,5},{2,10},{10,2},... | collective-permute-start | bytes 3145736 | tf_op jit(solution)/shard_map/ppermute | solution.py:39
  23.1 33.7 %all-to-all-start = ((bf16[3,4,288,128]{3,2,0,1:T(8,128)(2,1)}), bf16[3,4,288,128]{3,2,0,1:T(8,128)(2,1)S(1)}, u32[]{:S(2)}, u32[]{:S(2)}) async-start(bf16[3,4,288,128]{3,2,0,1:T(8,128)(2,1)} %copy.94), calls=%async_computation | async-start | bytes 1769472 | tf_op jit(solution)/shard_map/all_to_all | solution.py:853
  26.7 60.6 %all-gather.7.cloned.1.call-start = ((), (), s32[]{:S(2)}) async-start(), calls=%async_computation.8 | async-start | bytes 1474560 | tf_op jit(solution)/shard_map/all_gather | solution.py:877
  37.3 33.1 %collective-permute-start.1 = (bf16[2,256,1024]{2,1,0:T(8,128)(2,1)}, bf16[2,256,1024]{2,1,0:T(8,128)(2,1)}, u32[]{:S(2)}, u32[]{:S(2)}) collective-permute-start(bf16[2,256,1024]{2,1,0:T(8,128)(2,1)} %multiply_convert_fusion.1.refs_0_.refs_2_), channel_id=1, source_target_pairs={{0,4},{4,0},{8,12},{12,8},{1,5},{5,1},{9,13},{13,9},{2,6},{6,2},{1... | collective-permute-start | bytes 3145736 | tf_op jit(solution)/shard_map/ppermute | solution.py:40
  57.8 108.6 %all-gather.9.cloned.1.call-start = ((), (), s32[]{:S(2)}) async-start(), calls=%async_computation.9 | async-start | bytes 1474560 | tf_op jit(solution)/shard_map/all_gather | solution.py:879
  87.2 49.5 %collective-permute-start.14 = (bf16[4,288,512]{2,1,0:T(8,128)(2,1)}, bf16[4,288,512]{2,1,0:T(8,128)(2,1)}, u32[]{:S(2)}, u32[]{:S(2)}) collective-permute-start(bf16[4,288,512]{2,1,0:T(8,128)(2,1)} %bitcast.224), channel_id=1, source_target_pairs={{0,16},{16,0},{1,17},{17,1},{2,18},{18,2},{3,19},{19,3},{4,20},{20... | collective-permute-start | bytes 3538952 | tf_op jit(solution)/shard_map/ppermute | solution.py:75
  89.3 47.1 %collective-permute-start.11 = (bf16[2,4,512,128]{3,2,1,0:T(8,128)(2,1)}, bf16[2,4,512,128]{3,2,1,0:T(8,128)(2,1)}, u32[]{:S(2)}, u32[]{:S(2)}) collective-permute-start(bf16[2,4,512,128]{3,2,1,0:T(8,128)(2,1)} %get-tuple-element.116), channel_id=1, source_target_pairs={{0,1},{1,0},{2,3},{3,2},{4,5},{5,4},{6,7},{7,6},{8,9},{9,8},{10,11... | collective-permute-start | bytes 3145736 | tf_op jit(solution)/shard_map/ppermute | solution.py:62
  89.9 46.9 %collective-permute-start.16 = (bf16[2,256,1024]{2,1,0:T(8,128)(2,1)S(1)}, bf16[2,256,1024]{2,1,0:T(8,128)(2,1)}, u32[]{:S(2)}, u32[]{:S(2)}) collective-permute-start(bf16[2,256,1024]{2,1,0:T(8,128)(2,1)S(1)} %copy-done.10), channel_id=1, source_target_pairs={{0,4},{4,0},{8,12},{12,8},{1,5},{5,1},{9,13},{13,9},{2,6},{6,2},{1... | collective-permute-start | bytes 3145736 | tf_op jit(solution)/shard_map/ppermute | solution.py:40
  107.9 28.9 %collective-permute-start.17 = (bf16[2,256,1024]{2,1,0:T(8,128)(2,1)}, bf16[2,256,1024]{2,1,0:T(8,128)(2,1)}, u32[]{:S(2)}, u32[]{:S(2)}) collective-permute-start(bf16[2,256,1024]{2,1,0:T(8,128)(2,1)} %collective-permute-done.15.refs_6_.refs_3_), channel_id=1, source_target_pairs={{0,4},{4,0},{8,12},{12,8},{1,5},{5,1},{9,13},{13,9},{2,6},{6,2},{1... | collective-permute-start | bytes 3145736 | tf_op jit(solution)/shard_map/ppermute | solution.py:41
  136.5 84.3 %all-gather.11.cloned.1.call-start = ((), (), s32[]{:S(2)}) async-start(), calls=%async_computation.10 | async-start | bytes 1474560 | tf_op jit(solution)/shard_map/all_gather | solution.py:879
  186.7 379.1 %reduce-scatter.4.cloned.1.call-start = ((), (), s32[]{:S(2)}) async-start(), calls=%async_computation.5 | async-start | bytes 1474560 | tf_op jit(solution)/shard_map/reduce_scatter | solution.py:945
  186.7 34.0 %collective-permute-start.20 = (bf16[4,288,512]{2,1,0:T(8,128)(2,1)}, bf16[4,288,512]{2,1,0:T(8,128)(2,1)}, u32[]{:S(2)}, u32[]{:S(2)}) collective-permute-start(bf16[4,288,512]{2,1,0:T(8,128)(2,1)} %bitcast.227), channel_id=1, source_target_pairs={{0,16},{16,0},{1,17},{17,1},{2,18},{18,2},{3,19},{19,3},{4,20},{20... | collective-permute-start | bytes 3538952 | tf_op jit(solution)/shard_map/ppermute | solution.py:75
  347.1 28.6 %collective-permute-start.35 = (bf16[4,288,512]{2,1,0:T(8,128)(2,1)}, bf16[4,288,512]{2,1,0:T(8,128)(2,1)S(1)}, u32[]{:S(2)}, u32[]{:S(2)}) collective-permute-start(bf16[4,288,512]{2,1,0:T(8,128)(2,1)} %get-tuple-element.161), channel_id=1, source_target_pairs={{0,16},{16,0},{1,17},{17,1},{2,18},{18,2},{3,19},{19,3},{4,20},{20... | collective-permute-start | bytes 3538952 | tf_op jit(solution)/shard_map/ppermute | solution.py:82
  354.2 31.8 %collective-permute-start.34 = (bf16[2,2,256,1024]{3,2,1,0:T(8,128)(2,1)}, bf16[2,2,256,1024]{3,2,1,0:T(8,128)(2,1)}, u32[]{:S(2)}, u32[]{:S(2)}) collective-permute-start(bf16[2,2,256,1024]{3,2,1,0:T(8,128)(2,1)} %get-tuple-element.160), channel_id=1, source_target_pairs={{0,4},{4,0},{8,12},{12,8},{1,5},{5,1},{9,13},{13,9},{2,6},{6,2},{1... | collective-permute-start | bytes 6291464 | tf_op jit(solution)/shard_map/ppermute | solution.py:957
  377.1 188.7 %reduce-scatter.6.cloned.1.call-start = ((), (), s32[]{:S(2)}) async-start(), calls=%async_computation.6 | async-start | bytes 1474560 | tf_op jit(solution)/shard_map/reduce_scatter | solution.py:945
  378.6 45.9 %collective-permute-start.41 = (bf16[4,288,512]{2,1,0:T(8,128)(2,1)}, bf16[4,288,512]{2,1,0:T(8,128)(2,1)S(1)}, u32[]{:S(2)}, u32[]{:S(2)}) collective-permute-start(bf16[4,288,512]{2,1,0:T(8,128)(2,1)} %get-tuple-element.170), channel_id=1, source_target_pairs={{0,16},{16,0},{1,17},{17,1},{2,18},{18,2},{3,19},{19,3},{4,20},{20... | collective-permute-start | bytes 3538952 | tf_op jit(solution)/shard_map/ppermute | solution.py:82
  389.0 58.3 %collective-permute-start.40 = (bf16[2,256,1024]{2,1,0:T(8,128)(2,1)}, bf16[2,256,1024]{2,1,0:T(8,128)(2,1)}, u32[]{:S(2)}, u32[]{:S(2)}) collective-permute-start(bf16[2,256,1024]{2,1,0:T(8,128)(2,1)} %fusion.1), channel_id=1, source_target_pairs={{0,8},{8,0},{4,12},{12,4},{1,9},{9,1},{5,13},{13,5},{2,10},{10,2},... | collective-permute-start | bytes 3145736 | tf_op jit(solution)/shard_map/ppermute | solution.py:959
  425.9 55.2 %collective-permute-start.43 = (bf16[4,288,512]{2,1,0:T(8,128)(2,1)}, bf16[4,288,512]{2,1,0:T(8,128)(2,1)}, u32[]{:S(2)}, u32[]{:S(2)}) collective-permute-start(bf16[4,288,512]{2,1,0:T(8,128)(2,1)} %get-tuple-element.182), channel_id=1, source_target_pairs={{0,16},{16,0},{1,17},{17,1},{2,18},{18,2},{3,19},{19,3},{4,20},{20... | collective-permute-start | bytes 3538952 | tf_op jit(solution)/shard_map/ppermute | solution.py:82
  426.4 67.4 %collective-permute-start.44 = (bf16[1,4,512,128]{3,2,1,0:T(8,128)(2,1)}, bf16[1,4,512,128]{3,2,1,0:T(8,128)(2,1)}, u32[]{:S(2)}, u32[]{:S(2)}) collective-permute-start(bf16[1,4,512,128]{3,2,1,0:T(8,128)(2,1)} %get-tuple-element.188), channel_id=1, source_target_pairs={{0,1},{1,0},{2,3},{3,2},{4,5},{5,4},{6,7},{7,6},{8,9},{9,8},{10,11... | collective-permute-start | bytes 1572872 | tf_op jit(solution)/shard_map/ppermute | solution.py:62
  428.3 65.5 %collective-permute-start.45 = (bf16[1,4,256,128]{3,2,1,0:T(8,128)(2,1)}, bf16[1,4,256,128]{3,2,1,0:T(8,128)(2,1)}, u32[]{:S(2)}, u32[]{:S(2)}) collective-permute-start(bf16[1,4,256,128]{3,2,1,0:T(8,128)(2,1)} %get-tuple-element.189), channel_id=1, source_target_pairs={{0,2},{1,3},{2,0},{3,1},{4,6},{5,7},{6,4},{7,5},{8,10},{9,11},{10,... | collective-permute-start | bytes 786440 | tf_op jit(solution)/shard_map/ppermute | solution.py:62
  447.2 46.6 %collective-permute-start.46 = (bf16[1,4,256,128]{3,2,1,0:T(8,128)(2,1)S(1)}, bf16[1,4,256,128]{3,2,1,0:T(8,128)(2,1)}, u32[]{:S(2)}, u32[]{:S(2)}) collective-permute-start(bf16[1,4,256,128]{3,2,1,0:T(8,128)(2,1)S(1)} %copy-done.34), channel_id=1, source_target_pairs={{0,3},{1,2},{2,1},{3,0},{4,7},{5,6},{6,5},{7,4},{8,11},{9,10},{10,... | collective-permute-start | bytes 786440 | tf_op jit(solution)/shard_map/ppermute | solution.py:62
  447.2 118.6 %reduce-scatter.8.cloned.1.call-start = ((), (), s32[]{:S(2)}) async-start(), calls=%async_computation.7 | async-start | bytes 1474560 | tf_op jit(solution)/shard_map/reduce_scatter | solution.py:945
  480.4 29.1 %collective-permute-start.49 = (bf16[1,4,512,128]{3,2,1,0:T(8,128)(2,1)}, bf16[1,4,512,128]{3,2,1,0:T(8,128)(2,1)S(1)}, u32[]{:S(2)}, u32[]{:S(2)}) collective-permute-start(bf16[1,4,512,128]{3,2,1,0:T(8,128)(2,1)} %get-tuple-element.196), channel_id=1, source_target_pairs={{0,1},{1,0},{2,3},{3,2},{4,5},{5,4},{6,7},{7,6},{8,9},{9,8},{10,11... | collective-permute-start | bytes 1572872 | tf_op jit(solution)/shard_map/ppermute | solution.py:62
  555.9 30.0 %collective-permute-start.56 = (bf16[768,128]{1,0:T(8,128)(2,1)}, bf16[768,128]{1,0:T(8,128)(2,1)}, u32[]{:S(2)}, u32[]{:S(2)}) collective-permute-start(bf16[768,128]{1,0:T(8,128)(2,1)} %get-tuple-element.311), channel_id=1, source_target_pairs={{0,1},{1,0},{2,3},{3,2},{4,5},{5,4},{6,7},{7,6},{8,9},{9,8},{10,11... | collective-permute-start | bytes 589832 | tf_op jit(solution)/shard_map/ppermute | solution.py:62
  (91 other events, 1248.8 us)
Sparse Core Ops, SparseCore 0:
  57.9 29.2 all-gather.6
  136.6 29.7 all-gather.8
  186.8 33.9 all-gather.10
  377.2 31.6 reduce-scatter.3
  447.4 38.7 reduce-scatter.5
  519.5 28.8 reduce-scatter.7

commit v5 on v4

--- a/solution.py
+++ b/solution.py
@@ -974,7 +974,7 @@
         gradient = back_rows[s] + norm_back(x[s], root[s], first_gain, first_back)
         return jnp.sum(first_back * x[s] * root[s], axis=0), gradient
 
-    backs, firsts, head_share, gradients = [], [], 0.0, []
+    backs, firsts, head_share, first_share, gradients = [], [], 0.0, 0.0, []
     for s in pair:
         back, own, other, share = line.run(qkv_back_call, place, s, got[s], raw, cosine, sine, gains, w_attn)
         backs.append(back)
@@ -987,12 +987,13 @@
     moved = lax.ppermute(parts[1], "shard", [(0, 1), (1, 0)]) if near else None
     mine, away = line.run(lambda got, own: add_near(own, got), other, own)
     firsts.append((lax.ppermute(away, "ctx", FAR), mine))
-    def finish(s):
+    for s in pair:
         share, gradient = line.run(lambda a, b: last(a, b, s), *firsts[s])
+        first_share = first_share + share
         gradients.append(gradient)
-        return share
-
-    first_share = finish(0)
+    shares = jnp.concatenate([first_share, second_share, head_share[0]])
+    shares = sum_all(shares, [(name, sizes[name]) for name in ("ctx", "shard", "tp")])
+
     if near:
         both = lambda a, b: (a.astype(F32) + b.astype(F32)).astype(BF16)
         g_attn = line.run(
@@ -1003,10 +1004,6 @@
         g_attn = jnp.concatenate([parts[0][0], out_parts[0][0]])
         g_attn = g_attn.reshape(-1, count, width // count).transpose(1, 0, 2)
         g_attn = lax.psum_scatter(g_attn, groups, scatter_dimension=0, tiled=False)
-    first_share = first_share + finish(1)
-    shares = jnp.concatenate([first_share, second_share, head_share[0]])
-    shares = sum_all(shares, [(name, sizes[name]) for name in ("ctx", "shard", "tp")])
-
     def settle(g):
         g = g.reshape(3, units, depth).astype(F32)
         return g[0].T, g[1].T, g[2]

time: 622 us -> 616 us (level)
    ppermute x3, waiting for transfers between devices: 0.01 us -> 7.1 us  [send_shard(): return lax.ppermute(parts[1], 'shard', [(0, 1), (1, 0)])]
    ppermute x15, starting transfers between devices: 43.8 us -> 37.6 us  [to_tp(): return lax.ppermute(value, 'tp', [(i, i ^ e) for i in range(4)])]
    ppermute x2, waiting for transfers between devices: 18.9 us -> 12.7 us  [per_device(): firsts.append((lax.ppermute(away, 'ctx', FAR), mine))]
    unnamed x97 -> x95, local copies, waits for them, and re-layouts: 13.9 us -> 14.1 us
  transfers between devices with their start and end apart: 73 -> 73, of which waited for: 25 -> 29; matrix products, arithmetic and copies ran while one was open for 11% -> 11% of each run, Pallas kernels for 31% -> 31%
where the time goes in v5:
time: 616 us; the launch traced here: 606 us
  Pallas kernels  222 us (36%)
  waiting for transfers between devices  195 us (32%)
  starting transfers between devices  84.8 us (14%)
  other arithmetic  66.1 us (11%)
  local copies, waits for them, and re-layouts  22.2 us (4%)
  between operations  15.1 us (2%)
    pallas_call x2, Pallas kernels, attend_back_call(): pl.pallas_call(attend_back_kernel, grid=(4,), in_specs=[pl.BlockSpec(memo...  58.8 us
    ppermute x15, waiting for transfers between devices, to_tp(): return lax.ppermute(value, 'tp', [(i, i ^ e) for i in range(4)])  56.9 us
    pallas_call x2, Pallas kernels, ffn_call(): pl.pallas_call(functools.partial(ffn_kernel, at, halves), in_specs=[pl.Bl...  50.2 us
    ppermute x6, waiting for transfers between devices, gather_ctx(): far = lax.ppermute(own, 'ctx', FAR)  46.1 us
    ppermute x15, starting transfers between devices, to_tp(): return lax.ppermute(value, 'tp', [(i, i ^ e) for i in range(4)])  37.6 us
    pallas_call x3, Pallas kernels, weight_call(): pl.pallas_call(functools.partial(weight_kernel, halves), grid=(1,), in_sp...  30.6 us
    all_gather x2, waiting for transfers between devices, per_device(): lax.all_gather(after(large[j], *heads), 'tp', axis=0, tiled=False)  28.9 us
    pallas_call x1, Pallas kernels, attend_call(): pl.pallas_call(attend_kernel, grid=(pair, 4), in_specs=[pl.BlockSpec(memo...  26 us
  transfers between devices with their start and end apart: 73, of which 29 were waited for; matrix products, arithmetic and copies ran while one was open for 11% of the time, Pallas kernels for 31%

profile of v5, /device:TPU:6, one launch (start us, length us, event | category | flops | bytes accessed | tf_op | source)
XLA Modules:
  0.0 605.9 jit_solution(15491895103402016138)
XLA Ops:
  37.3 10.0 %collective-permute-done.5 = bf16[128,768]{0,1:T(8,128)(2,1)S(1)} collective-permute-done((bf16[128,768]{0,1:T(8,128)(2,1)S(1)}, bf16[128,768]{0,1:T(8,128)(2,1)S(1)}, u32[]{:S(2)}, u32[]{:S(2)}) %collective-permute-start.5) | collective-permute-done | bytes 196640 | tf_op jit(solution)/shard_map/ppermute | solution.py:109
  57.9 10.0 %collective-permute-done.7 = bf16[512,768]{1,0:T(8,128)(2,1)} collective-permute-done((bf16[512,768]{1,0:T(8,128)(2,1)S(1)}, bf16[512,768]{1,0:T(8,128)(2,1)}, u32[]{:S(2)}, u32[]{:S(2)}) %collective-permute-start.7) | collective-permute-done | bytes 786464 | tf_op jit(solution)/shard_map/ppermute | solution.py:122
  70.4 12.5 %qkv.1 = (bf16[2,4,256,128]{3,2,1,0:T(8,128)(2,1)}, bf16[2,4,256,128]{3,2,1,0:T(8,128)(2,1)}, bf16[2,4,512,128]{3,2,1,0:T(8,128)(2,1)}, bf16[2,4,256,128]{3,2,1,0:T(8,128)(2,1)}, f32[2,4,256,384]{3,2,1,0:T(8,128)}) custom-call(s32[2]{0:T(128)} %pad_add_fusion.place_ref, bf16[2,256,1024]{2,1,0:T(8,128)(2,1)} %multiply_convert_fusion.1.refs_0_.refs_2_, ...), custom_call_target="tpu_custom_call" | custom-call | flops 15000000512 | bytes 15000000 | tf_op jit(solution)/shard_map/qkv/pallas_call | solution.py:241
  89.9 17.9 %collective-permute-done.15.refs_6_.refs_3_ = bf16[2,256,1024]{2,1,0:T(8,128)(2,1)} collective-permute-done((bf16[2,256,1024]{2,1,0:T(8,128)(2,1)S(1)}, bf16[2,256,1024]{2,1,0:T(8,128)(2,1)}, u32[]{:S(2)}, u32[]{:S(2)}) %collective-permute-start.15) | collective-permute-done | bytes 1048608 | tf_op jit(solution)/shard_map/ppermute | solution.py:39
  116.3 20.2 %collective-permute-done.13.refs_4_ = bf16[2,4,256,128]{3,2,1,0:T(8,128)(2,1)} collective-permute-done((bf16[2,4,256,128]{3,2,1,0:T(8,128)(2,1)}, bf16[2,4,256,128]{3,2,1,0:T(8,128)(2,1)}, u32[]{:S(2)}, u32[]{:S(2)}) %collective-permute-start.13) | collective-permute-done | bytes 524320 | tf_op jit(solution)/shard_map/ppermute | solution.py:62
  136.8 26.0 %attend.1 = (bf16[2,4,256,128]{3,2,1,0:T(8,128)(2,1)}, bf16[2,4,256,128]{3,2,1,0:T(8,128)(2,1)}, f32[2,4,64,1024]{3,2,1,0:T(8,128)}, f32[2,4,1,1024]{3,2,1,0:T(1,128)}) custom-call(s32[2]{0:T(128)} %pad_add_fusion.place_ref, bf16[2,4,256,128]{3,2,1,0:T(8,128)(2,1)} %get-tuple-element.122.refs_0_, bf16[2,4,256,128]{3,2,1,0:T(8,128)(2,1)} %get-tuple-element.123.refs_1_, ...), custom_call_target="tpu_custom_call" | custom-call | flops 32000000000 | bytes 32000000 | tf_op jit(solution)/shard_map/attend/pallas_call | solution.py:353
  166.4 10.4 %collective-permute-done.18.get_other = bf16[2,4,256,128]{3,2,1,0:T(8,128)(2,1)S(1)} collective-permute-done((bf16[2,4,256,128]{3,2,1,0:T(8,128)(2,1)}, bf16[2,4,256,128]{3,2,1,0:T(8,128)(2,1)S(1)}, u32[]{:S(2)}, u32[]{:S(2)}) %collective-permute-start.18) | collective-permute-done | bytes 524320 | tf_op jit(solution)/shard_map/ppermute | solution.py:62
  177.6 8.1 %out.1 = (bf16[2,4,256,256]{3,2,1,0:T(8,128)(2,1)}, bf16[2,2,256,1024]{3,2,1,0:T(8,128)(2,1)}, bf16[2,2,256,1024]{3,2,1,0:T(8,128)(2,1)}) custom-call(s32[2]{0:T(128)} %pad_add_fusion.place_ref, bf16[2,4,256,128]{3,2,1,0:T(8,128)(2,1)} %get-tuple-element.130.get_own, bf16[2,4,256,128]{3,2,1,0:T(8,128)(2,1)} %copy-done.32, ...), custom_call_target="tpu_custom_call" | custom-call | flops 8999999488 | bytes 9000000 | tf_op jit(solution)/shard_map/out/pallas_call | solution.py:406
  194.7 26.0 %all-gather.11.cloned.1.call-done = bf16[1152,512]{1,0:T(8,128)(2,1)} async-done(((bf16[288,512]{1,0:T(8,128)(2,1)}), bf16[1152,512]{1,0:T(8,128)(2,1)}) %all-gather.11.cloned.1.call-update) | async-done | bytes 1179664 | tf_op jit(solution)/shard_map/all_gather | solution.py:879
  225.4 23.5 %collective-permute-done.22.refs_2_.refs_3_ = bf16[2,256,1024]{2,1,0:T(8,128)(2,1)} collective-permute-done((bf16[2,256,1024]{2,1,0:T(8,128)(2,1)}, bf16[2,256,1024]{2,1,0:T(8,128)(2,1)}, u32[]{:S(2)}, u32[]{:S(2)}) %collective-permute-start.22) | collective-permute-done | bytes 1048608 | tf_op jit(solution)/shard_map/ppermute | solution.py:39
  252.0 25.2 %ffn.2 = (bf16[3,4,256,1152]{3,2,1,0:T(8,128)(2,1)}, bf16[2,2,256,1024]{3,2,1,0:T(8,128)(2,1)}, bf16[2,2,256,1024]{3,2,1,0:T(8,128)(2,1)}, bf16[2,256,1024]{2,1,0:T(8,128)(2,1)}, bf16[2,256,1024]{2,1,0:T(8,128)(2,1)}) custom-call(s32[2]{0:T(128)} %add_multiply_fusion.refs_0_.offset_ref, bf16[2,256,1024]{2,1,0:T(8,128)(2,1)} %multiply_convert_fusion.refs_1_.refs_2_, ...), custom_call_target="tpu_custom_call" | custom-call | flops 22000001024 | bytes 22000000 | tf_op jit(solution)/shard_map/ffn/pallas_call | solution.py:715
  282.7 25.0 %ffn.3 = (bf16[3,4,256,1152]{3,2,1,0:T(8,128)(2,1)}, bf16[2,2,256,1024]{3,2,1,0:T(8,128)(2,1)}, bf16[2,2,256,1024]{3,2,1,0:T(8,128)(2,1)}, bf16[2,256,1024]{2,1,0:T(8,128)(2,1)}, bf16[2,256,1024]{2,1,0:T(8,128)(2,1)}) custom-call(s32[2]{0:T(128)} %add_multiply_fusion.refs_0_.offset_ref, ...), custom_call_target="tpu_custom_call", output_to_operand_aliasing={{1}: (15, {}), {2}: (16, {})} | custom-call | flops 22000001024 | bytes 22000000 | tf_op jit(solution)/shard_map/ffn/pallas_call | solution.py:715
  313.4 10.1 %weight.3 = (bf16[4,288,512]{2,1,0:T(8,128)(2,1)}, bf16[4,288,512]{2,1,0:T(8,128)(2,1)}) custom-call(s32[2]{0:T(128)} %add_multiply_fusion.refs_0_.offset_ref, bf16[3,4,256,1152]{3,2,1,0:T(8,128)(2,1)} %get-tuple-element.140.refs_0_, bf16[3,4,256,1152]{3,2,1,0:T(8,128)(2,1)} %get-tuple-element.149.refs_1_, ...), custom_call_target="tpu_custom_call" | custom-call | flops 10000000000 | bytes 10000000 | tf_op jit(solution)/shard_map/weight/pallas_call | solution.py:760
  326.6 10.1 %weight.4 = (bf16[4,288,512]{2,1,0:T(8,128)(2,1)}, bf16[4,288,512]{2,1,0:T(8,128)(2,1)}) custom-call(s32[2]{0:T(128)} %add_multiply_fusion.refs_0_.offset_ref, bf16[3,4,256,1152]{3,2,1,0:T(8,128)(2,1)} %get-tuple-element.140.refs_0_, bf16[3,4,256,1152]{3,2,1,0:T(8,128)(2,1)} %get-tuple-element.149.refs_1_, ...), custom_call_target="tpu_custom_call" | custom-call | flops 10000000000 | bytes 10000000 | tf_op jit(solution)/shard_map/weight/pallas_call | solution.py:760
  346.9 7.1 %collective-permute-done.33.refs_6_ = bf16[4,256,128]{2,1,0:T(8,128)(2,1)S(1)} collective-permute-done((bf16[4,256,128]{2,1,0:T(8,128)(2,1)S(1)}, bf16[4,256,128]{2,1,0:T(8,128)(2,1)S(1)}, u32[]{:S(2)}, u32[]{:S(2)}) %collective-permute-start.33) | collective-permute-done | bytes 262176 | tf_op jit(solution)/shard_map/ppermute | solution.py:62
  358.6 10.4 %weight.5 = (bf16[4,288,512]{2,1,0:T(8,128)(2,1)}, bf16[4,288,512]{2,1,0:T(8,128)(2,1)}) custom-call(s32[2]{0:T(128)} %add_multiply_fusion.refs_0_.offset_ref, bf16[3,4,256,1152]{3,2,1,0:T(8,128)(2,1)} %get-tuple-element.140.refs_0_, bf16[3,4,256,1152]{3,2,1,0:T(8,128)(2,1)} %get-tuple-element.149.refs_1_, bf16[2,256,1024]{2,1,0:T(8,128)(2,1)} %refs_2_, ...), custom_call_target="tpu_custom_call" | custom-call | flops 10000000000 | bytes 10000000 | tf_op jit(solution)/shard_map/weight/pallas_call | solution.py:760
  375.5 7.1 %collective-permute-done.35 = bf16[4,288,512]{2,1,0:T(8,128)(2,1)S(1)} collective-permute-done((bf16[4,288,512]{2,1,0:T(8,128)(2,1)}, bf16[4,288,512]{2,1,0:T(8,128)(2,1)S(1)}, u32[]{:S(2)}, u32[]{:S(2)}) %collective-permute-start.35) | collective-permute-done | bytes 1179680 | tf_op jit(solution)/shard_map/ppermute | solution.py:82
  395.2 29.2 %attend_back.2 = (bf16[1,4,256,128]{3,2,1,0:T(8,128)(2,1)}, bf16[1,4,256,128]{3,2,1,0:T(8,128)(2,1)}, bf16[1,4,512,128]{3,2,1,0:T(8,128)(2,1)}, bf16[1,4,256,128]{3,2,1,0:T(8,128)(2,1)}, bf16[1,4,256,128]{3,2,1,0:T(8,128)(2,1)}) custom-call(s32[2]{0:T(128)} %pad_add_fusion.place_ref, bf16[2,4,256,128]{3,2,1,0:T(8,128)(2,1)} %get-tuple-element.122.refs_0_, ...), custom_call_target="tpu_custom_call" | custom-call | flops 8000000000 | bytes 8000000 | tf_op jit(solution)/shard_map/attend_back/pallas_call | solution.py:517
  432.4 12.0 %collective-permute-start.45 = (bf16[1,4,256,128]{3,2,1,0:T(8,128)(2,1)}, bf16[1,4,256,128]{3,2,1,0:T(8,128)(2,1)}, u32[]{:S(2)}, u32[]{:S(2)}) collective-permute-start(bf16[1,4,256,128]{3,2,1,0:T(8,128)(2,1)} %get-tuple-element.189), channel_id=1, source_target_pairs={{0,2},{1,3},{2,0},{3,1},{4,6},{5,7},{6,4},{7,5},{8,10},{9,11},{10,... | collective-permute-start | bytes 786440 | tf_op jit(solution)/shard_map/ppermute | solution.py:62
  448.2 29.5 %attend_back.3 = (bf16[1,4,256,128]{3,2,1,0:T(8,128)(2,1)}, bf16[1,4,256,128]{3,2,1,0:T(8,128)(2,1)}, bf16[1,4,512,128]{3,2,1,0:T(8,128)(2,1)}, bf16[1,4,256,128]{3,2,1,0:T(8,128)(2,1)}, bf16[1,4,256,128]{3,2,1,0:T(8,128)(2,1)}) custom-call(s32[2]{0:T(128)} %pad_add_fusion.place_ref, bf16[2,4,256,128]{3,2,1,0:T(8,128)(2,1)} %get-tuple-element.122.refs_0_, ...), custom_call_target="tpu_custom_call" | custom-call | flops 8000000000 | bytes 8000000 | tf_op jit(solution)/shard_map/attend_back/pallas_call | solution.py:517
  481.0 10.1 %collective-permute-start.50 = (bf16[1,4,256,128]{3,2,1,0:T(8,128)(2,1)S(1)}, bf16[1,4,256,128]{3,2,1,0:T(8,128)(2,1)S(1)}, u32[]{:S(2)}, u32[]{:S(2)}) collective-permute-start(bf16[1,4,256,128]{3,2,1,0:T(8,128)(2,1)S(1)} %copy-done.36), channel_id=1, source_target_pairs={{0,2},{1,3},{2,0},{3,1},{4,6},{5,7},{6,4},{7,5},{8,10},{9,11},{10,... | collective-permute-start | bytes 786440 | tf_op jit(solution)/shard_map/ppermute | solution.py:62
  491.1 7.7 %qkv_back.2 = (bf16[1,4,256,512]{3,2,1,0:T(8,128)(2,1)}, bf16[2,1,256,1024]{3,2,1,0:T(8,128)(2,1)}, bf16[2,1,256,1024]{3,2,1,0:T(8,128)(2,1)}, f32[1,384]{1,0:T(1,128)}) custom-call(s32[2]{0:T(128)} %pad_add_fusion.place_ref, bf16[1,4,256,128]{3,2,1,0:T(8,128)(2,1)} %get-tuple-element.176.refs_0_, bf16[1,4,256,128]{3,2,1,0:T(8,128)(2,1)} %get-tuple-element.187.refs_1_, ...), custom_call_target="tpu_custom_call" | custom-call | flops 8000000000 | bytes 8000000 | tf_op jit(solution)/shard_map/qkv_back/pallas_call | solution.py:581
  508.4 7.6 %qkv_back.3 = (bf16[1,4,256,512]{3,2,1,0:T(8,128)(2,1)}, bf16[2,1,256,1024]{3,2,1,0:T(8,128)(2,1)}, bf16[2,1,256,1024]{3,2,1,0:T(8,128)(2,1)}, f32[1,384]{1,0:T(1,128)}) custom-call(s32[2]{0:T(128)} %pad_add_fusion.place_ref, bf16[1,4,256,128]{3,2,1,0:T(8,128)(2,1)} %get-tuple-element.184.refs_0_, bf16[1,4,256,128]{3,2,1,0:T(8,128)(2,1)} %get-tuple-element.195.refs_1_, ...), custom_call_target="tpu_custom_call" | custom-call | flops 8000000000 | bytes 8000000 | tf_op jit(solution)/shard_map/qkv_back/pallas_call | solution.py:581
  535.8 9.4 %collective-permute-done.53 = bf16[1,256,1024]{2,1,0:T(8,128)(2,1)S(1)} collective-permute-done((bf16[1,256,1024]{2,1,0:T(8,128)(2,1)S(1)}, bf16[1,256,1024]{2,1,0:T(8,128)(2,1)S(1)}, u32[]{:S(2)}, u32[]{:S(2)}) %collective-permute-start.53) | collective-permute-done | bytes 524320 | tf_op jit(solution)/shard_map/ppermute | solution.py:989
  (329 shorter events, 225.8 us)
Async XLA Ops:
  19.6 28.8 %collective-permute-start = (bf16[2,256,1024]{2,1,0:T(8,128)(2,1)}, bf16[2,256,1024]{2,1,0:T(8,128)(2,1)}, u32[]{:S(2)}, u32[]{:S(2)}) collective-permute-start(bf16[2,256,1024]{2,1,0:T(8,128)(2,1)} %multiply_convert_fusion.1.refs_0_.refs_2_), channel_id=1, source_target_pairs={{0,8},{8,0},{4,12},{12,4},{1,9},{9,1},{5,13},{13,5},{2,10},{10,2},... | collective-permute-start | bytes 3145736 | tf_op jit(solution)/shard_map/ppermute | solution.py:39
  23.2 33.7 %all-to-all-start = ((bf16[3,4,288,128]{3,2,0,1:T(8,128)(2,1)}), bf16[3,4,288,128]{3,2,0,1:T(8,128)(2,1)S(1)}, u32[]{:S(2)}, u32[]{:S(2)}) async-start(bf16[3,4,288,128]{3,2,0,1:T(8,128)(2,1)} %copy.94), calls=%async_computation | async-start | bytes 1769472 | tf_op jit(solution)/shard_map/all_to_all | solution.py:853
  26.7 60.6 %all-gather.7.cloned.1.call-start = ((), (), s32[]{:S(2)}) async-start(), calls=%async_computation.8 | async-start | bytes 1474560 | tf_op jit(solution)/shard_map/all_gather | solution.py:877
  37.3 33.1 %collective-permute-start.1 = (bf16[2,256,1024]{2,1,0:T(8,128)(2,1)}, bf16[2,256,1024]{2,1,0:T(8,128)(2,1)}, u32[]{:S(2)}, u32[]{:S(2)}) collective-permute-start(bf16[2,256,1024]{2,1,0:T(8,128)(2,1)} %multiply_convert_fusion.1.refs_0_.refs_2_), channel_id=1, source_target_pairs={{0,4},{4,0},{8,12},{12,8},{1,5},{5,1},{9,13},{13,9},{2,6},{6,2},{1... | collective-permute-start | bytes 3145736 | tf_op jit(solution)/shard_map/ppermute | solution.py:40
  57.8 108.6 %all-gather.9.cloned.1.call-start = ((), (), s32[]{:S(2)}) async-start(), calls=%async_computation.9 | async-start | bytes 1474560 | tf_op jit(solution)/shard_map/all_gather | solution.py:879
  87.3 49.5 %collective-permute-start.14 = (bf16[4,288,512]{2,1,0:T(8,128)(2,1)}, bf16[4,288,512]{2,1,0:T(8,128)(2,1)}, u32[]{:S(2)}, u32[]{:S(2)}) collective-permute-start(bf16[4,288,512]{2,1,0:T(8,128)(2,1)} %bitcast.224), channel_id=1, source_target_pairs={{0,16},{16,0},{1,17},{17,1},{2,18},{18,2},{3,19},{19,3},{4,20},{20... | collective-permute-start | bytes 3538952 | tf_op jit(solution)/shard_map/ppermute | solution.py:75
  89.3 47.1 %collective-permute-start.11 = (bf16[2,4,512,128]{3,2,1,0:T(8,128)(2,1)}, bf16[2,4,512,128]{3,2,1,0:T(8,128)(2,1)}, u32[]{:S(2)}, u32[]{:S(2)}) collective-permute-start(bf16[2,4,512,128]{3,2,1,0:T(8,128)(2,1)} %get-tuple-element.116), channel_id=1, source_target_pairs={{0,1},{1,0},{2,3},{3,2},{4,5},{5,4},{6,7},{7,6},{8,9},{9,8},{10,11... | collective-permute-start | bytes 3145736 | tf_op jit(solution)/shard_map/ppermute | solution.py:62
  89.9 46.9 %collective-permute-start.16 = (bf16[2,256,1024]{2,1,0:T(8,128)(2,1)S(1)}, bf16[2,256,1024]{2,1,0:T(8,128)(2,1)}, u32[]{:S(2)}, u32[]{:S(2)}) collective-permute-start(bf16[2,256,1024]{2,1,0:T(8,128)(2,1)S(1)} %copy-done.11), channel_id=1, source_target_pairs={{0,4},{4,0},{8,12},{12,8},{1,5},{5,1},{9,13},{13,9},{2,6},{6,2},{1... | collective-permute-start | bytes 3145736 | tf_op jit(solution)/shard_map/ppermute | solution.py:40
  107.8 28.9 %collective-permute-start.17 = (bf16[2,256,1024]{2,1,0:T(8,128)(2,1)}, bf16[2,256,1024]{2,1,0:T(8,128)(2,1)}, u32[]{:S(2)}, u32[]{:S(2)}) collective-permute-start(bf16[2,256,1024]{2,1,0:T(8,128)(2,1)} %collective-permute-done.15.refs_6_.refs_3_), channel_id=1, source_target_pairs={{0,4},{4,0},{8,12},{12,8},{1,5},{5,1},{9,13},{13,9},{2,6},{6,2},{1... | collective-permute-start | bytes 3145736 | tf_op jit(solution)/shard_map/ppermute | solution.py:41
  136.5 84.2 %all-gather.11.cloned.1.call-start = ((), (), s32[]{:S(2)}) async-start(), calls=%async_computation.10 | async-start | bytes 1474560 | tf_op jit(solution)/shard_map/all_gather | solution.py:879
  186.6 373.2 %reduce-scatter.4.cloned.1.call-start = ((), (), s32[]{:S(2)}) async-start(), calls=%async_computation.5 | async-start | bytes 1474560 | tf_op jit(solution)/shard_map/reduce_scatter | solution.py:945
  186.7 34.0 %collective-permute-start.20 = (bf16[4,288,512]{2,1,0:T(8,128)(2,1)}, bf16[4,288,512]{2,1,0:T(8,128)(2,1)}, u32[]{:S(2)}, u32[]{:S(2)}) collective-permute-start(bf16[4,288,512]{2,1,0:T(8,128)(2,1)} %bitcast.227), channel_id=1, source_target_pairs={{0,16},{16,0},{1,17},{17,1},{2,18},{18,2},{3,19},{19,3},{4,20},{20... | collective-permute-start | bytes 3538952 | tf_op jit(solution)/shard_map/ppermute | solution.py:75
  279.5 28.2 %collective-permute-start.27 = (bf16[256,1024]{1,0:T(8,128)(2,1)}, bf16[256,1024]{1,0:T(8,128)(2,1)S(1)}, u32[]{:S(2)}, u32[]{:S(2)}) collective-permute-start(bf16[256,1024]{1,0:T(8,128)(2,1)} %get-tuple-element.301), channel_id=1, source_target_pairs={{0,8},{8,0},{4,12},{12,4},{1,9},{9,1},{5,13},{13,5},{2,10},{10,2},... | collective-permute-start | bytes 1572872 | tf_op jit(solution)/shard_map/ppermute | solution.py:920
  354.0 37.5 %collective-permute-start.34 = (bf16[2,2,256,1024]{3,2,1,0:T(8,128)(2,1)}, bf16[2,2,256,1024]{3,2,1,0:T(8,128)(2,1)}, u32[]{:S(2)}, u32[]{:S(2)}) collective-permute-start(bf16[2,2,256,1024]{3,2,1,0:T(8,128)(2,1)} %get-tuple-element.160), channel_id=1, source_target_pairs={{0,4},{4,0},{8,12},{12,8},{1,5},{5,1},{9,13},{13,9},{2,6},{6,2},{1... | collective-permute-start | bytes 6291464 | tf_op jit(solution)/shard_map/ppermute | solution.py:957
  384.0 175.9 %reduce-scatter.6.cloned.1.call-start = ((), (), s32[]{:S(2)}) async-start(), calls=%async_computation.6 | async-start | bytes 1474560 | tf_op jit(solution)/shard_map/reduce_scatter | solution.py:945
  385.5 43.7 %collective-permute-start.41 = (bf16[4,288,512]{2,1,0:T(8,128)(2,1)}, bf16[4,288,512]{2,1,0:T(8,128)(2,1)S(1)}, u32[]{:S(2)}, u32[]{:S(2)}) collective-permute-start(bf16[4,288,512]{2,1,0:T(8,128)(2,1)} %get-tuple-element.170), channel_id=1, source_target_pairs={{0,16},{16,0},{1,17},{17,1},{2,18},{18,2},{3,19},{19,3},{4,20},{20... | collective-permute-start | bytes 3538952 | tf_op jit(solution)/shard_map/ppermute | solution.py:82
  394.6 49.9 %collective-permute-start.40 = (bf16[2,256,1024]{2,1,0:T(8,128)(2,1)}, bf16[2,256,1024]{2,1,0:T(8,128)(2,1)}, u32[]{:S(2)}, u32[]{:S(2)}) collective-permute-start(bf16[2,256,1024]{2,1,0:T(8,128)(2,1)} %fusion.1), channel_id=1, source_target_pairs={{0,8},{8,0},{4,12},{12,4},{1,9},{9,1},{5,13},{13,5},{2,10},{10,2},... | collective-permute-start | bytes 3145736 | tf_op jit(solution)/shard_map/ppermute | solution.py:959
  430.6 47.1 %collective-permute-start.43 = (bf16[4,288,512]{2,1,0:T(8,128)(2,1)}, bf16[4,288,512]{2,1,0:T(8,128)(2,1)}, u32[]{:S(2)}, u32[]{:S(2)}) collective-permute-start(bf16[4,288,512]{2,1,0:T(8,128)(2,1)} %get-tuple-element.182), channel_id=1, source_target_pairs={{0,16},{16,0},{1,17},{17,1},{2,18},{18,2},{3,19},{19,3},{4,20},{20... | collective-permute-start | bytes 3538952 | tf_op jit(solution)/shard_map/ppermute | solution.py:82
  431.2 60.0 %collective-permute-start.44 = (bf16[1,4,512,128]{3,2,1,0:T(8,128)(2,1)}, bf16[1,4,512,128]{3,2,1,0:T(8,128)(2,1)}, u32[]{:S(2)}, u32[]{:S(2)}) collective-permute-start(bf16[1,4,512,128]{3,2,1,0:T(8,128)(2,1)} %get-tuple-element.188), channel_id=1, source_target_pairs={{0,1},{1,0},{2,3},{3,2},{4,5},{5,4},{6,7},{7,6},{8,9},{9,8},{10,11... | collective-permute-start | bytes 1572872 | tf_op jit(solution)/shard_map/ppermute | solution.py:62
  432.4 48.5 %collective-permute-start.45 = (bf16[1,4,256,128]{3,2,1,0:T(8,128)(2,1)}, bf16[1,4,256,128]{3,2,1,0:T(8,128)(2,1)}, u32[]{:S(2)}, u32[]{:S(2)}) collective-permute-start(bf16[1,4,256,128]{3,2,1,0:T(8,128)(2,1)} %get-tuple-element.189), channel_id=1, source_target_pairs={{0,2},{1,3},{2,0},{3,1},{4,6},{5,7},{6,4},{7,5},{8,10},{9,11},{10,... | collective-permute-start | bytes 786440 | tf_op jit(solution)/shard_map/ppermute | solution.py:62
  444.4 46.7 %collective-permute-start.46 = (bf16[1,4,256,128]{3,2,1,0:T(8,128)(2,1)}, bf16[1,4,256,128]{3,2,1,0:T(8,128)(2,1)}, u32[]{:S(2)}, u32[]{:S(2)}) collective-permute-start(bf16[1,4,256,128]{3,2,1,0:T(8,128)(2,1)} %get-tuple-element.190), channel_id=1, source_target_pairs={{0,3},{1,2},{2,1},{3,0},{4,7},{5,6},{6,5},{7,4},{8,11},{9,10},{10,... | collective-permute-start | bytes 786440 | tf_op jit(solution)/shard_map/ppermute | solution.py:62
  444.5 115.4 %reduce-scatter.8.cloned.1.call-start = ((), (), s32[]{:S(2)}) async-start(), calls=%async_computation.7 | async-start | bytes 1474560 | tf_op jit(solution)/shard_map/reduce_scatter | solution.py:945
  444.5 72.4 %collective-permute-start.55 = (bf16[4,256,128]{2,1,0:T(8,128)(2,1)}, bf16[4,256,128]{2,1,0:T(8,128)(2,1)}, u32[]{:S(2)}, u32[]{:S(2)}) collective-permute-start(bf16[4,256,128]{2,1,0:T(8,128)(2,1)} %get-tuple-element.208), channel_id=1, source_target_pairs={{0,16},{16,0},{1,17},{17,1},{2,18},{18,2},{3,19},{19,3},{4,20},{20... | collective-permute-start | bytes 786440 | tf_op jit(solution)/shard_map/ppermute | solution.py:964
  477.7 29.8 %collective-permute-start.49 = (bf16[1,4,512,128]{3,2,1,0:T(8,128)(2,1)}, bf16[1,4,512,128]{3,2,1,0:T(8,128)(2,1)S(1)}, u32[]{:S(2)}, u32[]{:S(2)}) collective-permute-start(bf16[1,4,512,128]{3,2,1,0:T(8,128)(2,1)} %get-tuple-element.196), channel_id=1, source_target_pairs={{0,1},{1,0},{2,3},{3,2},{4,5},{5,4},{6,7},{7,6},{8,9},{9,8},{10,11... | collective-permute-start | bytes 1572872 | tf_op jit(solution)/shard_map/ppermute | solution.py:62
  (90 other events, 1263.9 us)
Sparse Core Ops, SparseCore 0:
  58.0 29.2 all-gather.6
  136.6 29.7 all-gather.8
  186.8 33.9 all-gather.10
  384.1 31.5 reduce-scatter.3
  444.6 39.4 reduce-scatter.5
  518.2 31.3 reduce-scatter.7

commit v6 on v5

--- a/solution.py
+++ b/solution.py
@@ -740,32 +740,45 @@
 
 def weight_kernel(halves, offset_ref, *refs):
     lefts, rights = refs[0:2], refs[2:6]
-    outs, total_ref = refs[6 : 6 + halves], refs[6 + halves]
+    outs, (total_ref, right_ref) = refs[6 : 6 + halves], refs[6 + halves :]
+    j = pl.program_id(0)
+    rows = rights[0].shape[1]
+
+    @pl.when(j == 0)
+    def _():
+        for s in range(2):
+            for k, ref in enumerate(rights):
+                right_ref[s, k * rows : (k + 1) * rows] = ref[s]
+
     total = 0.0
     for s, left in enumerate(lefts):
         a = left[0]
-        total = total + dot_tn(a.reshape(-1, a.shape[-1]), jnp.concatenate([ref[s] for ref in rights]))
-    total_ref[...] = total.astype(BF16)
+        total = total + dot_tn(a.reshape(-1, a.shape[-1]), right_ref[s])
+    third = total.shape[0]
+    total_ref[pl.ds(pl.multiple_of(j * third, 128), third)] = total.astype(BF16)
     blocks, depth, span = outs[0].shape
-    for p in range(halves):
-        start = pl.multiple_of(offset_ref[p], 128)
-        for i in range(blocks):
-            outs[p][i] = total_ref[i * depth : (i + 1) * depth, pl.ds(start, span)]
+
+    @pl.when(j == 2)
+    def _():
+        for p in range(halves):
+            start = pl.multiple_of(offset_ref[p], 128)
+            for i in range(blocks):
+                outs[p][i] = total_ref[i * depth : (i + 1) * depth, pl.ds(start, span)]
 
 
 def weight_call(offsets, kind, acts, rights, halves, blocks):
     units, width = acts[0].shape[-1], rights[0].shape[-1]
-    unit = (1, *acts[0].shape[1:])
+    unit = (1, *acts[0].shape[1:3], units // 3)
     part = (blocks, units // blocks, width // halves)
     return pl.pallas_call(
         functools.partial(weight_kernel, halves),
-        grid=(1,),
+        grid=(3,),
         in_specs=[pl.BlockSpec(memory_space=pltpu.SMEM)]
-        + [pl.BlockSpec(unit, lambda j: (kind, 0, 0, 0))] * 2
+        + [pl.BlockSpec(unit, lambda j: (kind, 0, 0, j))] * 2
         + [whole(one.shape) for one in rights],
         out_specs=[whole(part)] * halves,
         out_shape=[jax.ShapeDtypeStruct(part, BF16)] * halves,
-        scratch_shapes=[pltpu.VMEM((units, width), BF16)],
+        scratch_shapes=[pltpu.VMEM((units, width), BF16), pltpu.VMEM((2, 4 * rights[0].shape[1], width), BF16)],
         compiler_params=params(),
         cost_estimate=cost(10),
         name="weight",

time: 616 us -> 616 us (level)
  no operation moved by 1% of the time
where the time goes in v6:
time: 616 us; the launch traced here: 606 us
  Pallas kernels  222 us (36%)
  waiting for transfers between devices  195 us (32%)
  starting transfers between devices  84.8 us (14%)
  other arithmetic  66.1 us (11%)
  local copies, waits for them, and re-layouts  22.2 us (4%)
  between operations  15.3 us (2%)
    pallas_call x2, Pallas kernels, attend_back_call(): pl.pallas_call(attend_back_kernel, grid=(4,), in_specs=[pl.BlockSpec(memo...  58.8 us
    ppermute x15, waiting for transfers between devices, to_tp(): return lax.ppermute(value, 'tp', [(i, i ^ e) for i in range(4)])  56.9 us
    pallas_call x2, Pallas kernels, ffn_call(): pl.pallas_call(functools.partial(ffn_kernel, at, halves), in_specs=[pl.Bl...  50.2 us
    ppermute x6, waiting for transfers between devices, gather_ctx(): far = lax.ppermute(own, 'ctx', FAR)  46.2 us
    ppermute x15, starting transfers between devices, to_tp(): return lax.ppermute(value, 'tp', [(i, i ^ e) for i in range(4)])  37.6 us
    pallas_call x3, Pallas kernels, weight_call(): pl.pallas_call(functools.partial(weight_kernel, halves), grid=(3,), in_sp...  30.5 us
    all_gather x2, waiting for transfers between devices, per_device(): lax.all_gather(after(large[j], *heads), 'tp', axis=0, tiled=False)  28.9 us
    pallas_call x1, Pallas kernels, attend_call(): pl.pallas_call(attend_kernel, grid=(pair, 4), in_specs=[pl.BlockSpec(memo...  26 us
  transfers between devices with their start and end apart: 73, of which 29 were waited for; matrix products, arithmetic and copies ran while one was open for 11% of the time, Pallas kernels for 31%

profile of v6, /device:TPU:6, one launch (start us, length us, event | category | flops | bytes accessed | tf_op | source)
XLA Modules:
  0.0 605.9 jit_solution(5705916687114803836)
XLA Ops:
  37.3 10.0 %collective-permute-done.5 = bf16[128,768]{0,1:T(8,128)(2,1)S(1)} collective-permute-done((bf16[128,768]{0,1:T(8,128)(2,1)S(1)}, bf16[128,768]{0,1:T(8,128)(2,1)S(1)}, u32[]{:S(2)}, u32[]{:S(2)}) %collective-permute-start.5) | collective-permute-done | bytes 196640 | tf_op jit(solution)/shard_map/ppermute | solution.py:109
  57.9 10.0 %collective-permute-done.7 = bf16[512,768]{1,0:T(8,128)(2,1)} collective-permute-done((bf16[512,768]{1,0:T(8,128)(2,1)S(1)}, bf16[512,768]{1,0:T(8,128)(2,1)}, u32[]{:S(2)}, u32[]{:S(2)}) %collective-permute-start.7) | collective-permute-done | bytes 786464 | tf_op jit(solution)/shard_map/ppermute | solution.py:122
  70.4 12.5 %qkv.1 = (bf16[2,4,256,128]{3,2,1,0:T(8,128)(2,1)}, bf16[2,4,256,128]{3,2,1,0:T(8,128)(2,1)}, bf16[2,4,512,128]{3,2,1,0:T(8,128)(2,1)}, bf16[2,4,256,128]{3,2,1,0:T(8,128)(2,1)}, f32[2,4,256,384]{3,2,1,0:T(8,128)}) custom-call(s32[2]{0:T(128)} %pad_add_fusion.place_ref, bf16[2,256,1024]{2,1,0:T(8,128)(2,1)} %multiply_convert_fusion.1.refs_0_.refs_2_, ...), custom_call_target="tpu_custom_call" | custom-call | flops 15000000512 | bytes 15000000 | tf_op jit(solution)/shard_map/qkv/pallas_call | solution.py:241
  89.9 17.9 %collective-permute-done.15.refs_6_.refs_3_ = bf16[2,256,1024]{2,1,0:T(8,128)(2,1)} collective-permute-done((bf16[2,256,1024]{2,1,0:T(8,128)(2,1)S(1)}, bf16[2,256,1024]{2,1,0:T(8,128)(2,1)}, u32[]{:S(2)}, u32[]{:S(2)}) %collective-permute-start.15) | collective-permute-done | bytes 1048608 | tf_op jit(solution)/shard_map/ppermute | solution.py:39
  116.3 20.2 %collective-permute-done.13.refs_4_ = bf16[2,4,256,128]{3,2,1,0:T(8,128)(2,1)} collective-permute-done((bf16[2,4,256,128]{3,2,1,0:T(8,128)(2,1)}, bf16[2,4,256,128]{3,2,1,0:T(8,128)(2,1)}, u32[]{:S(2)}, u32[]{:S(2)}) %collective-permute-start.13) | collective-permute-done | bytes 524320 | tf_op jit(solution)/shard_map/ppermute | solution.py:62
  136.8 26.0 %attend.1 = (bf16[2,4,256,128]{3,2,1,0:T(8,128)(2,1)}, bf16[2,4,256,128]{3,2,1,0:T(8,128)(2,1)}, f32[2,4,64,1024]{3,2,1,0:T(8,128)}, f32[2,4,1,1024]{3,2,1,0:T(1,128)}) custom-call(s32[2]{0:T(128)} %pad_add_fusion.place_ref, bf16[2,4,256,128]{3,2,1,0:T(8,128)(2,1)} %get-tuple-element.122.refs_0_, bf16[2,4,256,128]{3,2,1,0:T(8,128)(2,1)} %get-tuple-element.123.refs_1_, ...), custom_call_target="tpu_custom_call" | custom-call | flops 32000000000 | bytes 32000000 | tf_op jit(solution)/shard_map/attend/pallas_call | solution.py:353
  166.4 10.4 %collective-permute-done.18.get_other = bf16[2,4,256,128]{3,2,1,0:T(8,128)(2,1)S(1)} collective-permute-done((bf16[2,4,256,128]{3,2,1,0:T(8,128)(2,1)}, bf16[2,4,256,128]{3,2,1,0:T(8,128)(2,1)S(1)}, u32[]{:S(2)}, u32[]{:S(2)}) %collective-permute-start.18) | collective-permute-done | bytes 524320 | tf_op jit(solution)/shard_map/ppermute | solution.py:62
  177.6 8.1 %out.1 = (bf16[2,4,256,256]{3,2,1,0:T(8,128)(2,1)}, bf16[2,2,256,1024]{3,2,1,0:T(8,128)(2,1)}, bf16[2,2,256,1024]{3,2,1,0:T(8,128)(2,1)}) custom-call(s32[2]{0:T(128)} %pad_add_fusion.place_ref, bf16[2,4,256,128]{3,2,1,0:T(8,128)(2,1)} %get-tuple-element.130.get_own, bf16[2,4,256,128]{3,2,1,0:T(8,128)(2,1)} %copy-done.32, ...), custom_call_target="tpu_custom_call" | custom-call | flops 8999999488 | bytes 9000000 | tf_op jit(solution)/shard_map/out/pallas_call | solution.py:406
  194.7 26.0 %all-gather.11.cloned.1.call-done = bf16[1152,512]{1,0:T(8,128)(2,1)} async-done(((bf16[288,512]{1,0:T(8,128)(2,1)}), bf16[1152,512]{1,0:T(8,128)(2,1)}) %all-gather.11.cloned.1.call-update) | async-done | bytes 1179664 | tf_op jit(solution)/shard_map/all_gather | solution.py:892
  225.4 23.5 %collective-permute-done.22.refs_2_.refs_3_ = bf16[2,256,1024]{2,1,0:T(8,128)(2,1)} collective-permute-done((bf16[2,256,1024]{2,1,0:T(8,128)(2,1)}, bf16[2,256,1024]{2,1,0:T(8,128)(2,1)}, u32[]{:S(2)}, u32[]{:S(2)}) %collective-permute-start.22) | collective-permute-done | bytes 1048608 | tf_op jit(solution)/shard_map/ppermute | solution.py:39
  252.0 25.2 %ffn.2 = (bf16[3,4,256,1152]{3,2,1,0:T(8,128)(2,1)}, bf16[2,2,256,1024]{3,2,1,0:T(8,128)(2,1)}, bf16[2,2,256,1024]{3,2,1,0:T(8,128)(2,1)}, bf16[2,256,1024]{2,1,0:T(8,128)(2,1)}, bf16[2,256,1024]{2,1,0:T(8,128)(2,1)}) custom-call(s32[2]{0:T(128)} %add_multiply_fusion.refs_0_.offset_ref, bf16[2,256,1024]{2,1,0:T(8,128)(2,1)} %multiply_convert_fusion.refs_1_.refs_2_, ...), custom_call_target="tpu_custom_call" | custom-call | flops 22000001024 | bytes 22000000 | tf_op jit(solution)/shard_map/ffn/pallas_call | solution.py:715
  282.7 25.0 %ffn.3 = (bf16[3,4,256,1152]{3,2,1,0:T(8,128)(2,1)}, bf16[2,2,256,1024]{3,2,1,0:T(8,128)(2,1)}, bf16[2,2,256,1024]{3,2,1,0:T(8,128)(2,1)}, bf16[2,256,1024]{2,1,0:T(8,128)(2,1)}, bf16[2,256,1024]{2,1,0:T(8,128)(2,1)}) custom-call(s32[2]{0:T(128)} %add_multiply_fusion.refs_0_.offset_ref, ...), custom_call_target="tpu_custom_call", output_to_operand_aliasing={{1}: (15, {}), {2}: (16, {})} | custom-call | flops 22000001024 | bytes 22000000 | tf_op jit(solution)/shard_map/ffn/pallas_call | solution.py:715
  313.5 10.0 %weight.3 = (bf16[4,288,512]{2,1,0:T(8,128)(2,1)}, bf16[4,288,512]{2,1,0:T(8,128)(2,1)}) custom-call(s32[2]{0:T(128)} %add_multiply_fusion.refs_0_.offset_ref, bf16[3,4,256,1152]{3,2,1,0:T(8,128)(2,1)} %get-tuple-element.140.refs_0_, bf16[3,4,256,1152]{3,2,1,0:T(8,128)(2,1)} %get-tuple-element.149.refs_1_, ...), custom_call_target="tpu_custom_call" | custom-call | flops 10000000000 | bytes 10000000 | tf_op jit(solution)/shard_map/weight/pallas_call | solution.py:773
  326.6 10.2 %weight.4 = (bf16[4,288,512]{2,1,0:T(8,128)(2,1)}, bf16[4,288,512]{2,1,0:T(8,128)(2,1)}) custom-call(s32[2]{0:T(128)} %add_multiply_fusion.refs_0_.offset_ref, bf16[3,4,256,1152]{3,2,1,0:T(8,128)(2,1)} %get-tuple-element.140.refs_0_, bf16[3,4,256,1152]{3,2,1,0:T(8,128)(2,1)} %get-tuple-element.149.refs_1_, ...), custom_call_target="tpu_custom_call" | custom-call | flops 10000000000 | bytes 10000000 | tf_op jit(solution)/shard_map/weight/pallas_call | solution.py:773
  346.7 7.1 %collective-permute-done.33.refs_6_ = bf16[4,256,128]{2,1,0:T(8,128)(2,1)S(1)} collective-permute-done((bf16[4,256,128]{2,1,0:T(8,128)(2,1)S(1)}, bf16[4,256,128]{2,1,0:T(8,128)(2,1)S(1)}, u32[]{:S(2)}, u32[]{:S(2)}) %collective-permute-start.33) | collective-permute-done | bytes 262176 | tf_op jit(solution)/shard_map/ppermute | solution.py:62
  358.4 10.3 %weight.5 = (bf16[4,288,512]{2,1,0:T(8,128)(2,1)}, bf16[4,288,512]{2,1,0:T(8,128)(2,1)}) custom-call(s32[2]{0:T(128)} %add_multiply_fusion.refs_0_.offset_ref, bf16[3,4,256,1152]{3,2,1,0:T(8,128)(2,1)} %get-tuple-element.140.refs_0_, bf16[3,4,256,1152]{3,2,1,0:T(8,128)(2,1)} %get-tuple-element.149.refs_1_, bf16[2,256,1024]{2,1,0:T(8,128)(2,1)} %refs_2_, ...), custom_call_target="tpu_custom_call" | custom-call | flops 10000000000 | bytes 10000000 | tf_op jit(solution)/shard_map/weight/pallas_call | solution.py:773
  375.1 7.2 %collective-permute-done.35 = bf16[4,288,512]{2,1,0:T(8,128)(2,1)S(1)} collective-permute-done((bf16[4,288,512]{2,1,0:T(8,128)(2,1)}, bf16[4,288,512]{2,1,0:T(8,128)(2,1)S(1)}, u32[]{:S(2)}, u32[]{:S(2)}) %collective-permute-start.35) | collective-permute-done | bytes 1179680 | tf_op jit(solution)/shard_map/ppermute | solution.py:82
  394.9 29.2 %attend_back.2 = (bf16[1,4,256,128]{3,2,1,0:T(8,128)(2,1)}, bf16[1,4,256,128]{3,2,1,0:T(8,128)(2,1)}, bf16[1,4,512,128]{3,2,1,0:T(8,128)(2,1)}, bf16[1,4,256,128]{3,2,1,0:T(8,128)(2,1)}, bf16[1,4,256,128]{3,2,1,0:T(8,128)(2,1)}) custom-call(s32[2]{0:T(128)} %pad_add_fusion.place_ref, bf16[2,4,256,128]{3,2,1,0:T(8,128)(2,1)} %get-tuple-element.122.refs_0_, ...), custom_call_target="tpu_custom_call" | custom-call | flops 8000000000 | bytes 8000000 | tf_op jit(solution)/shard_map/attend_back/pallas_call | solution.py:517
  432.2 12.0 %collective-permute-start.45 = (bf16[1,4,256,128]{3,2,1,0:T(8,128)(2,1)}, bf16[1,4,256,128]{3,2,1,0:T(8,128)(2,1)}, u32[]{:S(2)}, u32[]{:S(2)}) collective-permute-start(bf16[1,4,256,128]{3,2,1,0:T(8,128)(2,1)} %get-tuple-element.189), channel_id=1, source_target_pairs={{0,2},{1,3},{2,0},{3,1},{4,6},{5,7},{6,4},{7,5},{8,10},{9,11},{10,... | collective-permute-start | bytes 786440 | tf_op jit(solution)/shard_map/ppermute | solution.py:62
  447.9 29.6 %attend_back.3 = (bf16[1,4,256,128]{3,2,1,0:T(8,128)(2,1)}, bf16[1,4,256,128]{3,2,1,0:T(8,128)(2,1)}, bf16[1,4,512,128]{3,2,1,0:T(8,128)(2,1)}, bf16[1,4,256,128]{3,2,1,0:T(8,128)(2,1)}, bf16[1,4,256,128]{3,2,1,0:T(8,128)(2,1)}) custom-call(s32[2]{0:T(128)} %pad_add_fusion.place_ref, bf16[2,4,256,128]{3,2,1,0:T(8,128)(2,1)} %get-tuple-element.122.refs_0_, ...), custom_call_target="tpu_custom_call" | custom-call | flops 8000000000 | bytes 8000000 | tf_op jit(solution)/shard_map/attend_back/pallas_call | solution.py:517
  480.7 10.1 %collective-permute-start.50 = (bf16[1,4,256,128]{3,2,1,0:T(8,128)(2,1)S(1)}, bf16[1,4,256,128]{3,2,1,0:T(8,128)(2,1)S(1)}, u32[]{:S(2)}, u32[]{:S(2)}) collective-permute-start(bf16[1,4,256,128]{3,2,1,0:T(8,128)(2,1)S(1)} %copy-done.36), channel_id=1, source_target_pairs={{0,2},{1,3},{2,0},{3,1},{4,6},{5,7},{6,4},{7,5},{8,10},{9,11},{10,... | collective-permute-start | bytes 786440 | tf_op jit(solution)/shard_map/ppermute | solution.py:62
  490.9 7.7 %qkv_back.2 = (bf16[1,4,256,512]{3,2,1,0:T(8,128)(2,1)}, bf16[2,1,256,1024]{3,2,1,0:T(8,128)(2,1)}, bf16[2,1,256,1024]{3,2,1,0:T(8,128)(2,1)}, f32[1,384]{1,0:T(1,128)}) custom-call(s32[2]{0:T(128)} %pad_add_fusion.place_ref, bf16[1,4,256,128]{3,2,1,0:T(8,128)(2,1)} %get-tuple-element.176.refs_0_, bf16[1,4,256,128]{3,2,1,0:T(8,128)(2,1)} %get-tuple-element.187.refs_1_, ...), custom_call_target="tpu_custom_call" | custom-call | flops 8000000000 | bytes 8000000 | tf_op jit(solution)/shard_map/qkv_back/pallas_call | solution.py:581
  508.2 7.6 %qkv_back.3 = (bf16[1,4,256,512]{3,2,1,0:T(8,128)(2,1)}, bf16[2,1,256,1024]{3,2,1,0:T(8,128)(2,1)}, bf16[2,1,256,1024]{3,2,1,0:T(8,128)(2,1)}, f32[1,384]{1,0:T(1,128)}) custom-call(s32[2]{0:T(128)} %pad_add_fusion.place_ref, bf16[1,4,256,128]{3,2,1,0:T(8,128)(2,1)} %get-tuple-element.184.refs_0_, bf16[1,4,256,128]{3,2,1,0:T(8,128)(2,1)} %get-tuple-element.195.refs_1_, ...), custom_call_target="tpu_custom_call" | custom-call | flops 8000000000 | bytes 8000000 | tf_op jit(solution)/shard_map/qkv_back/pallas_call | solution.py:581
  535.5 9.4 %collective-permute-done.53 = bf16[1,256,1024]{2,1,0:T(8,128)(2,1)S(1)} collective-permute-done((bf16[1,256,1024]{2,1,0:T(8,128)(2,1)S(1)}, bf16[1,256,1024]{2,1,0:T(8,128)(2,1)S(1)}, u32[]{:S(2)}, u32[]{:S(2)}) %collective-permute-start.53) | collective-permute-done | bytes 524320 | tf_op jit(solution)/shard_map/ppermute | solution.py:1002
  (329 shorter events, 225.5 us)
Async XLA Ops:
  19.6 28.8 %collective-permute-start = (bf16[2,256,1024]{2,1,0:T(8,128)(2,1)}, bf16[2,256,1024]{2,1,0:T(8,128)(2,1)}, u32[]{:S(2)}, u32[]{:S(2)}) collective-permute-start(bf16[2,256,1024]{2,1,0:T(8,128)(2,1)} %multiply_convert_fusion.1.refs_0_.refs_2_), channel_id=1, source_target_pairs={{0,8},{8,0},{4,12},{12,4},{1,9},{9,1},{5,13},{13,5},{2,10},{10,2},... | collective-permute-start | bytes 3145736 | tf_op jit(solution)/shard_map/ppermute | solution.py:39
  23.2 33.7 %all-to-all-start = ((bf16[3,4,288,128]{3,2,0,1:T(8,128)(2,1)}), bf16[3,4,288,128]{3,2,0,1:T(8,128)(2,1)S(1)}, u32[]{:S(2)}, u32[]{:S(2)}) async-start(bf16[3,4,288,128]{3,2,0,1:T(8,128)(2,1)} %copy.94), calls=%async_computation | async-start | bytes 1769472 | tf_op jit(solution)/shard_map/all_to_all | solution.py:866
  26.7 60.6 %all-gather.7.cloned.1.call-start = ((), (), s32[]{:S(2)}) async-start(), calls=%async_computation.8 | async-start | bytes 1474560 | tf_op jit(solution)/shard_map/all_gather | solution.py:890
  37.3 33.1 %collective-permute-start.1 = (bf16[2,256,1024]{2,1,0:T(8,128)(2,1)}, bf16[2,256,1024]{2,1,0:T(8,128)(2,1)}, u32[]{:S(2)}, u32[]{:S(2)}) collective-permute-start(bf16[2,256,1024]{2,1,0:T(8,128)(2,1)} %multiply_convert_fusion.1.refs_0_.refs_2_), channel_id=1, source_target_pairs={{0,4},{4,0},{8,12},{12,8},{1,5},{5,1},{9,13},{13,9},{2,6},{6,2},{1... | collective-permute-start | bytes 3145736 | tf_op jit(solution)/shard_map/ppermute | solution.py:40
  57.8 108.6 %all-gather.9.cloned.1.call-start = ((), (), s32[]{:S(2)}) async-start(), calls=%async_computation.9 | async-start | bytes 1474560 | tf_op jit(solution)/shard_map/all_gather | solution.py:892
  87.3 49.5 %collective-permute-start.14 = (bf16[4,288,512]{2,1,0:T(8,128)(2,1)}, bf16[4,288,512]{2,1,0:T(8,128)(2,1)}, u32[]{:S(2)}, u32[]{:S(2)}) collective-permute-start(bf16[4,288,512]{2,1,0:T(8,128)(2,1)} %bitcast.224), channel_id=1, source_target_pairs={{0,16},{16,0},{1,17},{17,1},{2,18},{18,2},{3,19},{19,3},{4,20},{20... | collective-permute-start | bytes 3538952 | tf_op jit(solution)/shard_map/ppermute | solution.py:75
  89.3 47.1 %collective-permute-start.11 = (bf16[2,4,512,128]{3,2,1,0:T(8,128)(2,1)}, bf16[2,4,512,128]{3,2,1,0:T(8,128)(2,1)}, u32[]{:S(2)}, u32[]{:S(2)}) collective-permute-start(bf16[2,4,512,128]{3,2,1,0:T(8,128)(2,1)} %get-tuple-element.116), channel_id=1, source_target_pairs={{0,1},{1,0},{2,3},{3,2},{4,5},{5,4},{6,7},{7,6},{8,9},{9,8},{10,11... | collective-permute-start | bytes 3145736 | tf_op jit(solution)/shard_map/ppermute | solution.py:62
  89.9 46.9 %collective-permute-start.16 = (bf16[2,256,1024]{2,1,0:T(8,128)(2,1)S(1)}, bf16[2,256,1024]{2,1,0:T(8,128)(2,1)}, u32[]{:S(2)}, u32[]{:S(2)}) collective-permute-start(bf16[2,256,1024]{2,1,0:T(8,128)(2,1)S(1)} %copy-done.11), channel_id=1, source_target_pairs={{0,4},{4,0},{8,12},{12,8},{1,5},{5,1},{9,13},{13,9},{2,6},{6,2},{1... | collective-permute-start | bytes 3145736 | tf_op jit(solution)/shard_map/ppermute | solution.py:40
  107.8 29.0 %collective-permute-start.17 = (bf16[2,256,1024]{2,1,0:T(8,128)(2,1)}, bf16[2,256,1024]{2,1,0:T(8,128)(2,1)}, u32[]{:S(2)}, u32[]{:S(2)}) collective-permute-start(bf16[2,256,1024]{2,1,0:T(8,128)(2,1)} %collective-permute-done.15.refs_6_.refs_3_), channel_id=1, source_target_pairs={{0,4},{4,0},{8,12},{12,8},{1,5},{5,1},{9,13},{13,9},{2,6},{6,2},{1... | collective-permute-start | bytes 3145736 | tf_op jit(solution)/shard_map/ppermute | solution.py:41
  136.5 84.2 %all-gather.11.cloned.1.call-start = ((), (), s32[]{:S(2)}) async-start(), calls=%async_computation.10 | async-start | bytes 1474560 | tf_op jit(solution)/shard_map/all_gather | solution.py:892
  186.7 373.0 %reduce-scatter.4.cloned.1.call-start = ((), (), s32[]{:S(2)}) async-start(), calls=%async_computation.5 | async-start | bytes 1474560 | tf_op jit(solution)/shard_map/reduce_scatter | solution.py:958
  186.7 34.0 %collective-permute-start.20 = (bf16[4,288,512]{2,1,0:T(8,128)(2,1)}, bf16[4,288,512]{2,1,0:T(8,128)(2,1)}, u32[]{:S(2)}, u32[]{:S(2)}) collective-permute-start(bf16[4,288,512]{2,1,0:T(8,128)(2,1)} %bitcast.227), channel_id=1, source_target_pairs={{0,16},{16,0},{1,17},{17,1},{2,18},{18,2},{3,19},{19,3},{4,20},{20... | collective-permute-start | bytes 3538952 | tf_op jit(solution)/shard_map/ppermute | solution.py:75
  279.5 28.2 %collective-permute-start.27 = (bf16[256,1024]{1,0:T(8,128)(2,1)}, bf16[256,1024]{1,0:T(8,128)(2,1)S(1)}, u32[]{:S(2)}, u32[]{:S(2)}) collective-permute-start(bf16[256,1024]{1,0:T(8,128)(2,1)} %get-tuple-element.301), channel_id=1, source_target_pairs={{0,8},{8,0},{4,12},{12,4},{1,9},{9,1},{5,13},{13,5},{2,10},{10,2},... | collective-permute-start | bytes 1572872 | tf_op jit(solution)/shard_map/ppermute | solution.py:933
  353.7 37.5 %collective-permute-start.34 = (bf16[2,2,256,1024]{3,2,1,0:T(8,128)(2,1)}, bf16[2,2,256,1024]{3,2,1,0:T(8,128)(2,1)}, u32[]{:S(2)}, u32[]{:S(2)}) collective-permute-start(bf16[2,2,256,1024]{3,2,1,0:T(8,128)(2,1)} %get-tuple-element.160), channel_id=1, source_target_pairs={{0,4},{4,0},{8,12},{12,8},{1,5},{5,1},{9,13},{13,9},{2,6},{6,2},{1... | collective-permute-start | bytes 6291464 | tf_op jit(solution)/shard_map/ppermute | solution.py:970
  383.7 176.0 %reduce-scatter.6.cloned.1.call-start = ((), (), s32[]{:S(2)}) async-start(), calls=%async_computation.6 | async-start | bytes 1474560 | tf_op jit(solution)/shard_map/reduce_scatter | solution.py:958
  385.2 43.7 %collective-permute-start.41 = (bf16[4,288,512]{2,1,0:T(8,128)(2,1)}, bf16[4,288,512]{2,1,0:T(8,128)(2,1)S(1)}, u32[]{:S(2)}, u32[]{:S(2)}) collective-permute-start(bf16[4,288,512]{2,1,0:T(8,128)(2,1)} %get-tuple-element.170), channel_id=1, source_target_pairs={{0,16},{16,0},{1,17},{17,1},{2,18},{18,2},{3,19},{19,3},{4,20},{20... | collective-permute-start | bytes 3538952 | tf_op jit(solution)/shard_map/ppermute | solution.py:82
  394.3 49.9 %collective-permute-start.40 = (bf16[2,256,1024]{2,1,0:T(8,128)(2,1)}, bf16[2,256,1024]{2,1,0:T(8,128)(2,1)}, u32[]{:S(2)}, u32[]{:S(2)}) collective-permute-start(bf16[2,256,1024]{2,1,0:T(8,128)(2,1)} %fusion.1), channel_id=1, source_target_pairs={{0,8},{8,0},{4,12},{12,4},{1,9},{9,1},{5,13},{13,5},{2,10},{10,2},... | collective-permute-start | bytes 3145736 | tf_op jit(solution)/shard_map/ppermute | solution.py:972
  430.3 47.2 %collective-permute-start.43 = (bf16[4,288,512]{2,1,0:T(8,128)(2,1)}, bf16[4,288,512]{2,1,0:T(8,128)(2,1)}, u32[]{:S(2)}, u32[]{:S(2)}) collective-permute-start(bf16[4,288,512]{2,1,0:T(8,128)(2,1)} %get-tuple-element.182), channel_id=1, source_target_pairs={{0,16},{16,0},{1,17},{17,1},{2,18},{18,2},{3,19},{19,3},{4,20},{20... | collective-permute-start | bytes 3538952 | tf_op jit(solution)/shard_map/ppermute | solution.py:82
  430.9 60.0 %collective-permute-start.44 = (bf16[1,4,512,128]{3,2,1,0:T(8,128)(2,1)}, bf16[1,4,512,128]{3,2,1,0:T(8,128)(2,1)}, u32[]{:S(2)}, u32[]{:S(2)}) collective-permute-start(bf16[1,4,512,128]{3,2,1,0:T(8,128)(2,1)} %get-tuple-element.188), channel_id=1, source_target_pairs={{0,1},{1,0},{2,3},{3,2},{4,5},{5,4},{6,7},{7,6},{8,9},{9,8},{10,11... | collective-permute-start | bytes 1572872 | tf_op jit(solution)/shard_map/ppermute | solution.py:62
  432.2 48.6 %collective-permute-start.45 = (bf16[1,4,256,128]{3,2,1,0:T(8,128)(2,1)}, bf16[1,4,256,128]{3,2,1,0:T(8,128)(2,1)}, u32[]{:S(2)}, u32[]{:S(2)}) collective-permute-start(bf16[1,4,256,128]{3,2,1,0:T(8,128)(2,1)} %get-tuple-element.189), channel_id=1, source_target_pairs={{0,2},{1,3},{2,0},{3,1},{4,6},{5,7},{6,4},{7,5},{8,10},{9,11},{10,... | collective-permute-start | bytes 786440 | tf_op jit(solution)/shard_map/ppermute | solution.py:62
  444.1 46.8 %collective-permute-start.46 = (bf16[1,4,256,128]{3,2,1,0:T(8,128)(2,1)}, bf16[1,4,256,128]{3,2,1,0:T(8,128)(2,1)}, u32[]{:S(2)}, u32[]{:S(2)}) collective-permute-start(bf16[1,4,256,128]{3,2,1,0:T(8,128)(2,1)} %get-tuple-element.190), channel_id=1, source_target_pairs={{0,3},{1,2},{2,1},{3,0},{4,7},{5,6},{6,5},{7,4},{8,11},{9,10},{10,... | collective-permute-start | bytes 786440 | tf_op jit(solution)/shard_map/ppermute | solution.py:62
  444.2 115.5 %reduce-scatter.8.cloned.1.call-start = ((), (), s32[]{:S(2)}) async-start(), calls=%async_computation.7 | async-start | bytes 1474560 | tf_op jit(solution)/shard_map/reduce_scatter | solution.py:958
  444.2 72.5 %collective-permute-start.55 = (bf16[4,256,128]{2,1,0:T(8,128)(2,1)}, bf16[4,256,128]{2,1,0:T(8,128)(2,1)}, u32[]{:S(2)}, u32[]{:S(2)}) collective-permute-start(bf16[4,256,128]{2,1,0:T(8,128)(2,1)} %get-tuple-element.208), channel_id=1, source_target_pairs={{0,16},{16,0},{1,17},{17,1},{2,18},{18,2},{3,19},{19,3},{4,20},{20... | collective-permute-start | bytes 786440 | tf_op jit(solution)/shard_map/ppermute | solution.py:977
  477.5 29.8 %collective-permute-start.49 = (bf16[1,4,512,128]{3,2,1,0:T(8,128)(2,1)}, bf16[1,4,512,128]{3,2,1,0:T(8,128)(2,1)S(1)}, u32[]{:S(2)}, u32[]{:S(2)}) collective-permute-start(bf16[1,4,512,128]{3,2,1,0:T(8,128)(2,1)} %get-tuple-element.196), channel_id=1, source_target_pairs={{0,1},{1,0},{2,3},{3,2},{4,5},{5,4},{6,7},{7,6},{8,9},{9,8},{10,11... | collective-permute-start | bytes 1572872 | tf_op jit(solution)/shard_map/ppermute | solution.py:62
  (90 other events, 1263.8 us)
Sparse Core Ops, SparseCore 0:
  58.0 29.2 all-gather.6
  136.6 29.7 all-gather.8
  186.8 33.9 all-gather.10
  383.8 31.5 reduce-scatter.3
  444.3 39.4 reduce-scatter.5
  518.0 31.3 reduce-scatter.7
